TPU v7x, 256 devices: a whole 4x4x8 slice. The times are simulated.
256 devices in a mesh: rep: 2 (over y_hi), dp: 2 (over y_lo), seq: 64 (over x, z, core).
Axes of the slice: x: 4, y: 4 (y_hi: 2, y_lo: 2; y = y_hi * 2 + y_lo), z: 8, core: 2. Of those that a mesh axis runs over, the one named last changes fastest.
Arguments:
- tokens: bfloat16 [4, 128, 8, 16, 768], P(('rep', 'dp'), 'seq'), may hold values from -6 to 6
- cotangent: bfloat16 [4, 128, 8, 16, 768], P(('rep', 'dp'), 'seq'), may hold values from -6 to 6
- w_qkv: bfloat16 [768, 2304], P('dp'), may hold values from -0.21875 to 0.21875
- w_proj: bfloat16 [768, 768], P('dp'), may hold values from -0.21875 to 0.21875
- conv_weight: float32 [27, 768], replicated, may hold values from -1.25 to 1.25
- norm_gain: float32 [768], replicated, may hold values from 0.5 to 1.5
- head_scale: float32 [24], replicated, may hold values from 2 to 20
- shift_offsets: int32 [2], replicated, may hold values from 1 to 7, as said below
Outputs:
- output: bfloat16 [4, 128, 8, 16, 768], P(('rep', 'dp'), 'seq')
- grad_tokens: bfloat16 [4, 128, 8, 16, 768], P(('rep', 'dp'), 'seq')
- grad_qkv: float32 [768, 2304], P('dp')
- grad_proj: float32 [768, 768], P('dp')
- grad_conv: float32 [27, 768], replicated
- grad_gain: float32 [768], replicated
- grad_scale: float32 [24], replicated
Inputs may be any that keep to these rules, and one draw needn't show every extreme that they name: `shift_offsets`: the two offsets differ.
All inputs are finite; a program needn't handle non-finite values.
Results may differ from a plain program's by a relative error of at most 0.014.
The roundings to bfloat16 on the way count: a program that leaves them out, or rounds other values in their place, can miss the bound.
Values may be sent and summed in bfloat16 or wider, within the bound.
A program may use at most 128 MiB of HBM per device.

v0:
```python
import math

import jax
import jax.numpy as jnp
from jax import lax
from jax.sharding import PartitionSpec as P

WH = 8
WW = 8


def passed_along(x, axis, by):
    count = lax.axis_size(axis)
    return lax.ppermute(x, axis, [(i, (i + by) % count) for i in range(count)])


def with_halo(x, sides, width):
    for axis, dim in sides:
        count, length = (lax.axis_size(axis), x.shape[dim])
        up = [(i, (i + 1) % count) for i in range(count - 1)]
        down = [(j, i) for i, j in up]
        last = lax.slice_in_dim(x, length - width, length, axis=dim)
        initial = lax.slice_in_dim(x, 0, width, axis=dim)
        before = lax.ppermute(last, axis, up)
        after = lax.ppermute(initial, axis, down)
        x = jnp.concatenate([before, x, after], axis=dim)
    return x


def from_partner(x, axis, bit):
    return lax.ppermute(x, axis, [(i, i ^ 1 << bit) for i in range(lax.axis_size(axis))])


def tap_sum(padded, weight, slab_depth, height, grid_width, flipped):
    summed = jnp.zeros((slab_depth, height, grid_width, padded.shape[-1]), jnp.float32)
    for depth_tap in range(3):
        for row_tap in range(3):
            for col_tap in range(3):
                tap_index = 9 * depth_tap + 3 * row_tap + col_tap
                if flipped:
                    starts = (2 - depth_tap, 2 - row_tap, 2 - col_tap)
                else:
                    starts = (depth_tap, row_tap, col_tap)
                window_part = padded[
                    starts[0] : starts[0] + slab_depth,
                    starts[1] : starts[1] + height,
                    starts[2] : starts[2] + grid_width,
                ]
                summed = summed + weight[tap_index] * window_part.astype(jnp.float32)
    return summed


def into_blocks(field):
    slab_depth, height, grid_width, channels = field.shape
    shaped = field.reshape(slab_depth, height // WH, WH, grid_width // WW, WW, channels)
    shaped = shaped.transpose(1, 3, 0, 2, 4, 5)
    return shaped.reshape(height // WH * (grid_width // WW), slab_depth * WH * WW, channels)


def out_of_blocks(blocks, slab_depth, height, grid_width):
    channels = blocks.shape[-1]
    shaped = blocks.reshape(height // WH, grid_width // WW, slab_depth, WH, WW, channels)
    shaped = shaped.transpose(2, 0, 3, 1, 4, 5)
    return shaped.reshape(slab_depth, height, grid_width, channels)


def roll_local(field, rows_shift, cols_shift, direction):
    return jnp.roll(field, (direction * rows_shift, direction * cols_shift), axis=(1, 2))


def into_frame(field, rows_shift, cols_shift):
    return passed_along(roll_local(field, rows_shift, cols_shift, -1), "seq", -1)


def out_of_frame(field, rows_shift, cols_shift):
    moved = passed_along(field, "seq", 1)
    return roll_local(moved, rows_shift, cols_shift, 1)


def unit_rows(values):
    as_float = values.astype(jnp.float32)
    radius = jnp.sqrt(jnp.sum(as_float * as_float, axis=-1, keepdims=True) + 1.0)
    return (as_float, radius, (as_float / radius).astype(jnp.bfloat16))


def radius_back(as_float, radius, back_unit):
    inner = jnp.sum(as_float * back_unit, axis=-1, keepdims=True)
    return back_unit / radius - as_float * inner / (radius * radius * radius)


def window_forward(unit_query, unit_key, values, allowed, head_scale):
    cosine = jnp.einsum("wqhe,wkhe->whqk", unit_query, unit_key, preferred_element_type=jnp.float32)
    expo = jnp.exp(head_scale[:, None, None] * cosine) * allowed[:, None]
    probability = expo / jnp.sum(expo, axis=-1, keepdims=True)
    weights = probability.astype(jnp.bfloat16)
    attended = jnp.einsum(
        "whqk,wkhe->wqhe", weights, values, preferred_element_type=jnp.float32
    ).astype(jnp.bfloat16)
    return (cosine, probability, weights, attended)


def window_backward(unit_query, unit_key, values, head_scale, back_attended, forward_parts):
    cosine, probability, weights = forward_parts
    back_value = jnp.einsum(
        "whqk,wqhe->wkhe", weights, back_attended, preferred_element_type=jnp.float32
    )
    back_prob = jnp.einsum(
        "wqhe,wkhe->whqk", back_attended, values, preferred_element_type=jnp.float32
    )
    back_score = probability * (
        back_prob - jnp.sum(probability * back_prob, axis=-1, keepdims=True)
    )
    scale_rows = jnp.sum(back_score * cosine, axis=-1)
    scaled = (back_score * head_scale[:, None, None]).astype(jnp.bfloat16)
    back_uq = jnp.einsum("whqk,wkhe->wqhe", scaled, unit_key, preferred_element_type=jnp.float32)
    back_uk = jnp.einsum("whqk,wqhe->wkhe", scaled, unit_query, preferred_element_type=jnp.float32)
    return (back_uq, back_uk, back_value, scale_rows)


def order_halves(mine, other, upper_half):
    return jnp.where(
        upper_half, jnp.concatenate([other, mine], axis=1), jnp.concatenate([mine, other], axis=1)
    )


def pick_half(both, upper_half):
    middle = both.shape[1] // 2
    lower = both[:, :middle]
    higher = both[:, middle:]
    return (jnp.where(upper_half, higher, lower), jnp.where(upper_half, lower, higher))


def per_device(tokens, cotangent, w_qkv, w_proj, conv_weight, norm_gain, head_scale, shift_offsets):
    full_qkv, full_proj = (
        lax.all_gather(w_qkv, "dp", axis=0, tiled=True),
        lax.all_gather(w_proj, "dp", axis=0, tiled=True),
    )
    slab = tokens[0]
    slab_depth, height, grid_width, channels = slab.shape
    head_count = head_scale.shape[0]
    head_dim = channels // head_count
    seq_count = lax.axis_size("seq")
    seq_index = lax.axis_index("seq")
    rows_shift = shift_offsets[0]
    cols_shift = shift_offsets[1]
    spatial = ((0, 0), (1, 1), (1, 1), (0, 0))
    padded_tokens = jnp.pad(with_halo(slab, (("seq", 0),), 1), spatial)
    mixed_field = slab.astype(jnp.float32) + tap_sum(
        padded_tokens, conv_weight, slab_depth, height, grid_width, False
    )
    centred = mixed_field - jnp.mean(mixed_field, axis=-1, keepdims=True)
    inverse_std = lax.rsqrt(jnp.mean(centred * centred, axis=-1, keepdims=True) + 1e-05)
    unit_field = centred * inverse_std
    normed = (unit_field * norm_gain).astype(jnp.bfloat16)
    position_count = slab_depth * height * grid_width
    row_code = 2 * (jnp.arange(height) >= height - rows_shift).astype(jnp.int32)
    col_code = (jnp.arange(grid_width) >= grid_width - cols_shift).astype(jnp.int32)
    plane_code = row_code[:, None] + col_code[None, :]
    grid_code = jnp.broadcast_to(plane_code[None, :, :, None], (slab_depth, height, grid_width, 1))
    block_code = into_blocks(grid_code)[..., 0]
    cotangent_rows = cotangent[0].reshape(position_count, channels)
    back_restored = jnp.einsum(
        "tc,dc->td", cotangent_rows, full_proj, preferred_element_type=jnp.float32
    ).astype(jnp.bfloat16)
    back_restored_field = back_restored.reshape(slab_depth, height, grid_width, channels)
    shifted = into_frame(normed, rows_shift, cols_shift)
    shifted_rows = shifted.reshape(position_count, channels)
    qkv = jnp.dot(shifted_rows, full_qkv, preferred_element_type=jnp.float32).astype(jnp.bfloat16)
    qkv = qkv.reshape(slab_depth, height, grid_width, 3 * channels)
    upper_half = seq_index % 2 == 1
    partner_kv = from_partner(qkv[..., channels:], "seq", 0)
    key_code = order_halves(block_code, block_code, upper_half)
    my_allowed = (block_code[:, :, None] == key_code[:, None, :]).astype(jnp.float32)
    my_blocks = into_blocks(qkv)
    block_count = my_blocks.shape[0]
    half_positions = my_blocks.shape[1]

    def split_heads(part):
        return part.reshape(block_count, half_positions, head_count, head_dim)

    def merge_heads(part):
        return part.reshape(block_count, half_positions, channels)

    query = split_heads(my_blocks[..., :channels])
    my_key = split_heads(my_blocks[..., channels : 2 * channels])
    my_value = split_heads(my_blocks[..., 2 * channels :])
    partner_blocks = into_blocks(partner_kv)
    partner_key = split_heads(partner_blocks[..., :channels])
    partner_value = split_heads(partner_blocks[..., channels:])
    query_float, query_radius, unit_query = unit_rows(query)
    key_float, key_radius, my_unit_key = unit_rows(my_key)
    unused_a, unused_b, partner_unit_key = unit_rows(partner_key)
    unit_key = order_halves(my_unit_key, partner_unit_key, upper_half)
    all_values = order_halves(my_value, partner_value, upper_half)
    forward_all = window_forward(unit_query, unit_key, all_values, my_allowed, head_scale)
    restored = out_of_frame(
        out_of_blocks(merge_heads(forward_all[3]), slab_depth, height, grid_width),
        rows_shift,
        cols_shift,
    )
    back_attended = into_frame(back_restored_field, rows_shift, cols_shift)
    back_heads = split_heads(into_blocks(back_attended))
    back_uq, back_uk, back_value, scale_rows = window_backward(
        unit_query, unit_key, all_values, head_scale, back_heads, forward_all[:3]
    )
    scale_part = jnp.sum(scale_rows, axis=(0, 2))
    mine_uk, other_uk = pick_half(back_uk, upper_half)
    mine_value, other_value = pick_half(back_value, upper_half)
    received = from_partner(
        jnp.stack([other_uk, other_value]).astype(jnp.bfloat16), "seq", 0
    ).astype(jnp.float32)
    mine_uk = mine_uk + received[0]
    mine_value = mine_value + received[1]
    back_query = radius_back(query_float, query_radius, back_uq)
    back_key = radius_back(key_float, key_radius, mine_uk)
    back_blocks = jnp.concatenate(
        [merge_heads(back_query), merge_heads(back_key), merge_heads(mine_value)], axis=-1
    ).astype(jnp.bfloat16)
    back_qkv_rows = out_of_blocks(back_blocks, slab_depth, height, grid_width).reshape(
        position_count, 3 * channels
    )
    back_shifted = jnp.einsum(
        "tj,cj->tc", back_qkv_rows, full_qkv, preferred_element_type=jnp.float32
    ).astype(jnp.bfloat16)
    back_normed = out_of_frame(
        back_shifted.reshape(slab_depth, height, grid_width, channels), rows_shift, cols_shift
    )
    restored_rows = restored.reshape(position_count, channels)
    projected = jnp.dot(restored_rows, full_proj, preferred_element_type=jnp.float32)
    output = (mixed_field + projected.reshape(slab_depth, height, grid_width, channels)).astype(
        jnp.bfloat16
    )
    back_float = back_normed.astype(jnp.float32)
    gain_part = jnp.sum(back_float * unit_field, axis=(0, 1, 2))
    grad_unit = back_float * norm_gain
    back_mixed = cotangent[0].astype(jnp.float32) + inverse_std * (
        grad_unit
        - jnp.mean(grad_unit, axis=-1, keepdims=True)
        - unit_field * jnp.mean(grad_unit * unit_field, axis=-1, keepdims=True)
    )
    padded_back = jnp.pad(
        with_halo(back_mixed.astype(jnp.bfloat16), (("seq", 0),), 1).astype(back_mixed.dtype),
        spatial,
    )
    grad_tokens = (
        back_mixed + tap_sum(padded_back, conv_weight, slab_depth, height, grid_width, True)
    ).astype(jnp.bfloat16)
    conv_rows = []
    for depth_tap in range(3):
        for row_tap in range(3):
            for col_tap in range(3):
                window_part = padded_tokens[
                    depth_tap : depth_tap + slab_depth,
                    row_tap : row_tap + height,
                    col_tap : col_tap + grid_width,
                ]
                conv_rows.append(
                    jnp.sum(back_mixed * window_part.astype(jnp.float32), axis=(0, 1, 2))
                )
    conv_part = jnp.stack(conv_rows)
    qkv_term = jnp.einsum(
        "tc,tj->cj", shifted_rows, back_qkv_rows, preferred_element_type=jnp.float32
    )
    proj_term = jnp.einsum(
        "tc,tj->cj", restored_rows, cotangent_rows, preferred_element_type=jnp.float32
    )
    halves = lax.psum_scatter(
        jnp.concatenate([qkv_term, proj_term], axis=1).astype(jnp.bfloat16),
        "dp",
        scatter_dimension=0,
        tiled=True,
    ).astype(jnp.float32)
    totals = lax.psum(halves, ("rep", "seq"))
    conv_total, gain_total, scale_total = lax.psum(
        (conv_part, gain_part, scale_part), ("rep", "dp", "seq")
    )
    factor = 1.0 / math.sqrt(
        lax.axis_size("rep") * lax.axis_size("dp") * seq_count * position_count
    )
    return (
        output[None],
        grad_tokens[None],
        totals[:, : 3 * channels] * factor,
        totals[:, 3 * channels :] * factor,
        conv_total * factor,
        gain_total * factor,
        scale_total * factor,
    )


def solution(mesh):
    in_specs = (
        P(("rep", "dp"), "seq", None, None, None),
        P(("rep", "dp"), "seq", None, None, None),
        P("dp", None),
        P("dp", None),
        P(),
        P(),
        P(),
        P(),
    )
    out_specs = (
        P(("rep", "dp"), "seq", None, None, None),
        P(("rep", "dp"), "seq", None, None, None),
        P("dp", None),
        P("dp", None),
        P(),
        P(),
        P(),
    )
    return jax.shard_map(
        per_device, mesh=mesh, in_specs=in_specs, out_specs=out_specs, check_vma=False
    )
```

profile of v0, /device:TPU:1, one launch (start us, length us, event | category | flops | bytes accessed | tf_op | source)
XLA Modules:
  0.0 1221.1 jit_solution(9163128051118188027)
XLA Ops:
  9.0 4.9 collective-permute-start
  21.5 3.7 fusion.190
  27.0 14.5 %all-gather.5.cloned.1.call-done = bf16[768,768]{1,0:T(8,128)(2,1)} async-done(((bf16[384,768]{1,0:T(8,128)(2,1)}), bf16[768,768]{1,0:T(8,128)(2,1)}) %all-gather.5.cloned.1.call-update) | async-done | bytes 1179664 | tf_op jit(solution)/shard_map/all_gather | solution.py:136
  56.0 2.7 copy.44
  58.7 40.2 %all-gather.3.cloned.1.call-done = bf16[768,2304]{1,0:T(8,128)(2,1)} async-done(((bf16[384,2304]{1,0:T(8,128)(2,1)}), bf16[768,2304]{1,0:T(8,128)(2,1)}) %all-gather.3.cloned.1.call-update) | async-done | bytes 3538960 | tf_op jit(solution)/shard_map/all_gather | solution.py:135
  98.8 3.1 convolution_convert_fusion.1
  127.2 2.7 copy-done
  131.8 10.6 convolution_bitcast_fusion
  142.4 3.6 fusion.15
  147.4 2.5 copy.41
  149.9 3.0 reshape_reshape.13
  156.5 10.7 convolution_bitcast_fusion.1
  167.2 2.9 fusion.27
  170.2 2.5 copy.45
  172.7 2.9 concatenate.70
  181.3 2.6 copy.47
  183.9 3.0 concatenate.71
  188.5 3.0 concatenate.72
  196.7 2.9 convolution_convert_fusion
  201.2 2.6 fusion.90
  205.6 2.6 stack.126
  208.2 5.1 pad_maximum_fusion
  214.5 8.0 multiply_reduce_fusion
  222.5 2.5 fusion.34
  225.3 4.4 collective-permute-start.8
  229.7 3.5 collective-permute-start.9
  233.2 78.1 %all-reduce.2 = (f32[768]{0:T(1024)S(1)}, f32[24]{0:T(128)S(1)}) all-reduce(f32[768]{0:T(1024)S(1)} %copy-done.67, f32[24]{0:T(128)S(1)} %multiply_reduce_fusion), channel_id=1, replica_groups=mesh['rep'=2,'dp'=2,'seq'=64] {'rep','dp','seq'}, use_global_device_ids=true, to_apply=%region_42.44 | all-reduce | flops 792 | bytes 6336 | tf_op jit(solution)/shard_map/psum | solution.py:274
  312.4 139.8 %all-reduce.6.cloned.1.call-done = f32[27,768]{1,0:T(8,128)} async-done(((f32[27,768]{1,0:T(8,128)}), f32[27,768]{1,0:T(8,128)}) %all-reduce.6.cloned.1.call-update) | async-done | bytes 82960 | tf_op jit(solution)/shard_map/psum | solution.py:274
  454.0 3.9 fusion.168
  457.8 57.9 %reduce-scatter.2.cloned.1.call-done = bf16[384,3072]{1,0:T(8,128)(2,1)} async-done(((bf16[768,3072]{1,0:T(8,128)(2,1)}), bf16[384,3072]{1,0:T(8,128)(2,1)}) %reduce-scatter.2.cloned.1.call-update) | async-done | bytes 2359312 | tf_op jit(solution)/shard_map/reduce_scatter | solution.py:267
  515.8 692.0 %all-reduce.7 = f32[384,3072]{1,0:T(8,128)} all-reduce(bf16[384,3072]{1,0:T(8,128)(2,1)} %reduce-scatter.2.cloned.1.call-done), channel_id=1, replica_groups=mesh['rep'=2,'dp'=2,'seq'=64] {'rep','seq'}, use_global_device_ids=true, to_apply=%region_12.14 | all-reduce | flops 1179648 | bytes 7077888 | tf_op jit(solution)/shard_map/psum | solution.py:273
  1210.1 4.0 slice_multiply_fusion
  (261 shorter events, 72.7 us)
Async XLA Ops:
  7.2 34.3 %all-gather.5.cloned.1.call-start = ((), (), s32[]{:S(2)}) async-start(), calls=%async_computation.2 | async-start | bytes 1769472 | tf_op jit(solution)/shard_map/all_gather | solution.py:136
  7.9 90.9 %all-gather.3.cloned.1.call-start = ((), (), s32[]{:S(2)}) async-start(), calls=%async_computation.1 | async-start | bytes 5308416 | tf_op jit(solution)/shard_map/all_gather | solution.py:135
  9.0 10.7 collective-permute-start
  14.0 7.0 collective-permute-start.1
  15.9 436.2 %all-reduce.6.cloned.1.call-start = ((), (), s32[]{:S(2)}) async-start(), calls=%async_computation.4 | async-start | bytes 196608 | tf_op jit(solution)/shard_map/psum | solution.py:274
  25.6 15.9 %copy-start.10 = (bf16[1,2,8,16,768]{4,3,2,1,0:T(8,128)(2,1)S(1)}, bf16[1,2,8,16,768]{4,3,2,1,0:T(8,128)(2,1)}, u32[]{:S(2)}) copy-start(bf16[1,2,8,16,768]{4,3,2,1,0:T(8,128)(2,1)} %param.11) | copy-start | bytes 1179652
  27.0 31.6 %collective-permute-start.2 = (bf16[2,8,16,768]{3,2,1,0:T(8,128)(2,1)}, bf16[2,8,16,768]{3,2,1,0:T(8,128)(2,1)S(1)}, u32[]{:S(2)}, u32[]{:S(2)}) collective-permute-start(bf16[2,8,16,768]{3,2,1,0:T(8,128)(2,1)} %fusion.166), channel_id=1, source_target_pairs={{0,63},{1,0},{2,1},{3,2},{4,3},{5,4},{6,5},{7,6},{8,7},{9,8},{10,9... | collective-permute-start | bytes 1179656 | tf_op jit(solution)/shard_map/ppermute | solution.py:14
  44.5 7.5 collective-permute-start.5
  58.7 43.3 %copy-start.26 = (bf16[2,8,16,768]{3,2,1,0:T(8,128)(2,1)}, bf16[2,8,16,768]{3,2,1,0:T(8,128)(2,1)S(1)}, u32[]{:S(2)}) copy-start(bf16[2,8,16,768]{3,2,1,0:T(8,128)(2,1)S(1)} %collective-permute-done.2) | copy-start | bytes 1179652
  102.9 10.3 collective-permute-start.3
  147.4 30.5 %collective-permute-start.6 = (bf16[2,2,128,24,32]{2,4,3,1,0:T(8,128)(2,1)}, bf16[2,2,128,24,32]{2,4,3,1,0:T(8,128)(2,1)}, u32[]{:S(2)}, u32[]{:S(2)}) collective-permute-start(bf16[2,2,128,24,32]{2,4,3,1,0:T(8,128)(2,1)} %pad_maximum_fusion.1), channel_id=1, source_target_pairs={{0,1},{1,0},{2,3},{3,2},{4,5},{5,4},{6,7},{7,6},{8,9},{9,8},{10,11... | collective-permute-start | bytes 2359304 | tf_op jit(solution)/shard_map/ppermute | solution.py:31
  154.7 21.0 %collective-permute-start.4 = (bf16[2,8,16,768]{3,2,1,0:T(8,128)(2,1)}, bf16[2,8,16,768]{3,2,1,0:T(8,128)(2,1)}, u32[]{:S(2)}, u32[]{:S(2)}) collective-permute-start(bf16[2,8,16,768]{3,2,1,0:T(8,128)(2,1)} %copy_bitcast_fusion), channel_id=1, source_target_pairs={{0,1},{1,2},{2,3},{3,4},{4,5},{5,6},{6,7},{7,8},{8,9},{9,10},{10,1... | collective-permute-start | bytes 1179656 | tf_op jit(solution)/shard_map/ppermute | solution.py:14
  194.8 5.1 collective-permute-start.7
  208.2 307.6 %reduce-scatter.2.cloned.1.call-start = ((), (), s32[]{:S(2)}) async-start(), calls=%async_computation.3 | async-start | bytes 7077888 | tf_op jit(solution)/shard_map/reduce_scatter | solution.py:267
  225.1 228.7 %copy-start.34 = (f32[768]{0:T(1024)S(1)}, f32[768]{0:T(1024)}, u32[]{:S(2)}) copy-start(f32[768]{0:T(1024)} %copy-done.33) | copy-start | bytes 9220
  225.1 228.8 %copy-start.36 = (f32[768]{0:T(1024)S(1)}, f32[768]{0:T(1024)}, u32[]{:S(2)}) copy-start(f32[768]{0:T(1024)} %copy-done.35) | copy-start | bytes 9220
  225.1 228.8 %copy-start.38 = (f32[768]{0:T(1024)S(1)}, f32[768]{0:T(1024)}, u32[]{:S(2)}) copy-start(f32[768]{0:T(1024)} %copy-done.37) | copy-start | bytes 9220
  225.1 228.8 %copy-start.40 = (f32[768]{0:T(1024)S(1)}, f32[768]{0:T(1024)}, u32[]{:S(2)}) copy-start(f32[768]{0:T(1024)} %copy-done.39) | copy-start | bytes 9220
  225.1 228.8 %copy-start.42 = (f32[768]{0:T(1024)S(1)}, f32[768]{0:T(1024)}, u32[]{:S(2)}) copy-start(f32[768]{0:T(1024)} %copy-done.41) | copy-start | bytes 9220
  225.1 228.8 %copy-start.44 = (f32[768]{0:T(1024)S(1)}, f32[768]{0:T(1024)}, u32[]{:S(2)}) copy-start(f32[768]{0:T(1024)} %copy-done.43) | copy-start | bytes 9220
  225.1 228.8 %copy-start.46 = (f32[768]{0:T(1024)S(1)}, f32[768]{0:T(1024)}, u32[]{:S(2)}) copy-start(f32[768]{0:T(1024)} %copy-done.45) | copy-start | bytes 9220
  225.1 228.8 %copy-start.48 = (f32[768]{0:T(1024)S(1)}, f32[768]{0:T(1024)}, u32[]{:S(2)}) copy-start(f32[768]{0:T(1024)} %copy-done.47) | copy-start | bytes 9220
  225.2 228.8 %copy-start.50 = (f32[768]{0:T(1024)S(1)}, f32[768]{0:T(1024)}, u32[]{:S(2)}) copy-start(f32[768]{0:T(1024)} %copy-done.49) | copy-start | bytes 9220
  225.2 228.8 %copy-start.52 = (f32[768]{0:T(1024)S(1)}, f32[768]{0:T(1024)}, u32[]{:S(2)}) copy-start(f32[768]{0:T(1024)} %copy-done.51) | copy-start | bytes 9220
  225.2 228.8 %copy-start.54 = (f32[768]{0:T(1024)S(1)}, f32[768]{0:T(1024)}, u32[]{:S(2)}) copy-start(f32[768]{0:T(1024)} %copy-done.53) | copy-start | bytes 9220
  225.2 228.8 %copy-start.56 = (f32[768]{0:T(1024)S(1)}, f32[768]{0:T(1024)}, u32[]{:S(2)}) copy-start(f32[768]{0:T(1024)} %copy-done.55) | copy-start | bytes 9220
  225.2 228.8 %copy-start.58 = (f32[768]{0:T(1024)S(1)}, f32[768]{0:T(1024)}, u32[]{:S(2)}) copy-start(f32[768]{0:T(1024)} %copy-done.57) | copy-start | bytes 9220
  225.2 228.8 %copy-start.60 = (f32[768]{0:T(1024)S(1)}, f32[768]{0:T(1024)}, u32[]{:S(2)}) copy-start(f32[768]{0:T(1024)} %copy-done.59) | copy-start | bytes 9220
  225.2 228.8 %copy-start.62 = (f32[768]{0:T(1024)S(1)}, f32[768]{0:T(1024)}, u32[]{:S(2)}) copy-start(f32[768]{0:T(1024)} %copy-done.61) | copy-start | bytes 9220
  225.2 228.8 %copy-start.64 = (f32[768]{0:T(1024)S(1)}, f32[768]{0:T(1024)}, u32[]{:S(2)}) copy-start(f32[768]{0:T(1024)} %copy-done.63) | copy-start | bytes 9220
  225.3 228.4 %collective-permute-start.8 = (bf16[1,8,16,768]{3,2,1,0:T(8,128)(2,1)S(1)}, bf16[1,8,16,768]{3,2,1,0:T(8,128)(2,1)S(1)}, u32[]{:S(2)}, u32[]{:S(2)}) collective-permute-start(bf16[1,8,16,768]{3,2,1,0:T(8,128)(2,1)S(1)} %get-tuple-element.85), channel_id=1, source_target_pairs={{0,1},{1,2},{2,3},{3,4},{4,5},{5,6},{6,7},{7,8},{8,9},{9,10},{10,1... | collective-permute-start | bytes 589832 | tf_op jit(solution)/shard_map/ppermute | solution.py:24
  229.7 224.0 %collective-permute-start.9 = (bf16[1,8,16,768]{3,2,1,0:T(8,128)(2,1)S(1)}, bf16[1,8,16,768]{3,2,1,0:T(8,128)(2,1)S(1)}, u32[]{:S(2)}, u32[]{:S(2)}) collective-permute-start(bf16[1,8,16,768]{3,2,1,0:T(8,128)(2,1)S(1)} %get-tuple-element.86), channel_id=1, source_target_pairs={{1,0},{2,1},{3,2},{4,3},{5,4},{6,5},{7,6},{8,7},{9,8},{10,9},{11,1... | collective-permute-start | bytes 589832 | tf_op jit(solution)/shard_map/ppermute | solution.py:25
  (53 other events, 282.7 us)
Sparse Core Ops, SparseCore 0:
  9.8 31.6 all-gather.4
  43.3 55.4 all-gather.2
  208.3 243.8 all-reduce.5
  454.6 61.1 reduce-scatter.1
where the time goes:
time: 1230 us; the launch traced here: 1220 us
  blocking collectives  770 us (63%)
  waiting for transfers between devices  257 us (21%)
  other arithmetic  52.3 us (4%)
  local copies, waits for them, and re-layouts  51.5 us (4%)
  matrix products  50 us (4%)
  between operations  22.1 us (2%)
  starting transfers between devices  18.6 us (2%)
    psum x1, blocking collectives, per_device(): totals = lax.psum(halves, ('rep', 'seq'))  692 us
    psum x1, waiting for transfers between devices, per_device(): lax.psum((conv_part, gain_part, scale_part), ('rep', 'dp', 'seq'))  140 us
    psum x1, blocking collectives, per_device(): lax.psum((conv_part, gain_part, scale_part), ('rep', 'dp', 'seq'))  78.1 us
    reduce_scatter x1, waiting for transfers between devices, per_device(): lax.psum_scatter(jnp.concatenate([qkv_term, proj_term], axis=1).astype(jn...  57.9 us
    all_gather x1, waiting for transfers between devices, per_device(): lax.all_gather(w_qkv, 'dp', axis=0, tiled=True)  40.2 us
  transfers between devices with their start and end apart: 14, of which 7 were waited for; matrix products, arithmetic and copies ran while one was open for 7% of the time, Pallas kernels for 0%

commit v1 on v0

--- a/solution.py
+++ b/solution.py
@@ -3,10 +3,175 @@
 import jax
 import jax.numpy as jnp
 from jax import lax
+from jax.experimental import pallas as pl
+from jax.experimental.pallas import tpu as pltpu
 from jax.sharding import PartitionSpec as P
 
 WH = 8
 WW = 8
+MESH = pl.DeviceIdType.MESH
+XC = 4
+ZC = 8
+
+
+def reduce_kernel(g, out, ra0, ra1, sa0, sa1, rb0, rb1, sb, rc,
+                  a_send, a_recv, b_send, b_recv, c_send, c_recv, d_send, d_recv,
+                  e_send, e_recv, f_send, f_recv, h_send, h_recv):
+    rep, dp, seq = lax.axis_index("rep"), lax.axis_index("dp"), lax.axis_index("seq")
+    core = lax.rem(seq, 2)
+    z = lax.rem(seq // 2, ZC)
+    x = seq // (2 * ZC)
+    y = rep * 2 + dp
+    half = ZC // 2
+
+    def at_y(step):
+        there = lax.rem(y + step, 4)
+        return (there // 2, lax.rem(there, 2), seq)
+
+    def at_x(step):
+        there = lax.rem(x + step, XC)
+        return (rep, dp, (there * ZC + z) * 2 + core)
+
+    def at_z(step):
+        there = lax.rem(z + step, ZC)
+        return (rep, dp, (x * ZC + there) * 2 + core)
+
+    other_core = (rep, dp, (x * ZC + z) * 2 + 1 - core)
+    other_rep = (1 - rep, dp, seq)
+    peers = [at_y(k) for k in range(1, 4)] + [at_x(k) for k in range(1, XC)]
+    peers += [at_z(k) for k in range(1, ZC)] + [other_core]
+    barrier = pltpu.get_barrier_semaphore()
+    for peer in peers:
+        pl.semaphore_signal(barrier, inc=1, device_id=peer, device_id_type=MESH)
+    pl.semaphore_wait(barrier, len(peers))
+
+    def send(src, dst, s, r, to):
+        c = pltpu.make_async_remote_copy(
+            src_ref=src, dst_ref=dst, send_sem=s, recv_sem=r, device_id=to, device_id_type=MESH
+        )
+        c.start()
+        return c
+
+    copies = []
+    for k in range(1, 4):
+        to = at_y(k)
+        copies.append(send(g.at[to[1], to[0], :, pl.ds(0, half)], ra0.at[k - 1],
+                           a_send.at[k - 1], a_recv.at[k - 1], to))
+    for k in range(1, XC):
+        to = at_x(k)
+        there = lax.rem(x + k, XC)
+        copies.append(send(g.at[:, :, there, pl.ds(half, half)], ra1.at[k - 1],
+                           a_send.at[k + 2], a_recv.at[k + 2], to))
+    for c in copies:
+        c.wait()
+
+    def add_a0(i, carry):
+        total = g[dp, rep, i, pl.ds(0, half)].astype(jnp.float32)
+        for k in range(3):
+            total = total + ra0[k, i].astype(jnp.float32)
+        sa0[i] = total.astype(jnp.bfloat16)
+        return carry
+
+    lax.fori_loop(0, XC, add_a0, 0)
+
+    def add_a1(i, carry):
+        d, r = lax.rem(i, 2), i // 2
+        total = g[d, r, x, pl.ds(half, half)].astype(jnp.float32)
+        for k in range(XC - 1):
+            total = total + ra1[k, d, r].astype(jnp.float32)
+        sa1[d, r] = total.astype(jnp.bfloat16)
+        return carry
+
+    lax.fori_loop(0, 4, add_a1, 0)
+
+    copies = []
+    for k in range(1, XC):
+        there = lax.rem(x + k, XC)
+        copies.append(send(sa0.at[there], rb0.at[k - 1], b_send.at[k - 1], b_recv.at[k - 1], at_x(k)))
+    for k in range(1, 4):
+        to = at_y(k)
+        copies.append(send(sa1.at[to[1], to[0]], rb1.at[k - 1], b_send.at[k + 2], b_recv.at[k + 2], to))
+    for c in copies:
+        c.wait()
+
+    def add_b(i, carry):
+        total = sa0[x, i].astype(jnp.float32)
+        for k in range(XC - 1):
+            total = total + rb0[k, i].astype(jnp.float32)
+        sb[i] = total.astype(jnp.bfloat16)
+        total = sa1[dp, rep, i].astype(jnp.float32)
+        for k in range(3):
+            total = total + rb1[k, i].astype(jnp.float32)
+        sb[i + half] = total.astype(jnp.bfloat16)
+        return carry
+
+    lax.fori_loop(0, half, add_b, 0)
+
+    copies = []
+    for k in range(1, ZC):
+        there = lax.rem(z + k, ZC)
+        copies.append(send(sb.at[there], rc.at[k - 1], c_send.at[k - 1], c_recv.at[k - 1], at_z(k)))
+    for c in copies:
+        c.wait()
+    total = sb[z].astype(jnp.float32)
+    for k in range(ZC - 1):
+        total = total + rc[k].astype(jnp.float32)
+    out[core, rep, x, z] = total.astype(jnp.bfloat16)
+
+    copies = []
+    for k in range(1, ZC):
+        mine = out.at[core, rep, x, z]
+        copies.append(send(mine, mine, d_send.at[k - 1], d_recv.at[k - 1], at_z(k)))
+    for c in copies:
+        c.wait()
+    mine = out.at[core, rep, x]
+    to_rep = send(mine, mine, e_send, e_recv, other_rep)
+    handed = [send(mine, mine, h_send.at[0], h_recv.at[0], other_core)]
+    to_rep.wait()
+    theirs = out.at[core, 1 - rep, x]
+    both = out.at[core, :, x]
+    copies = []
+    for k in range(1, XC):
+        copies.append(send(both, both, f_send.at[k - 1], f_recv.at[k - 1], at_x(k)))
+    handed.append(send(theirs, theirs, h_send.at[1], h_recv.at[1], other_core))
+    for k in range(1, XC):
+        copies[k - 1].wait()
+        came = lax.rem(x + XC - k, XC)
+        piece = out.at[core, :, came]
+        handed.append(send(piece, piece, h_send.at[k + 1], h_recv.at[k + 1], other_core))
+    for c in handed:
+        c.wait()
+
+
+def reduce_all(g):
+    tail = g.shape[4:]
+    half = ZC // 2
+    bf = jnp.bfloat16
+    dma = pltpu.SemaphoreType.DMA
+    return pl.pallas_call(
+        reduce_kernel,
+        out_shape=jax.ShapeDtypeStruct((2, 2, XC, ZC) + tail, bf),
+        in_specs=[pl.BlockSpec(memory_space=pltpu.VMEM)],
+        out_specs=pl.BlockSpec(memory_space=pltpu.VMEM),
+        scratch_shapes=[
+            pltpu.VMEM((3, XC, half) + tail, bf),
+            pltpu.VMEM((XC - 1, 2, 2, half) + tail, bf),
+            pltpu.VMEM((XC, half) + tail, bf),
+            pltpu.VMEM((2, 2, half) + tail, bf),
+            pltpu.VMEM((XC - 1, half) + tail, bf),
+            pltpu.VMEM((3, half) + tail, bf),
+            pltpu.VMEM((ZC,) + tail, bf),
+            pltpu.VMEM((ZC - 1,) + tail, bf),
+            dma((6,)), dma((6,)), dma((6,)), dma((6,)),
+            dma((ZC - 1,)), dma((ZC - 1,)), dma((ZC - 1,)), dma((ZC - 1,)),
+            dma, dma, dma((XC - 1,)), dma((XC - 1,)), dma((XC + 1,)), dma((XC + 1,)),
+        ],
+        compiler_params=pltpu.CompilerParams(
+            collective_id=0, has_side_effects=True, vmem_limit_bytes=40 << 20
+        ),
+        cost_estimate=pl.CostEstimate(flops=10_000_000, bytes_accessed=60_000_000, transcendentals=0),
+        name="grad_reduce",
+    )(g)
 
 
 def passed_along(x, axis, by):
@@ -264,13 +429,18 @@
     proj_term = jnp.einsum(
         "tc,tj->cj", restored_rows, cotangent_rows, preferred_element_type=jnp.float32
     )
-    halves = lax.psum_scatter(
-        jnp.concatenate([qkv_term, proj_term], axis=1).astype(jnp.bfloat16),
-        "dp",
-        scatter_dimension=0,
-        tiled=True,
-    ).astype(jnp.float32)
-    totals = lax.psum(halves, ("rep", "seq"))
+    grads = jnp.concatenate([qkv_term, proj_term], axis=1)
+    width = grads.shape[1] // 2
+    odd = seq_index % 2 == 1
+    mine = jnp.where(odd, grads[:, width:], grads[:, :width])
+    given = jnp.where(odd, grads[:, :width], grads[:, width:]).astype(jnp.bfloat16)
+    mine = mine + from_partner(given, "seq", 0).astype(jnp.float32)
+    tiles = mine.reshape(2, 2, XC, channels // (32 * XC), 8, width // 128, 128)
+    tiles = tiles.transpose(0, 1, 2, 3, 5, 4, 6).astype(jnp.bfloat16)
+    summed = reduce_all(tiles.reshape(2, 2, XC, ZC, -1, 8, 128))
+    summed = summed.reshape(2, 2, XC, channels // (32 * XC), width // 128, 8, 128)
+    totals = summed.transpose(1, 2, 3, 5, 0, 4, 6).reshape(channels // 2, 2 * width)
+    totals = totals.astype(jnp.float32)
     conv_total, gain_total, scale_total = lax.psum(
         (conv_part, gain_part, scale_part), ("rep", "dp", "seq")
     )

time: 1230 us -> 561 us (0.46)
  blocking collectives: 770 us -> 77.5 us
  Pallas kernels: 0 us -> 58.2 us
  waiting for transfers between devices: 257 us -> 219 us
    psum x1 -> x0, blocking collectives: 692 us -> none  [per_device(): totals = lax.psum(halves, ('rep', 'seq'))]
    pallas_call x0 -> x1, Pallas kernels: none -> 58.2 us  [reduce_all(): pl.pallas_call(reduce_kernel, out_shape=jax.ShapeDtypeStruct((2, 2, XC, Z...]
    reduce_scatter x1 -> x0, waiting for transfers between devices: 57.9 us -> none  [per_device(): lax.psum_scatter(jnp.concatenate([qkv_term, proj_term], axis=1).astype(jn...]
    psum x1, waiting for transfers between devices: 140 us -> 158 us  [per_device(): lax.psum((conv_part, gain_part, scale_part), ('rep', 'dp', 'seq'))]
  transfers between devices with their start and end apart: 14 -> 14, of which waited for: 7 -> 6; matrix products, arithmetic and copies ran while one was open for 7% -> 11% of each run, Pallas kernels for 0% -> 0%
where the time goes in v1:
time: 561 us; the launch traced here: 552 us
  waiting for transfers between devices  219 us (39%)
  blocking collectives  77.5 us (14%)
  Pallas kernels  58.2 us (10%)
  matrix products  57.8 us (10%)
  other arithmetic  52.5 us (9%)
  local copies, waits for them, and re-layouts  47.3 us (8%)
  between operations  21.8 us (4%)
  starting transfers between devices  18.7 us (3%)
    psum x1, waiting for transfers between devices, per_device(): lax.psum((conv_part, gain_part, scale_part), ('rep', 'dp', 'seq'))  158 us
    psum x1, blocking collectives, per_device(): lax.psum((conv_part, gain_part, scale_part), ('rep', 'dp', 'seq'))  77.5 us
    pallas_call x1, Pallas kernels, reduce_all(): pl.pallas_call(reduce_kernel, out_shape=jax.ShapeDtypeStruct((2, 2, XC, Z...  58.2 us
    all_gather x1, waiting for transfers between devices, per_device(): lax.all_gather(w_qkv, 'dp', axis=0, tiled=True)  40.2 us
    all_gather x1, waiting for transfers between devices, per_device(): lax.all_gather(w_proj, 'dp', axis=0, tiled=True)  14.4 us
  transfers between devices with their start and end apart: 14, of which 6 were waited for; matrix products, arithmetic and copies ran while one was open for 11% of the time, Pallas kernels for 0%

profile of v1, /device:TPU:1, one launch (start us, length us, event | category | flops | bytes accessed | tf_op | source)
XLA Modules:
  0.0 552.4 jit_solution(1353303110685424326)
XLA Ops:
  9.0 4.9 collective-permute-start
  21.7 3.6 fusion.190
  27.1 14.4 %all-gather.5.cloned.1.call-done = bf16[768,768]{1,0:T(8,128)(2,1)} async-done(((bf16[384,768]{1,0:T(8,128)(2,1)}), bf16[768,768]{1,0:T(8,128)(2,1)}) %all-gather.5.cloned.1.call-update) | async-done | bytes 1179664 | tf_op jit(solution)/shard_map/all_gather | solution.py:301
  53.8 2.2 reshape_reshape.14
  56.0 2.7 copy.46
  58.7 40.2 %all-gather.3.cloned.1.call-done = bf16[768,2304]{1,0:T(8,128)(2,1)} async-done(((bf16[384,2304]{1,0:T(8,128)(2,1)}), bf16[768,2304]{1,0:T(8,128)(2,1)}) %all-gather.3.cloned.1.call-update) | async-done | bytes 3538960 | tf_op jit(solution)/shard_map/all_gather | solution.py:300
  98.8 3.1 convolution_convert_fusion
  107.5 2.3 copy.40
  117.4 2.3 copy.41
  122.2 3.8 fusion.5
  126.1 4.5 fusion.4
  130.5 10.8 %multiply_reduce_fusion = f32[24]{0:T(128)} fusion(f32[2,24,128,256]{3,2,1,0:T(8,128)} %copy-done.1, f32[2,24,128,256]{3,2,1,0:T(8,128)} %fusion.4, bf16[2,128,24,32]{1,3,2,0:T(8,128)(2,1)} %copy.46, bf16[2,128,24,32]{1,3,2,0:T(8,128)(2,1)} %bitcast.137, bf16[2,128,24,32]{1,3,2,0:T(8,128)(2,1)} %bitcast.141, pred[]{:T(512)S(6)} %eq.29), kind=kOutput, calls=%fused_computation.27 | convolution fusion | flops 216275168 | bytes 13762657 | tf_op jit(solution)/shard_map/sub | solution.py:276
  141.3 10.9 %convolution_bitcast_fusion.1 = f32[2,128,24,32]{1,3,2,0:T(8,128)} fusion(bf16[2,128,24,32]{1,3,2,0:T(8,128)(2,1)} %divide_convert_fusion, bf16[2,128,24,32]{1,3,2,0:T(8,128)(2,1)} %copy-done.21, pred[]{:T(512)S(6)} %eq.29, f32[24]{0:T(128)} %param.16, f32[2,24,128,256]{3,2,1,0:T(8,128)} %fusion.4, bf16[2,128,24,32]{1,3,2,0:T(8,128)(2,1)} %copy.46, ...), kind=kOutput, calls=%fused_computation.64 | convolution fusion | flops 320477440 | bytes 9044065 | tf_op jit(solution)/shard_map/whqk,wkhe->wqhe/dot_general | solution.py:280
  152.2 5.2 fusion.31
  157.4 10.9 %convolution_bitcast_fusion = f32[2,256,24,32]{1,3,2,0:T(8,128)} fusion(f32[2,128,24,32]{1,3,2,0:T(8,128)} %bitcast.155, f32[2,128,24]{1,2,0:T(8,128)} %get-tuple-element.90, f32[24]{0:T(128)} %param.16, f32[2,24,128,256]{3,2,1,0:T(8,128)} %fusion.4, bf16[2,128,24,32]{1,3,2,0:T(8,128)(2,1)} %copy.46, bf16[2,128,24,32]{1,3,2,0:T(8,128)(2,1)} %bitcast.140, ...), kind=kOutput, calls=%fused_computation.53 | convolution fusion | flops 317331712 | bytes 9855073 | tf_op jit(solution)/shard_map/whqk,wqhe->wkhe/dot_general | solution.py:281
  168.3 4.7 fusion.15
  173.0 2.5 copy.43
  175.5 3.3 reshape_reshape.13
  185.9 2.5 copy.47
  188.4 2.9 concatenate.69
  192.9 2.5 fusion.34
  200.8 2.6 copy.49
  203.4 3.0 concatenate.70
  208.0 2.3 concatenate.71
  222.6 2.6 fusion.90
  226.5 2.6 stack.126
  229.2 77.5 %all-reduce.2 = (f32[768]{0:T(1024)S(1)}, f32[24]{0:T(128)S(1)}) all-reduce(f32[768]{0:T(1024)S(1)} %copy-done.58, f32[24]{0:T(128)S(1)} %copy-done.59), channel_id=1, replica_groups=mesh['rep'=2,'dp'=2,'seq'=64] {'rep','dp','seq'}, use_global_device_ids=true, to_apply=%region_40.42 | all-reduce | flops 792 | bytes 6336 | tf_op jit(solution)/shard_map/psum | solution.py:444
  307.8 4.6 collective-permute-start.8
  314.3 158.1 %all-reduce.5.cloned.1.call-done = f32[27,768]{1,0:T(8,128)} async-done(((f32[27,768]{1,0:T(8,128)}), f32[27,768]{1,0:T(8,128)}) %all-reduce.5.cloned.1.call-update) | async-done | bytes 82960 | tf_op jit(solution)/shard_map/psum | solution.py:444
  474.3 3.9 fusion.168
  478.2 5.0 add_convert_fusion
  483.1 58.2 %grad_reduce.1 = bf16[2,2,4,8,9,8,128]{6,5,4,3,2,1,0:T(8,128)(2,1)S(1)} custom-call(bf16[2,2,4,8,9,8,128]{6,5,4,3,2,1,0:T(8,128)(2,1)S(1)} %bitcast.126), custom_call_target="tpu_custom_call" | custom-call | flops 10000000 | bytes 60000000 | tf_op jit(solution)/shard_map/grad_reduce/pallas_call | solution.py:151
  (249 shorter events, 70.0 us)
Async XLA Ops:
  7.2 34.3 %all-gather.5.cloned.1.call-start = ((), (), s32[]{:S(2)}) async-start(), calls=%async_computation.1 | async-start | bytes 1769472 | tf_op jit(solution)/shard_map/all_gather | solution.py:301
  7.9 90.9 %all-gather.3.cloned.1.call-start = ((), (), s32[]{:S(2)}) async-start(), calls=%async_computation | async-start | bytes 5308416 | tf_op jit(solution)/shard_map/all_gather | solution.py:300
  9.0 10.7 %collective-permute-start = (bf16[1,8,16,768]{3,2,1,0:T(8,128)(2,1)S(1)}, bf16[1,8,16,768]{3,2,1,0:T(8,128)(2,1)S(1)}, u32[]{:S(2)}, u32[]{:S(2)}) collective-permute-start(bf16[1,8,16,768]{3,2,1,0:T(8,128)(2,1)S(1)} %get-tuple-element.87), channel_id=1, source_target_pairs={{0,1},{1,2},{2,3},{3,4},{4,5},{5,6},{6,7},{7,8},{8,9},{9,10},{10,1... | collective-permute-start | bytes 589832 | tf_op jit(solution)/shard_map/ppermute | solution.py:189
  14.0 7.0 %collective-permute-start.1 = (bf16[1,8,16,768]{3,2,1,0:T(8,128)(2,1)S(1)}, bf16[1,8,16,768]{3,2,1,0:T(8,128)(2,1)S(1)}, u32[]{:S(2)}, u32[]{:S(2)}) collective-permute-start(bf16[1,8,16,768]{3,2,1,0:T(8,128)(2,1)S(1)} %get-tuple-element.88), channel_id=1, source_target_pairs={{1,0},{2,1},{3,2},{4,3},{5,4},{6,5},{7,6},{8,7},{9,8},{10,9},{11,1... | collective-permute-start | bytes 589832 | tf_op jit(solution)/shard_map/ppermute | solution.py:190
  15.9 456.5 %all-reduce.5.cloned.1.call-start = ((), (), s32[]{:S(2)}) async-start(), calls=%async_computation.2 | async-start | bytes 196608 | tf_op jit(solution)/shard_map/psum | solution.py:444
  25.4 16.1 %copy-start.6 = (bf16[1,2,8,16,768]{4,3,2,1,0:T(8,128)(2,1)S(1)}, bf16[1,2,8,16,768]{4,3,2,1,0:T(8,128)(2,1)}, u32[]{:S(2)}) copy-start(bf16[1,2,8,16,768]{4,3,2,1,0:T(8,128)(2,1)} %param.11) | copy-start | bytes 1179652
  27.1 31.6 %collective-permute-start.2 = (bf16[2,8,16,768]{3,2,1,0:T(8,128)(2,1)}, bf16[2,8,16,768]{3,2,1,0:T(8,128)(2,1)S(1)}, u32[]{:S(2)}, u32[]{:S(2)}) collective-permute-start(bf16[2,8,16,768]{3,2,1,0:T(8,128)(2,1)} %fusion.166), channel_id=1, source_target_pairs={{0,63},{1,0},{2,1},{3,2},{4,3},{5,4},{6,5},{7,6},{8,7},{9,8},{10,9... | collective-permute-start | bytes 1179656 | tf_op jit(solution)/shard_map/ppermute | solution.py:179
  44.5 7.5 %collective-permute-start.5 = (bf16[2,8,16,768]{3,2,1,0:T(8,128)(2,1)}, bf16[2,8,16,768]{3,2,1,0:T(8,128)(2,1)S(1)}, u32[]{:S(2)}, u32[]{:S(2)}) collective-permute-start(bf16[2,8,16,768]{3,2,1,0:T(8,128)(2,1)} %fusion.162), channel_id=1, source_target_pairs={{0,63},{1,0},{2,1},{3,2},{4,3},{5,4},{6,5},{7,6},{8,7},{9,8},{10,9... | collective-permute-start | bytes 1179656 | tf_op jit(solution)/shard_map/ppermute | solution.py:179
  58.7 43.3 %copy-start.18 = (bf16[2,8,16,768]{3,2,1,0:T(8,128)(2,1)}, bf16[2,8,16,768]{3,2,1,0:T(8,128)(2,1)S(1)}, u32[]{:S(2)}) copy-start(bf16[2,8,16,768]{3,2,1,0:T(8,128)(2,1)S(1)} %collective-permute-done.2) | copy-start | bytes 1179652
  102.9 10.3 %collective-permute-start.3 = (bf16[2,8,16,1536]{3,2,1,0:T(8,128)(2,1)}, bf16[2,8,16,1536]{3,2,1,0:T(8,128)(2,1)}, u32[]{:S(2)}, u32[]{:S(2)}) collective-permute-start(bf16[2,8,16,1536]{3,2,1,0:T(8,128)(2,1)} %slice.506), channel_id=1, source_target_pairs={{0,1},{1,0},{2,3},{3,2},{4,5},{5,4},{6,7},{7,6},{8,9},{9,8},{10,11... | collective-permute-start | bytes 2359304 | tf_op jit(solution)/shard_map/ppermute | solution.py:196
  180.8 10.6 %collective-permute-start.4 = (bf16[2,8,16,768]{3,2,1,0:T(8,128)(2,1)}, bf16[2,8,16,768]{3,2,1,0:T(8,128)(2,1)}, u32[]{:S(2)}, u32[]{:S(2)}) collective-permute-start(bf16[2,8,16,768]{3,2,1,0:T(8,128)(2,1)} %copy_bitcast_fusion), channel_id=1, source_target_pairs={{0,1},{1,2},{2,3},{3,4},{4,5},{5,6},{6,7},{7,8},{8,9},{9,10},{10,1... | collective-permute-start | bytes 1179656 | tf_op jit(solution)/shard_map/ppermute | solution.py:179
  184.9 12.4 %collective-permute-start.6 = (bf16[2,2,128,24,32]{2,4,3,1,0:T(8,128)(2,1)}, bf16[2,2,128,24,32]{2,4,3,1,0:T(8,128)(2,1)}, u32[]{:S(2)}, u32[]{:S(2)}) collective-permute-start(bf16[2,2,128,24,32]{2,4,3,1,0:T(8,128)(2,1)} %pad_maximum_fusion.1), channel_id=1, source_target_pairs={{0,1},{1,0},{2,3},{3,2},{4,5},{5,4},{6,7},{7,6},{8,9},{9,8},{10,11... | collective-permute-start | bytes 2359304 | tf_op jit(solution)/shard_map/ppermute | solution.py:196
  214.7 6.6 %collective-permute-start.7 = (bf16[2,8,16,768]{3,2,1,0:T(8,128)(2,1)S(1)}, bf16[2,8,16,768]{3,2,1,0:T(8,128)(2,1)S(1)}, u32[]{:S(2)}, u32[]{:S(2)}) collective-permute-start(bf16[2,8,16,768]{3,2,1,0:T(8,128)(2,1)S(1)} %bitcast.162), channel_id=1, source_target_pairs={{0,1},{1,2},{2,3},{3,4},{4,5},{5,6},{6,7},{7,8},{8,9},{9,10},{10,1... | collective-permute-start | bytes 1179656 | tf_op jit(solution)/shard_map/ppermute | solution.py:179
  218.8 259.4 %collective-permute-start.10 = (bf16[768,1536]{1,0:T(8,128)(2,1)}, bf16[768,1536]{1,0:T(8,128)(2,1)}, u32[]{:S(2)}, u32[]{:S(2)}) collective-permute-start(bf16[768,1536]{1,0:T(8,128)(2,1)} %select_convert_fusion), channel_id=1, source_target_pairs={{0,1},{1,0},{2,3},{3,2},{4,5},{5,4},{6,7},{7,6},{8,9},{9,8},{10,11... | collective-permute-start | bytes 7077896 | tf_op jit(solution)/shard_map/ppermute | solution.py:196
  226.1 248.1 %copy-start.25 = (f32[768]{0:T(1024)S(1)}, f32[768]{0:T(1024)}, u32[]{:S(2)}) copy-start(f32[768]{0:T(1024)} %copy-done.24) | copy-start | bytes 9220
  226.1 248.1 %copy-start.27 = (f32[768]{0:T(1024)S(1)}, f32[768]{0:T(1024)}, u32[]{:S(2)}) copy-start(f32[768]{0:T(1024)} %copy-done.26) | copy-start | bytes 9220
  226.1 248.1 %copy-start.29 = (f32[768]{0:T(1024)S(1)}, f32[768]{0:T(1024)}, u32[]{:S(2)}) copy-start(f32[768]{0:T(1024)} %copy-done.28) | copy-start | bytes 9220
  226.1 248.1 %copy-start.31 = (f32[768]{0:T(1024)S(1)}, f32[768]{0:T(1024)}, u32[]{:S(2)}) copy-start(f32[768]{0:T(1024)} %copy-done.30) | copy-start | bytes 9220
  226.1 248.1 %copy-start.33 = (f32[768]{0:T(1024)S(1)}, f32[768]{0:T(1024)}, u32[]{:S(2)}) copy-start(f32[768]{0:T(1024)} %copy-done.32) | copy-start | bytes 9220
  226.1 248.1 %copy-start.35 = (f32[768]{0:T(1024)S(1)}, f32[768]{0:T(1024)}, u32[]{:S(2)}) copy-start(f32[768]{0:T(1024)} %copy-done.34) | copy-start | bytes 9220
  226.1 248.1 %copy-start.37 = (f32[768]{0:T(1024)S(1)}, f32[768]{0:T(1024)}, u32[]{:S(2)}) copy-start(f32[768]{0:T(1024)} %copy-done.36) | copy-start | bytes 9220
  226.1 248.1 %copy-start.39 = (f32[768]{0:T(1024)S(1)}, f32[768]{0:T(1024)}, u32[]{:S(2)}) copy-start(f32[768]{0:T(1024)} %copy-done.38) | copy-start | bytes 9220
  226.1 248.1 %copy-start.41 = (f32[768]{0:T(1024)S(1)}, f32[768]{0:T(1024)}, u32[]{:S(2)}) copy-start(f32[768]{0:T(1024)} %copy-done.40) | copy-start | bytes 9220
  226.1 248.1 %copy-start.43 = (f32[768]{0:T(1024)S(1)}, f32[768]{0:T(1024)}, u32[]{:S(2)}) copy-start(f32[768]{0:T(1024)} %copy-done.42) | copy-start | bytes 9220
  226.2 248.1 %copy-start.45 = (f32[768]{0:T(1024)S(1)}, f32[768]{0:T(1024)}, u32[]{:S(2)}) copy-start(f32[768]{0:T(1024)} %copy-done.44) | copy-start | bytes 9220
  226.2 248.1 %copy-start.47 = (f32[768]{0:T(1024)S(1)}, f32[768]{0:T(1024)}, u32[]{:S(2)}) copy-start(f32[768]{0:T(1024)} %copy-done.46) | copy-start | bytes 9220
  226.2 248.1 %copy-start.49 = (f32[768]{0:T(1024)S(1)}, f32[768]{0:T(1024)}, u32[]{:S(2)}) copy-start(f32[768]{0:T(1024)} %copy-done.48) | copy-start | bytes 9220
  226.2 248.1 %copy-start.51 = (f32[768]{0:T(1024)S(1)}, f32[768]{0:T(1024)}, u32[]{:S(2)}) copy-start(f32[768]{0:T(1024)} %copy-done.50) | copy-start | bytes 9220
  226.2 248.1 %copy-start.53 = (f32[768]{0:T(1024)S(1)}, f32[768]{0:T(1024)}, u32[]{:S(2)}) copy-start(f32[768]{0:T(1024)} %copy-done.52) | copy-start | bytes 9220
  226.2 248.1 %copy-start.55 = (f32[768]{0:T(1024)S(1)}, f32[768]{0:T(1024)}, u32[]{:S(2)}) copy-start(f32[768]{0:T(1024)} %copy-done.54) | copy-start | bytes 9220
  307.8 166.2 %collective-permute-start.8 = (bf16[1,8,16,768]{3,2,1,0:T(8,128)(2,1)S(1)}, bf16[1,8,16,768]{3,2,1,0:T(8,128)(2,1)S(1)}, u32[]{:S(2)}, u32[]{:S(2)}) collective-permute-start(bf16[1,8,16,768]{3,2,1,0:T(8,128)(2,1)S(1)} %get-tuple-element.85), channel_id=1, source_target_pairs={{0,1},{1,2},{2,3},{3,4},{4,5},{5,6},{6,7},{7,8},{8,9},{9,10},{10,1... | collective-permute-start | bytes 589832 | tf_op jit(solution)/shard_map/ppermute | solution.py:189
  312.4 161.6 %collective-permute-start.9 = (bf16[1,8,16,768]{3,2,1,0:T(8,128)(2,1)S(1)}, bf16[1,8,16,768]{3,2,1,0:T(8,128)(2,1)S(1)}, u32[]{:S(2)}, u32[]{:S(2)}) collective-permute-start(bf16[1,8,16,768]{3,2,1,0:T(8,128)(2,1)S(1)} %get-tuple-element.86), channel_id=1, source_target_pairs={{1,0},{2,1},{3,2},{4,3},{5,4},{6,5},{7,6},{8,7},{9,8},{10,9},{11,1... | collective-permute-start | bytes 589832 | tf_op jit(solution)/shard_map/ppermute | solution.py:190
  (46 other events, 271.5 us)
Sparse Core Ops, SparseCore 0:
  9.8 31.6 all-gather.4
  43.3 55.4 all-gather.2
  229.3 243.1 all-reduce.4

commit v2 on v1

v2 whole, which is shorter than its diff:
```python
import math

import jax
import jax.numpy as jnp
from jax import lax
from jax.experimental import pallas as pl
from jax.experimental.pallas import tpu as pltpu
from jax.sharding import PartitionSpec as P

MESH = pl.DeviceIdType.MESH
BF = jnp.bfloat16
F32 = jnp.float32
XC = 4
ZC = 8
SEQ = 64
C = 768
MINE = 384
VMEM = pl.BlockSpec(memory_space=pltpu.VMEM)
SMEM = pl.BlockSpec(memory_space=pltpu.SMEM)
DMA = pltpu.SemaphoreType.DMA


def nn(a, b):
    return lax.dot_general(a, b, (((1,), (0,)), ((), ())), preferred_element_type=F32)


def nt(a, b):
    return lax.dot_general(a, b, (((1,), (1,)), ((), ())), preferred_element_type=F32)


def tn(a, b):
    return lax.dot_general(a, b, (((0,), (0,)), ((), ())), preferred_element_type=F32)


def iota(shape, dim):
    return lax.broadcasted_iota(jnp.int32, shape, dim)


def place():
    rep, dp, seq = lax.axis_index("rep"), lax.axis_index("dp"), lax.axis_index("seq")
    return (rep, dp, seq, lax.rem(seq, 2))


def send(src, dst, s, r, to):
    c = pltpu.make_async_remote_copy(
        src_ref=src, dst_ref=dst, send_sem=s, recv_sem=r, device_id=to, device_id_type=MESH
    )
    c.start()
    return c


def greet(peers):
    barrier = pltpu.get_barrier_semaphore()
    for peer in peers:
        pl.semaphore_signal(barrier, inc=1, device_id=peer, device_id_type=MESH)
    pl.semaphore_wait(barrier, len(peers))


def fill_padded(xf, before, own, after):
    rows = jnp.zeros((4, 1, 16, C), F32)
    xf[:, 0:1] = rows
    xf[:, 9:10] = rows
    xf[0, 1:9] = before
    xf[1:3, 1:9] = own
    xf[3, 1:9] = after


def taps(xf, weight, d, lanes, flipped):
    sums = [jnp.zeros((8, 16, 128), F32) for _ in range(3)]
    for a in range(3):
        for b in range(3):
            rows = xf[d + a, b : b + 8, :, lanes]
            for e in range(3):
                t = 9 * a + 3 * b + e
                t = 26 - t if flipped else t
                sums[e] = sums[e] + weight[t : t + 1, lanes][None] * rows
    w = iota((8, 16, 128), 1)
    left = jnp.where(w == 0, 0.0, pltpu.roll(sums[0], 1, 1))
    right = jnp.where(w == 15, 0.0, pltpu.roll(sums[2], 15, 1))
    return sums[1] + left + right


def chunk(j):
    return pl.ds(pl.multiple_of(j * 128, 128), 128)


def normalise(rows):
    centred = rows - jnp.mean(rows, axis=-1, keepdims=True)
    inverse = lax.rsqrt(jnp.mean(centred * centred, axis=-1, keepdims=True) + 1e-05)
    return (centred * inverse, inverse)


def mix_kernel(tokens, cot, wq_in, wp_in, weight, gain, nwin, cwin, wq, wp, mixed, halo,
               xf, h_send, h_recv, w_send, w_recv, l_sem):
    rep, dp, seq, core = place()
    y = rep * 2 + dp
    up = (rep, dp, lax.rem(seq + 1, SEQ))
    down = (rep, dp, lax.rem(seq + SEQ - 1, SEQ))
    partner = (rep, dp, lax.rem(seq + SEQ - 1 + 2 * core, SEQ))
    other_core = (rep, dp, seq + 1 - 2 * core)
    y_to = lax.rem(y + 3 + 2 * core, 4)
    y_from = lax.rem(y + 1 + 2 * core, 4)
    y_peer = (y_to // 2, lax.rem(y_to, 2), seq)
    y_source = (y_from // 2, lax.rem(y_from, 2), seq)
    greet([up, down, y_peer, y_source])
    own = 1 - core
    halos = [
        send(tokens.at[0], halo.at[1], h_send.at[0], h_recv.at[0], down),
        send(tokens.at[1], halo.at[0], h_send.at[1], h_recv.at[1], up),
    ]
    weights = [
        send(wq_in.at[core], wq.at[core, dp], w_send.at[0], w_recv.at[0], y_peer),
        send(wp_in.at[core], wp.at[core, dp], w_send.at[1], w_recv.at[1], y_peer),
    ]
    cots = send(cot, cwin.at[own], h_send.at[2], h_recv.at[2], partner)
    local = [
        pltpu.make_async_copy(cot, cwin.at[own], l_sem.at[0]),
        pltpu.make_async_copy(wq_in, wq.at[:, dp], l_sem.at[1]),
        pltpu.make_async_copy(wp_in, wp.at[:, dp], l_sem.at[2]),
    ]
    for c in local:
        c.start()
    for c in halos:
        c.wait()
    first = jnp.where(seq == 0, 0.0, 1.0).astype(F32)
    last = jnp.where(seq == SEQ - 1, 0.0, 1.0).astype(F32)
    fill_padded(xf, halo[0].astype(F32) * first, tokens[...].astype(F32), halo[1].astype(F32) * last)

    def filter_step(i, carry):
        d, j = i // 6, lax.rem(i, 6)
        lanes = chunk(j)
        mixed[d, :, :, lanes] = xf[d + 1, 1:9, :, lanes] + taps(xf, weight, d, lanes, False)
        return carry

    lax.fori_loop(0, 12, filter_step, 0)

    def norm_step(i, carry):
        d, h = i // 2, lax.rem(i, 2) * 4
        unit, _ = normalise(mixed[d, pl.ds(h, 4)].reshape(64, C))
        nwin[own, pl.ds(pl.multiple_of(i * 64, 64), 64)] = (unit * gain[...]).astype(BF)
        return carry

    lax.fori_loop(0, 4, norm_step, 0)
    norms = send(nwin.at[own], nwin.at[own], h_send.at[3], h_recv.at[3], partner)
    for c in weights:
        c.wait()
    back = [
        send(wq.at[core, 1 - dp], wq.at[core, 1 - dp], w_send.at[2], w_recv.at[2], other_core),
        send(wp.at[core, 1 - dp], wp.at[core, 1 - dp], w_send.at[3], w_recv.at[3], other_core),
    ]
    for c in local:
        c.wait()
    cots.wait()
    norms.wait()
    for c in back:
        c.wait()


def mix(tokens, cot, wq, wp, weight, gain):
    shape = jax.ShapeDtypeStruct
    return pl.pallas_call(
        mix_kernel,
        out_shape=(
            shape((2, 256, C), BF), shape((2, 256, C), BF),
            shape((2, 2, MINE, 3 * MINE), BF), shape((2, 2, MINE // 2, C), BF),
            shape((2, 8, 16, C), F32), shape((2, 8, 16, C), BF),
        ),
        in_specs=[VMEM] * 6,
        out_specs=(VMEM,) * 6,
        scratch_shapes=[
            pltpu.VMEM((4, 10, 16, C), F32),
            DMA((4,)), DMA((4,)), DMA((4,)), DMA((4,)), DMA((3,)),
        ],
        compiler_params=pltpu.CompilerParams(
            collective_id=1, has_side_effects=True, vmem_limit_bytes=48 << 20
        ),
        name="mix",
    )(tokens, cot, wq, wp, weight, gain)


def source_of(n, r):
    b, d, h, j = n >> 8, (n >> 6) & 3, (n >> 3) & 7, n & 7
    return d * 128 + h * 16 + ((8 * b + j + r) & 15)


def head_sums(x, ones):
    high = x.astype(BF)
    low = (x - high.astype(F32)).astype(BF)
    return nn(high, ones) + nn(low, ones)


def attend_kernel(shift, scales, nwin, cwin, wq, wp, own_out, given_out, g_out, scale_out,
                  x_s, ct_s, qkv_s, ba_s, att_s, bqkv_s, allow_s, gq_s, gp_s):
    core = lax.rem(lax.axis_index("seq"), 2)
    s, r = shift[0], shift[1]
    select = jnp.where(iota((512, 512), 1) == source_of(iota((512, 512), 0), r), 1.0, 0.0).astype(BF)
    x_s[...] = nn(select, nwin[...].reshape(512, C)).astype(BF)
    ct_s[...] = nn(select, cwin[...].reshape(512, C)).astype(BF)
    qkv_s[...] = nn(x_s[...], wq[core].reshape(C, 3 * MINE)).astype(BF)
    ba_s[...] = nt(ct_s[...], wp[core].reshape(MINE, C)).astype(BF)

    def code(n, b):
        h, j = (n >> 3) & 7, n & 7
        return jnp.where(h < s, 2, 0) + jnp.where(8 * b + j + r >= 16, 1, 0)

    for b in range(2):
        same = code(iota((256, 256), 0), b) == code(iota((256, 256), 1), b)
        allow_s[b] = jnp.where(same, 1.0, 0.0).astype(F32)
    ones = jnp.where(iota((128, 128), 0) // 32 == iota((128, 128), 1) // 32, 1.0, 0.0).astype(BF)
    lane_head = iota((256, 128), 1) // 32

    def group(i, carry):
        b, g = i // 3, lax.rem(i, 3)
        rows = pl.ds(pl.multiple_of(b * 256, 256), 256)

        def part(k):
            return pl.ds(pl.multiple_of(g * 128 + k * MINE, 128), 128)

        query = qkv_s[rows, part(0)].astype(F32)
        key = qkv_s[rows, part(1)].astype(F32)
        value = qkv_s[rows, part(2)]
        ba = ba_s[rows, part(0)]
        inv_q = lax.rsqrt(head_sums(query * query, ones) + 1.0)
        inv_k = lax.rsqrt(head_sums(key * key, ones) + 1.0)
        uq = (query * inv_q).astype(BF)
        uk = (key * inv_k).astype(BF)
        att = jnp.zeros((256, 128), F32)
        back_v = jnp.zeros((256, 128), F32)
        back_uq = jnp.zeros((256, 128), F32)
        back_uk = jnp.zeros((256, 128), F32)
        zero = jnp.zeros((256, 128), BF)
        for h in range(4):
            here = lane_head == h
            scale = scales[core, g * 4 + h]
            uq_h = jnp.where(here, uq, zero)
            uk_h = jnp.where(here, uk, zero)
            v_h = jnp.where(here, value, zero)
            ba_h = jnp.where(here, ba, zero)
            cosine = nt(uk_h, uq)
            expo = jnp.exp(scale * cosine) * allow_s[b]
            prob = expo * (1.0 / jnp.sum(expo, axis=0, keepdims=True))
            weights = prob.astype(BF)
            att = att + tn(weights, v_h)
            back_v = back_v + nn(weights, ba_h)
            back_prob = nt(v_h, ba)
            mean = jnp.sum(prob * back_prob, axis=0, keepdims=True)
            back_score = prob * (back_prob - mean)
            scale_out[b, pl.ds(g * 4 + h, 1)] = jnp.sum(back_score * cosine, axis=0, keepdims=True)
            scaled = (back_score * scale).astype(BF)
            back_uq = back_uq + tn(scaled, uk_h)
            back_uk = back_uk + nn(scaled, uq_h)
        att_s[rows, part(0)] = att.astype(BF)
        inner_q = head_sums(query * back_uq, ones)
        inner_k = head_sums(key * back_uk, ones)
        back_q = back_uq * inv_q - query * inner_q * (inv_q * inv_q * inv_q)
        back_k = back_uk * inv_k - key * inner_k * (inv_k * inv_k * inv_k)
        bqkv_s[rows, part(0)] = back_q.astype(BF)
        bqkv_s[rows, part(1)] = back_k.astype(BF)
        bqkv_s[rows, part(2)] = back_v.astype(BF)
        return carry

    lax.fori_loop(0, 6, group, 0)
    for half, out in ((1 - core, own_out), (core, given_out)):
        target = source_of(iota((256, 512), 1), r)
        restore = jnp.where(iota((256, 512), 0) + 256 * half == target, 1.0, 0.0).astype(BF)
        out[:, 0:MINE] = nn(restore, att_s[...]).astype(BF)
        out[:, MINE:] = nn(restore, bqkv_s[...]).astype(BF)
    gq_s[...] = tn(x_s[...], bqkv_s[...])
    gp_s[...] = tn(att_s[...], ct_s[...])

    def store(i, carry):
        d, p, x = i // 8, lax.rem(i // 4, 2), lax.rem(i, 4)
        for c in range(9):
            block = gq_s[pl.ds(pl.multiple_of(i * 48, 48), 48), c * 128 : (c + 1) * 128]
            g_out[d, p, x, c * 6 : c * 6 + 6] = block.reshape(6, 8, 128).astype(BF)
        for c in range(6):
            block = gp_s[pl.ds(pl.multiple_of(i * 24, 24), 24), c * 128 : (c + 1) * 128]
            g_out[d, p, x, 54 + c * 3 : 57 + c * 3] = block.reshape(3, 8, 128).astype(BF)
        return carry

    lax.fori_loop(0, 16, store, 0)


def attend(shift, scales, nwin, cwin, wq, wp):
    shape = jax.ShapeDtypeStruct
    return pl.pallas_call(
        attend_kernel,
        out_shape=(
            shape((256, 4 * MINE), BF), shape((256, 4 * MINE), BF),
            shape((2, 2, XC, 72, 8, 128), BF), shape((2, 12, 256), F32),
        ),
        in_specs=[SMEM, SMEM] + [VMEM] * 4,
        out_specs=(VMEM,) * 4,
        scratch_shapes=[
            pltpu.VMEM((512, C), BF), pltpu.VMEM((512, C), BF),
            pltpu.VMEM((512, 3 * MINE), BF), pltpu.VMEM((512, MINE), BF),
            pltpu.VMEM((512, MINE), BF), pltpu.VMEM((512, 3 * MINE), BF),
            pltpu.VMEM((2, 256, 256), F32), pltpu.VMEM((C, 3 * MINE), F32), pltpu.VMEM((MINE, C), F32),
        ],
        compiler_params=pltpu.CompilerParams(vmem_limit_bytes=48 << 20),
        name="attend",
    )(shift, scales, nwin, cwin, wq, wp)


def project_kernel(own, recv, wq, wp, mixed, cot, gain, out, bm, bmh, gain_out, bn_s):
    _, _, _, core = place()
    proj = nn(own[:, 0:MINE], wp[core].reshape(MINE, C))
    proj = proj + nn(recv[:, 0:MINE], wp[1 - core].reshape(MINE, C))
    out[...] = (mixed[...].reshape(256, C) + proj).astype(BF).reshape(2, 8, 16, C)
    back = nt(own[:, MINE:], wq[core].reshape(C, 3 * MINE))
    back = back + nt(recv[:, MINE:], wq[1 - core].reshape(C, 3 * MINE))
    bn_s[...] = back.astype(BF)

    def step(i, total):
        d, h = i // 2, lax.rem(i, 2) * 4
        rows = pl.ds(pl.multiple_of(i * 64, 64), 64)
        unit, inverse = normalise(mixed[d, pl.ds(h, 4)].reshape(64, C))
        back_float = bn_s[rows].astype(F32)
        total = total + jnp.sum((back_float * unit).reshape(8, 8, C), axis=0)
        grad_unit = back_float * gain[...]
        mean = jnp.mean(grad_unit, axis=-1, keepdims=True)
        slope = jnp.mean(grad_unit * unit, axis=-1, keepdims=True)
        result = cot[rows].astype(F32) + inverse * (grad_unit - mean - unit * slope)
        bm[d, pl.ds(h, 4)] = result.reshape(4, 16, C)
        bmh[d, pl.ds(h, 4)] = result.astype(BF).reshape(4, 16, C)
        return total

    total = lax.fori_loop(0, 4, step, jnp.zeros((8, C), F32))
    gain_out[...] = jnp.sum(total, axis=0, keepdims=True)


def project(own, recv, wq, wp, mixed, cot, gain):
    shape = jax.ShapeDtypeStruct
    field = (2, 8, 16, C)
    return pl.pallas_call(
        project_kernel,
        out_shape=(shape(field, BF), shape(field, F32), shape(field, BF), shape((1, C), F32)),
        in_specs=[VMEM] * 7,
        out_specs=(VMEM,) * 4,
        scratch_shapes=[pltpu.VMEM((256, C), BF)],
        compiler_params=pltpu.CompilerParams(vmem_limit_bytes=48 << 20),
        name="project",
    )(own, recv, wq, wp, mixed, cot, gain)


def unmix_kernel(bm, before, after, tokens, halo, weight, grad, conv_out, xf, tf, sh):
    _, _, seq, _ = place()
    first = jnp.where(seq == 0, 0.0, 1.0).astype(F32)
    last = jnp.where(seq == SEQ - 1, 0.0, 1.0).astype(F32)
    fill_padded(xf, before[...].astype(F32) * first, bm[...], after[...].astype(F32) * last)
    fill_padded(tf, halo[0].astype(F32) * first, tokens[...].astype(F32), halo[1].astype(F32) * last)

    def step(i, carry):
        d, j = i // 6, lax.rem(i, 6)
        lanes = chunk(j)
        own = xf[d + 1, 1:9, :, lanes]
        grad[d, :, :, lanes] = (own + taps(xf, weight, d, lanes, True)).astype(BF)
        w = iota((8, 16, 128), 1)
        sh[0, d, :, :, lanes] = jnp.where(w == 15, 0.0, pltpu.roll(own, 15, 1))
        sh[1, d, :, :, lanes] = own
        sh[2, d, :, :, lanes] = jnp.where(w == 0, 0.0, pltpu.roll(own, 1, 1))
        return carry

    lax.fori_loop(0, 12, step, 0)

    def conv_step(j, carry):
        lanes = chunk(j)
        for a in range(3):
            for b in range(3):
                rows = tf[a : a + 2, b : b + 8, :, lanes]
                for e in range(3):
                    total = jnp.sum((sh[e, :, :, :, lanes] * rows).reshape(16, 16, 128), axis=0)
                    t = 9 * a + 3 * b + e
                    conv_out[t : t + 1, lanes] = jnp.sum(total, axis=0, keepdims=True)
        return carry

    lax.fori_loop(0, 6, conv_step, 0)


def unmix(bm, before, after, tokens, halo, weight):
    shape = jax.ShapeDtypeStruct
    return pl.pallas_call(
        unmix_kernel,
        out_shape=(shape((2, 8, 16, C), BF), shape((27, C), F32)),
        in_specs=[VMEM] * 6,
        out_specs=(VMEM,) * 2,
        scratch_shapes=[
            pltpu.VMEM((4, 10, 16, C), F32), pltpu.VMEM((4, 10, 16, C), F32),
            pltpu.VMEM((3, 2, 8, 16, C), F32),
        ],
        compiler_params=pltpu.CompilerParams(vmem_limit_bytes=48 << 20),
        name="unmix",
    )(bm, before, after, tokens, halo, weight)


def reduce_kernel(g, small, out, small_out, ra0, ra1, sa0, sa1, rb0, rb1, sb, rc,
                   sy, sx, sz, qa, qb, qc,
               a_send, a_recv, b_send, b_recv, c_send, c_recv, d_send, d_recv,
                  e_send, e_recv, f_send, f_recv, h_send, h_recv):
    rep, dp, seq = lax.axis_index("rep"), lax.axis_index("dp"), lax.axis_index("seq")
    core = lax.rem(seq, 2)
    z = lax.rem(seq // 2, ZC)
    x = seq // (2 * ZC)
    y = rep * 2 + dp
    half = ZC // 2

    def at_y(step):
        there = lax.rem(y + step, 4)
        return (there // 2, lax.rem(there, 2), seq)

    def at_x(step):
        there = lax.rem(x + step, XC)
        return (rep, dp, (there * ZC + z) * 2 + core)

    def at_z(step):
        there = lax.rem(z + step, ZC)
        return (rep, dp, (x * ZC + there) * 2 + core)

    other_core = (rep, dp, (x * ZC + z) * 2 + 1 - core)
    other_rep = (1 - rep, dp, seq)
    peers = [at_y(k) for k in range(1, 4)] + [at_x(k) for k in range(1, XC)]
    peers += [at_z(k) for k in range(1, ZC)] + [other_core]
    greet(peers)

    copies = []
    for k in range(1, 4):
        to = at_y(k)
        copies.append(send(g.at[to[1], to[0], :, pl.ds(0, half)], ra0.at[k - 1],
                           a_send.at[k - 1], a_recv.at[k - 1], to))
    for k in range(1, XC):
        to = at_x(k)
        there = lax.rem(x + k, XC)
        copies.append(send(g.at[:, :, there, pl.ds(half, half)], ra1.at[k - 1],
                           a_send.at[k + 2], a_recv.at[k + 2], to))
    for k in range(1, 4):
        copies.append(send(small, qa.at[k - 1], a_send.at[k + 5], a_recv.at[k + 5], at_y(k)))
    for c in copies:
        c.wait()

    def add_a0(i, carry):
        total = g[dp, rep, i, pl.ds(0, half)].astype(jnp.float32)
        for k in range(3):
            total = total + ra0[k, i].astype(jnp.float32)
        sa0[i] = total.astype(jnp.bfloat16)
        return carry

    lax.fori_loop(0, XC, add_a0, 0)

    def add_a1(i, carry):
        d, r = lax.rem(i, 2), i // 2
        total = g[d, r, x, pl.ds(half, half)].astype(jnp.float32)
        for k in range(XC - 1):
            total = total + ra1[k, d, r].astype(jnp.float32)
        sa1[d, r] = total.astype(jnp.bfloat16)
        return carry

    lax.fori_loop(0, 4, add_a1, 0)
    sy[...] = small[...] + qa[0] + qa[1] + qa[2]

    copies = []
    for k in range(1, XC):
        there = lax.rem(x + k, XC)
        copies.append(send(sa0.at[there], rb0.at[k - 1], b_send.at[k - 1], b_recv.at[k - 1], at_x(k)))
    for k in range(1, 4):
        to = at_y(k)
        copies.append(send(sa1.at[to[1], to[0]], rb1.at[k - 1], b_send.at[k + 2], b_recv.at[k + 2], to))
    for k in range(1, XC):
        copies.append(send(sy, qb.at[k - 1], b_send.at[k + 5], b_recv.at[k + 5], at_x(k)))
    for c in copies:
        c.wait()

    def add_b(i, carry):
        total = sa0[x, i].astype(jnp.float32)
        for k in range(XC - 1):
            total = total + rb0[k, i].astype(jnp.float32)
        sb[i] = total.astype(jnp.bfloat16)
        total = sa1[dp, rep, i].astype(jnp.float32)
        for k in range(3):
            total = total + rb1[k, i].astype(jnp.float32)
        sb[i + half] = total.astype(jnp.bfloat16)
        return carry

    lax.fori_loop(0, half, add_b, 0)
    sx[...] = sy[...] + qb[0] + qb[1] + qb[2]

    copies = []
    for k in range(1, ZC):
        there = lax.rem(z + k, ZC)
        copies.append(send(sb.at[there], rc.at[k - 1], c_send.at[k - 1], c_recv.at[k - 1], at_z(k)))
        copies.append(send(sx.at[there], qc.at[k - 1], c_send.at[k + ZC - 2], c_recv.at[k + ZC - 2], at_z(k)))
    for c in copies:
        c.wait()
    total = sb[z].astype(jnp.float32)
    for k in range(ZC - 1):
        total = total + rc[k].astype(jnp.float32)
    out[core, rep, x, z] = total.astype(jnp.bfloat16)
    total = sx[z]
    for k in range(ZC - 1):
        total = total + qc[k]
    sz[core, z] = total

    copies = []
    for k in range(1, ZC):
        mine = out.at[core, rep, x, z]
        copies.append(send(mine, mine, d_send.at[k - 1], d_recv.at[k - 1], at_z(k)))
        copies.append(send(sz.at[core, z], sz.at[core, z], d_send.at[k + ZC - 2], d_recv.at[k + ZC - 2], at_z(k)))
    for c in copies:
        c.wait()
    mine = out.at[core, rep, x]
    to_rep = send(mine, mine, e_send, e_recv, other_rep)
    handed = [send(mine, mine, h_send.at[0], h_recv.at[0], other_core)]
    handed.append(send(sz.at[core], sz.at[core], h_send.at[XC + 1], h_recv.at[XC + 1], other_core))
    to_rep.wait()
    theirs = out.at[core, 1 - rep, x]
    both = out.at[core, :, x]
    copies = []
    for k in range(1, XC):
        copies.append(send(both, both, f_send.at[k - 1], f_recv.at[k - 1], at_x(k)))
    handed.append(send(theirs, theirs, h_send.at[1], h_recv.at[1], other_core))
    for k in range(1, XC):
        copies[k - 1].wait()
        came = lax.rem(x + XC - k, XC)
        piece = out.at[core, :, came]
        handed.append(send(piece, piece, h_send.at[k + 1], h_recv.at[k + 1], other_core))
    for c in handed:
        c.wait()
    small_out[...] = sz[0] + sz[1]


def reduce_all(g, small):
    tail = g.shape[4:]
    half = ZC // 2
    bf = jnp.bfloat16
    dma = pltpu.SemaphoreType.DMA
    return pl.pallas_call(
        reduce_kernel,
        out_shape=(
            jax.ShapeDtypeStruct((2, 2, XC, ZC) + tail, bf),
            jax.ShapeDtypeStruct(small.shape, F32),
        ),
        in_specs=[VMEM] * 2,
        out_specs=(VMEM,) * 2,
        scratch_shapes=[
            pltpu.VMEM((3, XC, half) + tail, bf),
            pltpu.VMEM((XC - 1, 2, 2, half) + tail, bf),
            pltpu.VMEM((XC, half) + tail, bf),
            pltpu.VMEM((2, 2, half) + tail, bf),
            pltpu.VMEM((XC - 1, half) + tail, bf),
            pltpu.VMEM((3, half) + tail, bf),
            pltpu.VMEM((ZC,) + tail, bf),
            pltpu.VMEM((ZC - 1,) + tail, bf),
            pltpu.VMEM(small.shape, F32), pltpu.VMEM(small.shape, F32), pltpu.VMEM((2,) + small.shape, F32),
            pltpu.VMEM((3,) + small.shape, F32), pltpu.VMEM((XC - 1,) + small.shape, F32),
            pltpu.VMEM((ZC - 1,) + small.shape[1:], F32),
            dma((9,)), dma((9,)), dma((9,)), dma((9,)),
            dma((2 * ZC - 2,)), dma((2 * ZC - 2,)), dma((2 * ZC - 2,)), dma((2 * ZC - 2,)),
            dma, dma, dma((XC - 1,)), dma((XC - 1,)), dma((XC + 2,)), dma((XC + 2,)),
        ],
        compiler_params=pltpu.CompilerParams(
            collective_id=0, has_side_effects=True, vmem_limit_bytes=40 << 20
        ),
        cost_estimate=pl.CostEstimate(flops=10_000_000, bytes_accessed=60_000_000, transcendentals=0),
        name="grad_reduce",
    )(g, small)


def per_device(tokens, cotangent, w_qkv, w_proj, conv_weight, norm_gain, head_scale, shift_offsets):
    slab = tokens[0]
    seq_index = lax.axis_index("seq")
    core = seq_index % 2
    rows = w_qkv.shape[0]
    cot = cotangent[0].reshape(256, C)
    gain = norm_gain.reshape(1, C)
    wq = w_qkv.reshape(rows, 3, 2, 2, 192)
    wq = jnp.stack([wq[:, :, :, c].reshape(rows, 3 * MINE) for c in range(2)])
    wp = w_proj.reshape(2, 192, C)
    scales = head_scale.reshape(2, 2, 6).transpose(1, 0, 2).reshape(2, 12)
    nwin, cwin, wq, wp, mixed, halo = mix(slab, cot, wq, wp, conv_weight, gain)
    own, given, grads, scale_rows = attend(shift_offsets, scales, nwin, cwin, wq, wp)
    pairs = [(i, (i + (1 if i % 2 else -1)) % SEQ) for i in range(SEQ)]
    recv = lax.ppermute(given, "seq", pairs)
    output, bm, bmh, gain_part = project(own, recv, wq, wp, mixed, cot, gain)
    before = lax.ppermute(bmh[1], "seq", [(i, i + 1) for i in range(SEQ - 1)])
    after = lax.ppermute(bmh[0], "seq", [(i + 1, i) for i in range(SEQ - 1)])
    grad_tokens, conv_part = unmix(bm, before, after, slab, halo, conv_weight)
    mine = jnp.sum(scale_rows, axis=(0, 2)).reshape(2, 1, 6)
    mine = jnp.where(core == 0, jnp.pad(mine, ((0, 0), (0, 1), (0, 0))), jnp.pad(mine, ((0, 0), (1, 0), (0, 0))))
    small = jnp.concatenate([
        conv_part.reshape(-1, 128), gain_part.reshape(-1, 128),
        jnp.pad(mine.reshape(1, 24), ((0, 23), (0, 104))),
    ])
    summed, small = reduce_all(grads.reshape(2, 2, XC, ZC, 9, 8, 128), small.reshape(8, 24, 128))
    small = small.reshape(192, 128)
    factor = 1.0 / math.sqrt(
        lax.axis_size("rep") * lax.axis_size("dp") * SEQ * 256
    )
    summed = summed.reshape(2, 2, XC, 72, 8, 128).astype(F32) * factor
    part = summed[:, :, :, :54].reshape(2, 2, XC, 9, 6, 8, 128).transpose(1, 2, 4, 5, 0, 3, 6)
    part = part.reshape(384, 2, 3, 2, 192).transpose(0, 2, 3, 1, 4).reshape(384, 3 * C)
    proj = summed[:, :, :, 54:].reshape(2, 2, XC, 6, 3, 8, 128).transpose(0, 1, 2, 4, 5, 3, 6)
    small = small * factor
    return (
        output[None],
        grad_tokens[None],
        part,
        proj.reshape(384, C),
        small[:162].reshape(27, C),
        small[162:168].reshape(C),
        small[168, :24],
    )


def solution(mesh):
    in_specs = (
        P(("rep", "dp"), "seq", None, None, None),
        P(("rep", "dp"), "seq", None, None, None),
        P("dp", None),
        P("dp", None),
        P(),
        P(),
        P(),
        P(),
    )
    out_specs = (
        P(("rep", "dp"), "seq", None, None, None),
        P(("rep", "dp"), "seq", None, None, None),
        P("dp", None),
        P("dp", None),
        P(),
        P(),
        P(),
    )
    return jax.shard_map(
        per_device, mesh=mesh, in_specs=in_specs, out_specs=out_specs, check_vma=False
    )
```

time: 561 us -> 205 us (0.37); the launches traced: 552 us -> 204 us
  waiting for transfers between devices: 219 us -> 13.3 us
  Pallas kernels: 58.2 us -> 138 us
  blocking collectives: 77.5 us -> 0 us
  matrix products: 57.8 us -> 0 us
  other arithmetic: 52.5 us -> 3.88 us
  between operations: 21.8 us -> 0.83 us
  starting transfers between devices: 18.7 us -> 7.3 us
  local copies, waits for them, and re-layouts: 47.3 us -> 41.2 us
    psum x1 -> x0, waiting for transfers between devices: 158 us -> none  [per_device(): lax.psum((conv_part, gain_part, scale_part), ('rep', 'dp', 'seq'))]
    pallas_call x1 -> x5, Pallas kernels: 58.2 us -> 138 us  [the longest x1 70.4 us: reduce_all(): pl.pallas_call(reduce_kernel, out_shape=(jax.ShapeDtypeStruct((2, 2, XC,...]
    psum x1 -> x0, blocking collectives: 77.5 us -> none  [per_device(): lax.psum((conv_part, gain_part, scale_part), ('rep', 'dp', 'seq'))]
    all_gather x2 -> x0, waiting for transfers between devices: 54.6 us -> none  [the longest x1 40.2 us: per_device(): lax.all_gather(w_qkv, 'dp', axis=0, tiled=True)]
    dot_general x11 -> x0, matrix products: 47.1 us -> none  [the longest x1 10.9 us: window_backward(): jnp.einsum('whqk,wkhe->wqhe', scaled, unit_key, preferred_element_type=jn...]
    another operation x35 -> x2, local copies, waits for them, and re-layouts: 17.8 us -> 3.08 us  [per_device(): wq = jnp.stack([wq[:, :, :, c].reshape(rows, 3 * MINE) for c in range(2)])]
    convert_element_type x10 -> x0, other arithmetic: 11.9 us -> none  [the longest x1 4.95 us: per_device(): tiles = tiles.transpose(0, 1, 2, 3, 5, 4, 6).astype(jnp.bfloat16)]
    ppermute x11 -> x3, starting transfers between devices: 18.6 us -> 7.3 us  [the longest x1 5.2 us: per_device(): after = lax.ppermute(bmh[0], 'seq', [(i + 1, i) for i in range(SEQ - 1)])]
  transfers between devices with their start and end apart: 14 -> 3, of which waited for: 6 -> 2; matrix products, arithmetic and copies ran while one was open for 11% -> 1% of each run, Pallas kernels for 0% -> 0%
where the time goes in v2:
time: 205 us; the launch traced here: 204 us
  Pallas kernels  138 us (67%)
  local copies, waits for them, and re-layouts  41.2 us (20%)
  waiting for transfers between devices  13.3 us (6%)
  starting transfers between devices  7.3 us (4%)
  other arithmetic  3.88 us (2%)
    pallas_call x1, Pallas kernels, reduce_all(): pl.pallas_call(reduce_kernel, out_shape=(jax.ShapeDtypeStruct((2, 2, XC,...  70.4 us
    pallas_call x1, Pallas kernels, mix(): pl.pallas_call(mix_kernel, out_shape=(shape((2, 256, C), BF), shape((2, 2...  30.6 us
    pallas_call x1, Pallas kernels, attend(): pl.pallas_call(attend_kernel, out_shape=(shape((256, 4 * MINE), BF), shap...  26.1 us
    ppermute x1, waiting for transfers between devices, per_device(): recv = lax.ppermute(given, 'seq', pairs)  11.7 us
    unnamed x24, local copies, waits for them, and re-layouts  8.27 us
    reshape x1, local copies, waits for them, and re-layouts, per_device(): part.reshape(384, 2, 3, 2, 192).transpose(0, 2, 3, 1, 4).reshape(384, 3 * C)  8.06 us
    transpose x1, local copies, waits for them, and re-layouts, per_device(): part.reshape(384, 2, 3, 2, 192).transpose(0, 2, 3, 1, 4).reshape(384, 3 * C)  6.27 us
    pallas_call x1, Pallas kernels, project(): pl.pallas_call(project_kernel, out_shape=(shape(field, BF), shape(field,...  5.42 us
  transfers between devices with their start and end apart: 3, of which 2 were waited for; matrix products, arithmetic and copies ran while one was open for 1% of the time, Pallas kernels for 0%

profile of v2, /device:TPU:1, one launch (start us, length us, event | category | flops | bytes accessed | tf_op | source)
XLA Modules:
  0.0 204.5 jit_solution(1529339596486364266)
XLA Ops:
  0.6 0.7 reshape.75
  1.5 0.7 reshape.79.gain
  2.1 2.8 %copy.29 = bf16[384,2304]{0,1:T(8,128)(2,1)S(1)} copy(bf16[384,2304]{1,0:T(8,128)(2,1)} %param.10) | data formatting | bytes 3538944 | tf_op args[2]
  4.9 1.1 fusion
  6.0 1.6 copy.30
  7.7 1.5 copy.31
  9.1 2.6 %pad_maximum_fusion.wq_in = bf16[2,384,1152]{2,1,0:T(8,128)(2,1)} fusion(bf16[1,384,1152]{2,1,0:T(8,128)(2,1)} %copy.31, bf16[1,384,1152]{2,1,0:T(8,128)(2,1)S(1)} %copy.30), kind=kLoop, calls=%fused_computation.1 | loop fusion | flops 884736 | bytes 3538944 | tf_op jit(solution)/shard_map/stack | solution.py:575
  11.7 30.6 %mix.1 = (bf16[2,256,768]{2,1,0:T(8,128)(2,1)S(1)}, bf16[2,256,768]{2,1,0:T(8,128)(2,1)S(1)}, bf16[2,2,384,1152]{3,2,1,0:T(8,128)(2,1)}, bf16[2,2,192,768]{3,2,1...) custom-call(bf16[2,8,16,768]{3,2,1,0:T(8,128)(2,1)S(1)} %bitcast.34, ...), custom_call_target="tpu_custom_call" | custom-call | tf_op jit(solution)/shard_map/mix/pallas_call | solution.py:161
  42.4 26.1 %attend.1 = (bf16[256,1536]{1,0:T(8,128)(2,1)S(1)}, bf16[256,1536]{1,0:T(8,128)(2,1)S(1)}, bf16[2,2,4,72,8,128]{5,4,3,2,1,0:T(8,128)(2,1)}, f32[2,12,256]{2,1,0:T(8,128)S(1)}) custom-call(s32[2]{0:T(128)S(1)} %copy-done.10, f32[2,12]{1,0:T(2,128)S(1)} %reshape.76.scales, bf16[2,256,768]{2,1,0:T(8,128)(2,1)S(1)} %get-tuple-element.25.nwin, ...), custom_call_target="tpu_custom_call" | custom-call | tf_op jit(solution)/shard_map/attend/pallas_call | solution.py:286
  68.5 11.7 %collective-permute-done.recv = bf16[256,1536]{1,0:T(8,128)(2,1)S(1)} collective-permute-done((bf16[256,1536]{1,0:T(8,128)(2,1)S(1)}, bf16[256,1536]{1,0:T(8,128)(2,1)S(1)}, u32[]{:S(2)}, u32[]{:S(2)}) %collective-permute-start) | collective-permute-done | bytes 786464 | tf_op jit(solution)/shard_map/ppermute | solution.py:581
  80.2 5.4 %project.1 = (bf16[2,8,16,768]{3,2,1,0:T(8,128)(2,1)}, f32[2,8,16,768]{3,2,1,0:T(8,128)S(1)}, bf16[2,8,16,768]{3,2,1,0:T(8,128)(2,1)S(1)}, f32[1,768]{1,0:T(1,128)S(1)}) custom-call(bf16[256,1536]{1,0:T(8,128)(2,1)S(1)} %get-tuple-element.29.own, bf16[256,1536]{1,0:T(8,128)(2,1)S(1)} %collective-permute-done.recv, ...), custom_call_target="tpu_custom_call" | custom-call | tf_op jit(solution)/shard_map/project/pallas_call | solution.py:335
  85.6 0.8 slice_bitcast_fusion
  86.4 5.2 %collective-permute-start.2 = (bf16[8,16,768]{2,1,0:T(8,128)(2,1)}, bf16[8,16,768]{2,1,0:T(8,128)(2,1)}, u32[]{:S(2)}, u32[]{:S(2)}) collective-permute-start(bf16[8,16,768]{2,1,0:T(8,128)(2,1)} %get-tuple-element.59), channel_id=1, source_target_pairs={{1,0},{2,1},{3,2},{4,3},{5,4},{6,5},{7,6},{8,7},{9,8},{10,9},{11,1... | collective-permute-start | bytes 589832 | tf_op jit(solution)/shard_map/ppermute | solution.py:584
  91.6 2.1 %collective-permute-start.1 = (bf16[8,16,768]{2,1,0:T(8,128)(2,1)}, bf16[8,16,768]{2,1,0:T(8,128)(2,1)}, u32[]{:S(2)}, u32[]{:S(2)}) collective-permute-start(bf16[8,16,768]{2,1,0:T(8,128)(2,1)} %get-tuple-element.60), channel_id=1, source_target_pairs={{0,1},{1,2},{2,3},{3,4},{4,5},{5,6},{6,7},{7,8},{8,9},{9,10},{10,1... | collective-permute-start | bytes 589832 | tf_op jit(solution)/shard_map/ppermute | solution.py:583
  93.7 0.9 reduce_sum.9
  94.8 1.6 collective-permute-done.1.before
  96.4 0.9 copy-done.5
  97.3 1.0 copy-done.7
  98.3 5.4 %unmix.1 = (bf16[2,8,16,768]{3,2,1,0:T(8,128)(2,1)}, f32[27,768]{1,0:T(8,128)S(1)}) custom-call(f32[2,8,16,768]{3,2,1,0:T(8,128)S(1)} %get-tuple-element.33.bm, bf16[8,16,768]{2,1,0:T(8,128)(2,1)} %collective-permute-done.1.before, bf16[8,16,768]{2,1,0:T(8,128)(2,1)} %collective-permute-done.2.after, bf16[2,8,16,768]{3,2,1,0:T(8,128)(2,1)S(1)} %bitcast.35, ...), custom_call_target="tpu_custom_call" | custom-call | tf_op jit(solution)/shard_map/unmix/pallas_call | solution.py:382
  103.7 0.6 copy-done.8
  104.4 0.9 reshape.81
  105.3 70.4 %grad_reduce.1 = (bf16[2,2,4,8,9,8,128]{6,5,4,3,2,1,0:T(8,128)(2,1)S(1)}, f32[8,24,128]{2,1,0:T(8,128)S(1)}) custom-call(bf16[2,2,4,8,9,8,128]{6,5,4,3,2,1,0:T(8,128)(2,1)S(1)} %bitcast.31, f32[8,24,128]{2,1,0:T(8,128)S(1)} %bitcast.37), custom_call_target="tpu_custom_call" | custom-call | flops 10000000 | bytes 60000000 | tf_op jit(solution)/shard_map/grad_reduce/pallas_call | solution.py:535
  175.7 0.5 slice_bitcast_fusion.3
  176.2 0.6 slice_bitcast_fusion.2
  176.8 0.6 slice.40
  177.9 1.1 slice.39
  179.2 1.5 reshape.91
  180.8 2.4 %copy.35 = f32[2,2,4,3,8,6,128]{6,4,5,3,2,1,0:T(8,128)} copy(f32[2,2,4,3,8,6,128]{6,4,3,5,2,1,0:T(8,128)} %bitcast.44) | data formatting | bytes 2359296 | tf_op jit(solution)/shard_map/transpose | solution.py:600
  183.2 4.0 %copy.33 = f32[2,4,6,8,2,9,128]{6,5,4,3,2,1,0:T(8,128)} copy(f32[2,4,6,8,2,9,128]{6,3,2,5,1,0,4:T(8,128)S(1)} %bitcast.41) | data formatting | bytes 7077888 | tf_op jit(solution)/shard_map/transpose | solution.py:598
  187.2 8.1 %reshape.87 = f32[384,2,3,2,192]{4,3,2,1,0:T(2,128)} reshape(f32[2,4,6,8,2,9,128]{6,5,4,3,2,1,0:T(8,128)} %copy.33) | data formatting | bytes 7077888 | tf_op jit(solution)/shard_map/reshape | solution.py:599
  195.2 6.3 %copy.34 = f32[384,3,2,2,192]{0,4,3,2,1:T(8,128)S(1)} copy(f32[384,3,2,2,192]{4,2,1,3,0:T(2,128)} %bitcast.40) | data formatting | bytes 7077888 | tf_op jit(solution)/shard_map/transpose | solution.py:599
  201.5 2.9 %copy.36 = f32[384,2304]{1,0:T(8,128)} copy(f32[384,2304]{0,1:T(8,128)S(1)} %bitcast.42) | data formatting | bytes 7077888
  (32 shorter events, 1.0 us)
Async XLA Ops:
  7.6 4.1 %copy-start.1 = (bf16[1,2,8,16,768]{4,3,2,1,0:T(8,128)(2,1)S(1)}, bf16[1,2,8,16,768]{4,3,2,1,0:T(8,128)(2,1)}, u32[]{:S(2)}) copy-start(bf16[1,2,8,16,768]{4,3,2,1,0:T(8,128)(2,1)} %param.9) | copy-start | bytes 1179652
  7.6 4.1 %copy-start.2 = (bf16[1,2,8,16,768]{4,3,2,1,0:T(8,128)(2,1)S(1)}, bf16[1,2,8,16,768]{4,3,2,1,0:T(8,128)(2,1)}, u32[]{:S(2)}) copy-start(bf16[1,2,8,16,768]{4,3,2,1,0:T(8,128)(2,1)} %param.8) | copy-start | bytes 1179652
  7.6 4.1 %copy-start.3 = (bf16[384,768]{1,0:T(8,128)(2,1)S(1)}, bf16[384,768]{1,0:T(8,128)(2,1)}, u32[]{:S(2)}) copy-start(bf16[384,768]{1,0:T(8,128)(2,1)} %param.11) | copy-start | bytes 1769476
  7.6 4.1 %copy-start.4 = (f32[27,768]{1,0:T(8,128)S(1)}, f32[27,768]{1,0:T(8,128)}, u32[]{:S(2)}) copy-start(f32[27,768]{1,0:T(8,128)} %weight.3) | copy-start | bytes 248836
  11.7 30.7 %copy-start.10 = (s32[2]{0:T(128)S(1)}, s32[2]{0:T(128)}, u32[]{:S(2)}) copy-start(s32[2]{0:T(128)} %shift.1) | copy-start | bytes 28
  42.3 26.1 %copy-start.6 = (bf16[2,8,16,768]{3,2,1,0:T(8,128)(2,1)}, bf16[2,8,16,768]{3,2,1,0:T(8,128)(2,1)S(1)}, u32[]{:S(2)}) copy-start(bf16[2,8,16,768]{3,2,1,0:T(8,128)(2,1)S(1)} %get-tuple-element.35.halo) | copy-start | bytes 1179652
  68.5 17.1 %copy-start.9 = (f32[2,12,256]{2,1,0:T(8,128)}, f32[2,12,256]{2,1,0:T(8,128)S(1)}, u32[]{:S(2)}) copy-start(f32[2,12,256]{2,1,0:T(8,128)S(1)} %get-tuple-element.40) | copy-start | bytes 73732
  68.5 11.7 %collective-permute-start = (bf16[256,1536]{1,0:T(8,128)(2,1)S(1)}, bf16[256,1536]{1,0:T(8,128)(2,1)S(1)}, u32[]{:S(2)}, u32[]{:S(2)}) collective-permute-start(bf16[256,1536]{1,0:T(8,128)(2,1)S(1)} %get-tuple-element.30), channel_id=1, source_target_pairs={{0,63},{1,2},{2,1},{3,4},{4,3},{5,6},{6,5},{7,8},{8,7},{9,10},{10,... | collective-permute-start | bytes 2359304 | tf_op jit(solution)/shard_map/ppermute | solution.py:581
  85.6 19.7 %copy-start = (bf16[2,2,4,72,8,128]{5,4,3,2,1,0:T(8,128)(2,1)S(1)}, bf16[2,2,4,72,8,128]{5,4,3,2,1,0:T(8,128)(2,1)}, u32[]{:S(2)}) copy-start(bf16[2,2,4,72,8,128]{5,4,3,2,1,0:T(8,128)(2,1)} %get-tuple-element.37) | copy-start | bytes 7077892
  86.4 8.4 %collective-permute-start.2 = (bf16[8,16,768]{2,1,0:T(8,128)(2,1)}, bf16[8,16,768]{2,1,0:T(8,128)(2,1)}, u32[]{:S(2)}, u32[]{:S(2)}) collective-permute-start(bf16[8,16,768]{2,1,0:T(8,128)(2,1)} %get-tuple-element.59), channel_id=1, source_target_pairs={{1,0},{2,1},{3,2},{4,3},{5,4},{6,5},{7,6},{8,7},{9,8},{10,9},{11,1... | collective-permute-start | bytes 589832 | tf_op jit(solution)/shard_map/ppermute | solution.py:584
  91.6 4.8 %collective-permute-start.1 = (bf16[8,16,768]{2,1,0:T(8,128)(2,1)}, bf16[8,16,768]{2,1,0:T(8,128)(2,1)}, u32[]{:S(2)}, u32[]{:S(2)}) collective-permute-start(bf16[8,16,768]{2,1,0:T(8,128)(2,1)} %get-tuple-element.60), channel_id=1, source_target_pairs={{0,1},{1,2},{2,3},{3,4},{4,5},{5,6},{6,7},{7,8},{8,9},{9,10},{10,1... | collective-permute-start | bytes 589832 | tf_op jit(solution)/shard_map/ppermute | solution.py:583
  96.4 0.9 copy-start.5
  97.3 1.0 copy-start.7
  103.7 0.6 copy-start.8

commit v3 on v2

v3 whole, which is shorter than its diff:
```python
import math

import jax
import jax.numpy as jnp
from jax import lax
from jax.experimental import pallas as pl
from jax.experimental.pallas import tpu as pltpu
from jax.sharding import PartitionSpec as P

MESH = pl.DeviceIdType.MESH
BF = jnp.bfloat16
F32 = jnp.float32
XC = 4
ZC = 8
SEQ = 64
C = 768
MINE = 384
VMEM = pl.BlockSpec(memory_space=pltpu.VMEM)
SMEM = pl.BlockSpec(memory_space=pltpu.SMEM)
DMA = pltpu.SemaphoreType.DMA


def nn(a, b):
    return lax.dot_general(a, b, (((1,), (0,)), ((), ())), preferred_element_type=F32)


def nt(a, b):
    return lax.dot_general(a, b, (((1,), (1,)), ((), ())), preferred_element_type=F32)


def tn(a, b):
    return lax.dot_general(a, b, (((0,), (0,)), ((), ())), preferred_element_type=F32)


def iota(shape, dim):
    return lax.broadcasted_iota(jnp.int32, shape, dim)


def place():
    rep, dp, seq = lax.axis_index("rep"), lax.axis_index("dp"), lax.axis_index("seq")
    return (rep, dp, seq, lax.rem(seq, 2))


def send(src, dst, s, r, to):
    c = pltpu.make_async_remote_copy(
        src_ref=src, dst_ref=dst, send_sem=s, recv_sem=r, device_id=to, device_id_type=MESH
    )
    c.start()
    return c


def greet(peers):
    barrier = pltpu.get_barrier_semaphore()
    for peer in peers:
        pl.semaphore_signal(barrier, inc=1, device_id=peer, device_id_type=MESH)
    pl.semaphore_wait(barrier, len(peers))


def fill_padded(xf, before, own, after):
    rows = jnp.zeros((4, 1, 16, C), F32)
    xf[:, 0:1] = rows
    xf[:, 9:10] = rows
    xf[0, 1:9] = before
    xf[1:3, 1:9] = own
    xf[3, 1:9] = after


def taps(xf, weight, d, lanes, flipped):
    sums = [jnp.zeros((8, 16, 128), F32) for _ in range(3)]
    for a in range(3):
        for b in range(3):
            rows = xf[d + a, b : b + 8, :, lanes]
            for e in range(3):
                t = 9 * a + 3 * b + e
                t = 26 - t if flipped else t
                sums[e] = sums[e] + weight[t : t + 1, lanes][None] * rows
    w = iota((8, 16, 128), 1)
    left = jnp.where(w == 0, 0.0, pltpu.roll(sums[0], 1, 1))
    right = jnp.where(w == 15, 0.0, pltpu.roll(sums[2], 15, 1))
    return sums[1] + left + right


def chunk(j):
    return pl.ds(pl.multiple_of(j * 128, 128), 128)


def normalise(rows):
    centred = rows - jnp.mean(rows, axis=-1, keepdims=True)
    inverse = lax.rsqrt(jnp.mean(centred * centred, axis=-1, keepdims=True) + 1e-05)
    return (centred * inverse, inverse)


def arrange(w, into, dp):
    lane, other = iota((128, 128), 0), iota((128, 128), 1)
    moves = {}
    for had in range(2):
        for gets in range(2):
            hit = (lane - 64 * had == other - 64 * gets) & (other // 64 == gets)
            moves[had, gets] = jnp.where(hit, 1.0, 0.0).astype(BF)
    for c in range(2):
        for k in range(9):
            pieces = []
            for gets in range(2):
                part, block = (2 * k + gets) // 6, (2 * k + gets) % 6
                old = part * 12 + block // 3 * 6 + c * 3 + block % 3
                start = old // 2 * 128
                pieces.append(nn(w[:, start : start + 128], moves[old % 2, gets]))
            into[c, dp, :, k * 128 : k * 128 + 128] = (pieces[0] + pieces[1]).astype(BF)


def mix_kernel(tokens, cot, wq_in, wp_in, weight, gain, nwin, cwin, wq, wp, mixed, halo,
               xf, h_send, h_recv, w_send, w_recv, l_sem):
    rep, dp, seq, core = place()
    y = rep * 2 + dp
    up = (rep, dp, lax.rem(seq + 1, SEQ))
    down = (rep, dp, lax.rem(seq + SEQ - 1, SEQ))
    partner = (rep, dp, lax.rem(seq + SEQ - 1 + 2 * core, SEQ))
    other_core = (rep, dp, seq + 1 - 2 * core)
    y_to = lax.rem(y + 3 + 2 * core, 4)
    y_from = lax.rem(y + 1 + 2 * core, 4)
    y_peer = (y_to // 2, lax.rem(y_to, 2), seq)
    y_source = (y_from // 2, lax.rem(y_from, 2), seq)
    greet([up, down, y_peer, y_source])
    own = 1 - core
    halos = [
        send(tokens.at[0], halo.at[1], h_send.at[0], h_recv.at[0], down),
        send(tokens.at[1], halo.at[0], h_send.at[1], h_recv.at[1], up),
    ]
    cots = send(cot, cwin.at[own], h_send.at[2], h_recv.at[2], partner)
    local = [
        pltpu.make_async_copy(cot, cwin.at[own], l_sem.at[0]),
        pltpu.make_async_copy(wp_in, wp.at[:, dp], l_sem.at[1]),
    ]
    for c in local:
        c.start()
    arrange(wq_in, wq, dp)
    weights = [
        send(wq.at[core, dp], wq.at[core, dp], w_send.at[0], w_recv.at[0], y_peer),
        send(wp_in.at[core], wp.at[core, dp], w_send.at[1], w_recv.at[1], y_peer),
    ]
    for c in halos:
        c.wait()
    first = jnp.where(seq == 0, 0.0, 1.0).astype(F32)
    last = jnp.where(seq == SEQ - 1, 0.0, 1.0).astype(F32)
    fill_padded(xf, halo[0].astype(F32) * first, tokens[...].astype(F32), halo[1].astype(F32) * last)

    def filter_step(i, carry):
        d, j = i // 6, lax.rem(i, 6)
        lanes = chunk(j)
        mixed[d, :, :, lanes] = xf[d + 1, 1:9, :, lanes] + taps(xf, weight, d, lanes, False)
        return carry

    lax.fori_loop(0, 12, filter_step, 0)

    def norm_step(i, carry):
        d, h = i // 2, lax.rem(i, 2) * 4
        unit, _ = normalise(mixed[d, pl.ds(h, 4)].reshape(64, C))
        nwin[own, pl.ds(pl.multiple_of(i * 64, 64), 64)] = (unit * gain[...]).astype(BF)
        return carry

    lax.fori_loop(0, 4, norm_step, 0)
    norms = send(nwin.at[own], nwin.at[own], h_send.at[3], h_recv.at[3], partner)
    for c in weights:
        c.wait()
    back = [
        send(wq.at[core, 1 - dp], wq.at[core, 1 - dp], w_send.at[2], w_recv.at[2], other_core),
        send(wp.at[core, 1 - dp], wp.at[core, 1 - dp], w_send.at[3], w_recv.at[3], other_core),
    ]
    for c in local:
        c.wait()
    cots.wait()
    norms.wait()
    for c in back:
        c.wait()


def mix(tokens, cot, wq, wp, weight, gain):
    shape = jax.ShapeDtypeStruct
    return pl.pallas_call(
        mix_kernel,
        out_shape=(
            shape((2, 256, C), BF), shape((2, 256, C), BF),
            shape((2, 2, MINE, 3 * MINE), BF), shape((2, 2, MINE // 2, C), BF),
            shape((2, 8, 16, C), F32), shape((2, 8, 16, C), BF),
        ),
        in_specs=[VMEM] * 6,
        out_specs=(VMEM,) * 6,
        scratch_shapes=[
            pltpu.VMEM((4, 10, 16, C), F32),
            DMA((4,)), DMA((4,)), DMA((4,)), DMA((4,)), DMA((2,)),
        ],
        compiler_params=pltpu.CompilerParams(
            collective_id=1, has_side_effects=True, vmem_limit_bytes=48 << 20
        ),
        name="mix",
    )(tokens, cot, wq, wp, weight, gain)


def source_of(n, r):
    b, d, h, j = n >> 8, (n >> 6) & 3, (n >> 3) & 7, n & 7
    return d * 128 + h * 16 + ((8 * b + j + r) & 15)


def head_sums(x, ones):
    high = x.astype(BF)
    low = (x - high.astype(F32)).astype(BF)
    return nn(high, ones) + nn(low, ones)


def attend_kernel(shift, scales, nwin, cwin, wq, wp, own_out, given_out, g_out, scale_out,
                  x_s, ct_s, qkv_s, ba_s, att_s, bqkv_s, allow_s, gq_s, gp_s):
    core = lax.rem(lax.axis_index("seq"), 2)
    s, r = shift[0], shift[1]
    select = jnp.where(iota((512, 512), 1) == source_of(iota((512, 512), 0), r), 1.0, 0.0).astype(BF)
    x_s[...] = nn(select, nwin[...].reshape(512, C)).astype(BF)
    ct_s[...] = nn(select, cwin[...].reshape(512, C)).astype(BF)
    qkv_s[...] = nn(x_s[...], wq[core].reshape(C, 3 * MINE)).astype(BF)
    ba_s[...] = nt(ct_s[...], wp[core].reshape(MINE, C)).astype(BF)

    def code(n, b):
        h, j = (n >> 3) & 7, n & 7
        return jnp.where(h < s, 2, 0) + jnp.where(8 * b + j + r >= 16, 1, 0)

    for b in range(2):
        same = code(iota((256, 256), 0), b) == code(iota((256, 256), 1), b)
        allow_s[b] = jnp.where(same, 1.0, 0.0).astype(F32)
    scale_out[...] = jnp.zeros((2, 16, 256), F32)
    ones = jnp.where(iota((128, 128), 0) // 32 == iota((128, 128), 1) // 32, 1.0, 0.0).astype(BF)
    lane_head = iota((256, 128), 1) // 32

    def group(i, carry):
        b, g = i // 3, lax.rem(i, 3)
        rows = pl.ds(pl.multiple_of(b * 256, 256), 256)

        def part(k):
            return pl.ds(pl.multiple_of(g * 128 + k * MINE, 128), 128)

        query = qkv_s[rows, part(0)].astype(F32)
        key = qkv_s[rows, part(1)].astype(F32)
        value = qkv_s[rows, part(2)]
        ba = ba_s[rows, part(0)]
        inv_q = lax.rsqrt(head_sums(query * query, ones) + 1.0)
        inv_k = lax.rsqrt(head_sums(key * key, ones) + 1.0)
        uq = (query * inv_q).astype(BF)
        uk = (key * inv_k).astype(BF)
        att = jnp.zeros((256, 128), F32)
        back_v = jnp.zeros((256, 128), F32)
        back_uq = jnp.zeros((256, 128), F32)
        back_uk = jnp.zeros((256, 128), F32)
        zero = jnp.zeros((256, 128), BF)
        for h in range(4):
            here = lane_head == h
            scale = scales[core, g * 4 + h]
            uq_h = jnp.where(here, uq, zero)
            uk_h = jnp.where(here, uk, zero)
            v_h = jnp.where(here, value, zero)
            ba_h = jnp.where(here, ba, zero)
            cosine = nt(uk_h, uq)
            expo = jnp.exp(scale * cosine) * allow_s[b]
            prob = expo * (1.0 / jnp.sum(expo, axis=0, keepdims=True))
            weights = prob.astype(BF)
            att = att + tn(weights, v_h)
            back_v = back_v + nn(weights, ba_h)
            back_prob = nt(v_h, ba)
            mean = jnp.sum(prob * back_prob, axis=0, keepdims=True)
            back_score = prob * (back_prob - mean)
            scale_out[b, pl.ds(g * 4 + h, 1)] = jnp.sum(back_score * cosine, axis=0, keepdims=True)
            scaled = (back_score * scale).astype(BF)
            back_uq = back_uq + tn(scaled, uk_h)
            back_uk = back_uk + nn(scaled, uq_h)
        att_s[rows, part(0)] = att.astype(BF)
        inner_q = head_sums(query * back_uq, ones)
        inner_k = head_sums(key * back_uk, ones)
        back_q = back_uq * inv_q - query * inner_q * (inv_q * inv_q * inv_q)
        back_k = back_uk * inv_k - key * inner_k * (inv_k * inv_k * inv_k)
        bqkv_s[rows, part(0)] = back_q.astype(BF)
        bqkv_s[rows, part(1)] = back_k.astype(BF)
        bqkv_s[rows, part(2)] = back_v.astype(BF)
        return carry

    lax.fori_loop(0, 6, group, 0)
    for half, out in ((1 - core, own_out), (core, given_out)):
        target = source_of(iota((256, 512), 1), r)
        restore = jnp.where(iota((256, 512), 0) + 256 * half == target, 1.0, 0.0).astype(BF)
        out[:, 0:MINE] = nn(restore, att_s[...]).astype(BF)
        out[:, MINE:] = nn(restore, bqkv_s[...]).astype(BF)
    gq_s[...] = tn(x_s[...], bqkv_s[...])
    gp_s[...] = tn(att_s[...], ct_s[...])

    def store(i, carry):
        d, p, x = i // 8, lax.rem(i // 4, 2), lax.rem(i, 4)
        for c in range(9):
            block = gq_s[pl.ds(pl.multiple_of(i * 48, 48), 48), c * 128 : (c + 1) * 128]
            g_out[d, p, x, c * 6 : c * 6 + 6] = block.reshape(6, 8, 128).astype(BF)
        for c in range(6):
            block = gp_s[pl.ds(pl.multiple_of(i * 24, 24), 24), c * 128 : (c + 1) * 128]
            g_out[d, p, x, 54 + c * 3 : 57 + c * 3] = block.reshape(3, 8, 128).astype(BF)
        return carry

    lax.fori_loop(0, 16, store, 0)


def attend(shift, scales, nwin, cwin, wq, wp):
    shape = jax.ShapeDtypeStruct
    return pl.pallas_call(
        attend_kernel,
        out_shape=(
            shape((256, 4 * MINE), BF), shape((256, 4 * MINE), BF),
            shape((2, 2, XC, 72, 8, 128), BF), shape((2, 16, 256), F32),
        ),
        in_specs=[SMEM, SMEM] + [VMEM] * 4,
        out_specs=(VMEM,) * 4,
        scratch_shapes=[
            pltpu.VMEM((512, C), BF), pltpu.VMEM((512, C), BF),
            pltpu.VMEM((512, 3 * MINE), BF), pltpu.VMEM((512, MINE), BF),
            pltpu.VMEM((512, MINE), BF), pltpu.VMEM((512, 3 * MINE), BF),
            pltpu.VMEM((2, 256, 256), F32), pltpu.VMEM((C, 3 * MINE), F32), pltpu.VMEM((MINE, C), F32),
        ],
        compiler_params=pltpu.CompilerParams(vmem_limit_bytes=48 << 20),
        name="attend",
    )(shift, scales, nwin, cwin, wq, wp)


def finish_kernel(own, given, g, scale_rows, wq, wp, mixed, cot, tokens, halo, weight, gain,
                  out, grad, gq_out, gp_out, conv_out, gain_out, scale_out,
                  recv, bn_s, bm, bmh, ph, xf, tf, sh, ra0, ra1, sa0, sa1, rb0, rb1, sb, rc, full,
                  sm, s2, s3, sz, qy1, qx1, qx2, qy2, qz, s_sem, r_sem):
    rep, dp, seq, core = place()
    z = lax.rem(seq // 2, ZC)
    x = seq // (2 * ZC)
    y = rep * 2 + dp

    def at_y(step):
        there = lax.rem(y + step, 4)
        return (there // 2, lax.rem(there, 2), seq)

    def at_x(step):
        there = lax.rem(x + step, XC)
        return (rep, dp, (there * ZC + z) * 2 + core)

    def at_z(step):
        there = lax.rem(z + step, ZC)
        return (rep, dp, (x * ZC + there) * 2 + core)

    up = (rep, dp, lax.rem(seq + 1, SEQ))
    down = (rep, dp, lax.rem(seq + SEQ - 1, SEQ))
    partner = (rep, dp, lax.rem(seq + SEQ - 1 + 2 * core, SEQ))
    other_core = (rep, dp, seq + 1 - 2 * core)
    other_rep = (1 - rep, dp, seq)
    peers = [at_y(k) for k in range(1, 4)] + [at_x(k) for k in range(1, XC)]
    peers += [at_z(k) for k in range(1, ZC)] + [up, down]
    greet(peers)
    used = [0]

    def go(src, dst, to):
        n = used[0]
        used[0] += 1
        return send(src, dst, s_sem.at[n], r_sem.at[n], to)

    def finish(copies):
        for c in copies:
            c.wait()

    low, high = pl.ds(0, 36), pl.ds(36, 36)
    exchange = go(given, recv, partner)
    stage = []
    for k in range(1, 4):
        to = at_y(k)
        stage.append(go(g.at[to[1], to[0], :, low], ra0.at[k - 1], to))
    for k in range(1, XC):
        stage.append(go(g.at[:, :, lax.rem(x + k, XC), high], ra1.at[k - 1], at_x(k)))

    first = jnp.where(seq == 0, 0.0, 1.0).astype(F32)
    last = jnp.where(seq == SEQ - 1, 0.0, 1.0).astype(F32)
    fill_padded(tf, halo[0].astype(F32) * first, tokens[...].astype(F32), halo[1].astype(F32) * last)
    exchange.wait()
    back = nt(own[:, MINE:], wq[core].reshape(C, 3 * MINE))
    back = back + nt(recv[:, MINE:], wq[1 - core].reshape(C, 3 * MINE))
    bn_s[...] = back.astype(BF)

    def norm_step(i, total):
        d, h = i // 2, lax.rem(i, 2) * 4
        rows = pl.ds(pl.multiple_of(i * 64, 64), 64)
        unit, inverse = normalise(mixed[d, pl.ds(h, 4)].reshape(64, C))
        back_float = bn_s[rows].astype(F32)
        total = total + jnp.sum((back_float * unit).reshape(8, 8, C), axis=0)
        grad_unit = back_float * gain[...]
        mean = jnp.mean(grad_unit, axis=-1, keepdims=True)
        slope = jnp.mean(grad_unit * unit, axis=-1, keepdims=True)
        result = cot[rows].astype(F32) + inverse * (grad_unit - mean - unit * slope)
        bm[d, pl.ds(h, 4)] = result.reshape(4, 16, C)
        bmh[d, pl.ds(h, 4)] = result.astype(BF).reshape(4, 16, C)
        return total

    gain_part = jnp.sum(lax.fori_loop(0, 4, norm_step, jnp.zeros((8, C), F32)), axis=0, keepdims=True)
    planes = [go(bmh.at[0], ph.at[1], down), go(bmh.at[1], ph.at[0], up)]
    proj = nn(own[:, 0:MINE], wp[core].reshape(MINE, C))
    proj = proj + nn(recv[:, 0:MINE], wp[1 - core].reshape(MINE, C))
    out[...] = (mixed[...].reshape(256, C) + proj).astype(BF).reshape(2, 8, 16, C)

    finish(stage)

    def add_a(i, carry):
        total = g[dp, rep, i, low].astype(F32)
        for k in range(3):
            total = total + ra0[k, i].astype(F32)
        sa0[i] = total.astype(BF)
        d, r = lax.rem(i, 2), i // 2
        total = g[d, r, x, high].astype(F32)
        for k in range(XC - 1):
            total = total + ra1[k, d, r].astype(F32)
        sa1[d, r] = total.astype(BF)
        return carry

    lax.fori_loop(0, 4, add_a, 0)
    stage = []
    for k in range(1, XC):
        stage.append(go(sa0.at[lax.rem(x + k, XC)], rb0.at[k - 1], at_x(k)))
    for k in range(1, 4):
        to = at_y(k)
        stage.append(go(sa1.at[to[1], to[0]], rb1.at[k - 1], to))

    finish(planes)
    fill_padded(xf, ph[0].astype(F32) * first, bm[...], ph[1].astype(F32) * last)

    def filter_step(i, carry):
        d, j = i // 6, lax.rem(i, 6)
        lanes = chunk(j)
        here = xf[d + 1, 1:9, :, lanes]
        grad[d, :, :, lanes] = (here + taps(xf, weight, d, lanes, True)).astype(BF)
        w = iota((8, 16, 128), 1)
        sh[0, d, :, :, lanes] = jnp.where(w == 15, 0.0, pltpu.roll(here, 15, 1))
        sh[1, d, :, :, lanes] = here
        sh[2, d, :, :, lanes] = jnp.where(w == 0, 0.0, pltpu.roll(here, 1, 1))
        return carry

    lax.fori_loop(0, 12, filter_step, 0)

    finish(stage)
    total = sa0[x].astype(F32)
    for k in range(XC - 1):
        total = total + rb0[k].astype(F32)
    sb[low] = total.astype(BF)
    total = sa1[dp, rep].astype(F32)
    for k in range(3):
        total = total + rb1[k].astype(F32)
    sb[high] = total.astype(BF)
    stage = []
    for k in range(1, ZC):
        stage.append(go(sb.at[pl.ds(lax.rem(z + k, ZC) * 9, 9)], rc.at[k - 1], at_z(k)))

    sm[...] = jnp.zeros((8, 32, 128), F32)

    def conv_step(j, carry):
        lanes = chunk(j)
        for a in range(3):
            for b in range(3):
                rows = tf[a : a + 2, b : b + 8, :, lanes]
                for e in range(3):
                    total = jnp.sum((sh[e, :, :, :, lanes] * rows).reshape(16, 16, 128), axis=0)
                    t = 9 * a + 3 * b + e
                    sm[j, t : t + 1] = jnp.sum(total, axis=0, keepdims=True)
        return carry

    lax.fori_loop(0, 6, conv_step, 0)
    for j in range(6):
        sm[j, 27:28] = gain_part[:, j * 128 : j * 128 + 128]
    scale = jnp.sum(scale_rows[0] + scale_rows[1], axis=-1, keepdims=True)
    sm[6, pl.ds(pl.multiple_of(core * 16, 16), 16)] = jnp.broadcast_to(scale, (16, 128))
    few, rest = pl.ds(0, 4), pl.ds(4, 4)
    little = []
    for k in range(1, 4):
        little.append(go(sm.at[few], qy1.at[k - 1], at_y(k)))
        little.append(go(sm.at[rest], qx1.at[k - 1], at_x(k)))

    finish(stage)
    mine = pl.ds(z * 9, 9)
    total = sb[mine].astype(F32)
    for k in range(ZC - 1):
        total = total + rc[k].astype(F32)
    full[core, rep, x, mine] = total.astype(BF)
    stage = []
    piece = full.at[core, rep, x, mine]
    for k in range(1, ZC):
        stage.append(go(piece, piece, at_z(k)))

    finish(little)
    s2[few] = sm[few] + qy1[0] + qy1[1] + qy1[2]
    s2[rest] = sm[rest] + qx1[0] + qx1[1] + qx1[2]
    little = []
    for k in range(1, 4):
        little.append(go(s2.at[few], qx2.at[k - 1], at_x(k)))
        little.append(go(s2.at[rest], qy2.at[k - 1], at_y(k)))

    finish(stage)
    piece = full.at[core, rep, x, low]
    stage = [go(piece, piece, other_rep)]
    piece = full.at[core, rep, x, high]
    stage += [go(piece, piece, at_x(k)) for k in range(1, XC)]
    piece = full.at[core, rep, x]
    handed = [go(piece, piece, other_core)]

    finish(little)
    s3[few] = s2[few] + qx2[0] + qx2[1] + qx2[2]
    s3[rest] = s2[rest] + qy2[0] + qy2[1] + qy2[2]
    little = [go(s3.at[lax.rem(z + k, ZC)], qz.at[k - 1], at_z(k)) for k in range(1, ZC)]

    finish(stage)
    piece = full.at[core, :, x, low]
    along = [go(piece, piece, at_x(k)) for k in range(1, XC)]
    piece = full.at[core, rep, :, high]
    across = go(piece, piece, other_rep)
    piece = full.at[core, 1 - rep, x, low]
    handed.append(go(piece, piece, other_core))
    for k in range(1, XC):
        piece = full.at[core, rep, lax.rem(x + k, XC), high]
        handed.append(go(piece, piece, other_core))

    finish(little)
    total = s3[z]
    for k in range(ZC - 1):
        total = total + qz[k]
    sz[core, z] = total
    little = [go(sz.at[core, z], sz.at[core, z], at_z(k)) for k in range(1, ZC)]

    for k in range(1, XC):
        along[k - 1].wait()
        piece = full.at[core, :, lax.rem(x + XC - k, XC), low]
        handed.append(go(piece, piece, other_core))
    across.wait()
    piece = full.at[core, 1 - rep, :, high]
    handed.append(go(piece, piece, other_core))
    finish(little)
    little = go(sz.at[core], sz.at[core], other_core)
    finish(handed)

    lane = iota((48, 128), 1)

    def assemble(i, carry):
        r, k = i // 4, lax.rem(i, 4)
        rows = pl.ds(pl.multiple_of(i * 48, 48), 48)
        for part in range(3):
            for m in range(6):
                halves = []
                for gets in range(2):
                    block = 2 * m + gets
                    c = block % 6 // 3
                    old = part * 6 + block // 6 * 3 + block % 3
                    tile = full[c, r, k, old // 2 * 6 : old // 2 * 6 + 6].astype(F32).reshape(48, 128)
                    halves.append(tile if old % 2 == gets else pltpu.roll(tile, 64, 1))
                start = part * C + m * 128
                gq_out[rows, start : start + 128] = jnp.where(lane < 64, halves[0], halves[1])
        for c in range(2):
            for m in range(6):
                tile = full[c, r, k, 54 + m * 3 : 57 + m * 3].astype(F32).reshape(24, 128)
                start = pl.multiple_of(c * 192 + i * 24, 8)
                gp_out[pl.ds(start, 24), m * 128 : m * 128 + 128] = tile
        return carry

    lax.fori_loop(0, 8, assemble, 0)
    little.wait()
    for j in range(6):
        total = sz[0, j] + sz[1, j]
        conv_out[:, j * 128 : j * 128 + 128] = total[0:27]
        gain_out[:, j * 128 : j * 128 + 128] = total[27:28]
    scale_out[...] = sz[0, 6] + sz[1, 6]


def finish_all(own, given, g, scale_rows, wq, wp, mixed, cot, tokens, halo, weight, gain):
    shape = jax.ShapeDtypeStruct
    field = (2, 8, 16, C)
    tile = (8, 128)
    some = (32, 128)
    copies = 1 + 6 + 2 + 6 + 7 + 6 + 7 + 6 + 5 + 7 + 4 + 4 + 7 + 4 + 1
    return pl.pallas_call(
        finish_kernel,
        out_shape=(
            shape(field, BF), shape(field, BF), shape((MINE, 3 * C), F32), shape((MINE, C), F32),
            shape((27, C), F32), shape((1, C), F32), shape(some, F32),
        ),
        in_specs=[VMEM] * 12,
        out_specs=(VMEM,) * 7,
        scratch_shapes=[
            pltpu.VMEM((256, 4 * MINE), BF), pltpu.VMEM((256, C), BF),
            pltpu.VMEM(field, F32), pltpu.VMEM(field, BF), pltpu.VMEM(field, BF),
            pltpu.VMEM((4, 10, 16, C), F32), pltpu.VMEM((4, 10, 16, C), F32), pltpu.VMEM((3,) + field, F32),
            pltpu.VMEM((3, XC, 36) + tile, BF), pltpu.VMEM((XC - 1, 2, 2, 36) + tile, BF),
            pltpu.VMEM((XC, 36) + tile, BF), pltpu.VMEM((2, 2, 36) + tile, BF),
            pltpu.VMEM((XC - 1, 36) + tile, BF), pltpu.VMEM((3, 36) + tile, BF),
            pltpu.VMEM((72,) + tile, BF), pltpu.VMEM((ZC - 1, 9) + tile, BF),
            pltpu.VMEM((2, 2, XC, 72) + tile, BF),
            pltpu.VMEM((8,) + some, F32), pltpu.VMEM((8,) + some, F32), pltpu.VMEM((8,) + some, F32),
            pltpu.VMEM((2, 8) + some, F32),
            pltpu.VMEM((3, 4) + some, F32), pltpu.VMEM((3, 4) + some, F32),
            pltpu.VMEM((3, 4) + some, F32), pltpu.VMEM((3, 4) + some, F32),
            pltpu.VMEM((ZC - 1,) + some, F32),
            DMA((copies,)), DMA((copies,)),
        ],
        compiler_params=pltpu.CompilerParams(
            collective_id=0, has_side_effects=True, vmem_limit_bytes=60 << 20
        ),
        name="finish",
    )(own, given, g, scale_rows, wq, wp, mixed, cot, tokens, halo, weight, gain)


def per_device(tokens, cotangent, w_qkv, w_proj, conv_weight, norm_gain, head_scale, shift_offsets):
    slab = tokens[0]
    cot = cotangent[0].reshape(256, C)
    gain = norm_gain.reshape(1, C)
    scales = head_scale.reshape(2, 2, 6).transpose(1, 0, 2).reshape(2, 12)
    nwin, cwin, wq, wp, mixed, halo = mix(slab, cot, w_qkv, w_proj.reshape(2, 192, C), conv_weight, gain)
    own, given, grads, scale_rows = attend(shift_offsets, scales, nwin, cwin, wq, wp)
    output, grad_tokens, grad_qkv, grad_proj, conv, gain_sum, scale = finish_all(
        own, given, grads, scale_rows, wq, wp, mixed, cot, slab, halo, conv_weight, gain
    )
    factor = 1.0 / math.sqrt(lax.axis_size("rep") * lax.axis_size("dp") * SEQ * 256)
    scale = scale[:, 0].reshape(2, 16)[:, :12].reshape(2, 2, 6).transpose(1, 0, 2).reshape(24)
    return (
        output[None],
        grad_tokens[None],
        grad_qkv * factor,
        grad_proj * factor,
        conv * factor,
        gain_sum.reshape(C) * factor,
        scale * factor,
    )


def solution(mesh):
    in_specs = (
        P(("rep", "dp"), "seq", None, None, None),
        P(("rep", "dp"), "seq", None, None, None),
        P("dp", None),
        P("dp", None),
        P(),
        P(),
        P(),
        P(),
    )
    out_specs = (
        P(("rep", "dp"), "seq", None, None, None),
        P(("rep", "dp"), "seq", None, None, None),
        P("dp", None),
        P("dp", None),
        P(),
        P(),
        P(),
    )
    return jax.shard_map(
        per_device, mesh=mesh, in_specs=in_specs, out_specs=out_specs, check_vma=False
    )
```

time: 205 us -> 151 us (0.74)
  local copies, waits for them, and re-layouts: 41.2 us -> 11.9 us
  waiting for transfers between devices: 13.3 us -> 0 us
  Pallas kernels: 138 us -> 128 us
  starting transfers between devices: 7.3 us -> 0 us
  other arithmetic: 3.88 us -> 9.29 us
    ppermute x3 -> x0, waiting for transfers between devices: 13.3 us -> none  [the longest x1 11.7 us: per_device(): recv = lax.ppermute(given, 'seq', pairs)]
    transpose x3 -> x0, local copies, waits for them, and re-layouts: 12.7 us -> none  [the longest x1 6.27 us: per_device(): part.reshape(384, 2, 3, 2, 192).transpose(0, 2, 3, 1, 4).reshape(384, 3 * C)]
    reshape x6 -> x0, local copies, waits for them, and re-layouts: 11.3 us -> none  [the longest x1 8.06 us: per_device(): part.reshape(384, 2, 3, 2, 192).transpose(0, 2, 3, 1, 4).reshape(384, 3 * C)]
    pallas_call x3 -> x1, Pallas kernels: 81.2 us -> 70.1 us  [finish_all(): pl.pallas_call(finish_kernel, out_shape=(shape(field, BF), shape(field, B...]
    mul x2 -> x5, other arithmetic: 0.42 us -> 9.29 us  [the longest x1 4.09 us: per_device(): grad_qkv * factor]
    ppermute x3 -> x0, starting transfers between devices: 7.3 us -> none  [the longest x1 5.2 us: per_device(): after = lax.ppermute(bmh[0], 'seq', [(i + 1, i) for i in range(SEQ - 1)])]
    another operation x2 -> x1, local copies, waits for them, and re-layouts: 3.08 us -> 0.08 us  [per_device(): scale[:, 0].reshape(2, 16)[:, :12].reshape(2, 2, 6).transpose(1, 0, 2)]
    another operation x1 -> x0, other arithmetic: 2.55 us -> none  [per_device(): wq = jnp.stack([wq[:, :, :, c].reshape(rows, 3 * MINE) for c in range(2)])]
  transfers between devices with their start and end apart: 3 -> 0, of which waited for: 2 -> 0; matrix products, arithmetic and copies ran while one was open for 1% -> 0% of each run, Pallas kernels for 0% -> 0%
where the time goes in v3:
time: 151 us; the launch traced here: 150 us
  Pallas kernels  128 us (85%)
  local copies, waits for them, and re-layouts  11.9 us (8%)
  other arithmetic  9.29 us (6%)
    pallas_call x1, Pallas kernels, finish_all(): pl.pallas_call(finish_kernel, out_shape=(shape(field, BF), shape(field, B...  70.1 us
    pallas_call x1, Pallas kernels, mix(): pl.pallas_call(mix_kernel, out_shape=(shape((2, 256, C), BF), shape((2, 2...  31.8 us
    pallas_call x1, Pallas kernels, attend(): pl.pallas_call(attend_kernel, out_shape=(shape((256, 4 * MINE), BF), shap...  26.5 us
    unnamed x30, local copies, waits for them, and re-layouts  8.76 us
    mul x1, other arithmetic, per_device(): grad_qkv * factor  4.09 us

profile of v3, /device:TPU:1, one launch (start us, length us, event | category | flops | bytes accessed | tf_op | source)
XLA Modules:
  0.0 150.3 jit_solution(1164463098657946511)
XLA Ops:
  0.6 0.0 copy-start.11
  0.6 0.7 reshape.35
  1.4 0.1 reshape.36.scales
  1.5 0.7 reshape.38.gain
  2.2 1.0 copy-done.1
  3.2 1.0 copy-done.2
  4.2 1.1 copy-done.6
  5.2 0.9 copy-done.8
  6.1 31.8 %mix.1 = (bf16[2,256,768]{2,1,0:T(8,128)(2,1)S(1)}, bf16[2,256,768]{2,1,0:T(8,128)(2,1)S(1)}, bf16[2,2,384,1152]{3,2,1,0:T(8,128)(2,1)}, bf16[2,2,192,768]{3,2,1...) custom-call(bf16[2,8,16,768]{3,2,1,0:T(8,128)(2,1)S(1)} %bitcast.8, ...), custom_call_target="tpu_custom_call" | custom-call | tf_op jit(solution)/shard_map/mix/pallas_call | solution.py:179
  37.9 0.0 copy-start.3
  37.9 0.9 copy-done.3
  38.8 0.0 copy-done.11
  38.8 26.5 %attend.1 = (bf16[256,1536]{1,0:T(8,128)(2,1)S(1)}, bf16[256,1536]{1,0:T(8,128)(2,1)S(1)}, bf16[2,2,4,72,8,128]{5,4,3,2,1,0:T(8,128)(2,1)}, f32[2,16,256]{2,1,0:T(8,128)S(1)}) custom-call(s32[2]{0:T(128)S(1)} %copy-done.11, f32[2,12]{1,0:T(2,128)S(1)} %reshape.36.scales, bf16[2,256,768]{2,1,0:T(8,128)(2,1)S(1)} %get-tuple-element.24.nwin, ...), custom_call_target="tpu_custom_call" | custom-call | tf_op jit(solution)/shard_map/attend/pallas_call | solution.py:305
  65.4 0.0 copy-done.10
  65.4 0.0 copy-done
  65.4 0.0 copy-done.7
  65.4 0.0 copy-start.4
  65.4 0.9 copy-done.4
  66.3 0.9 copy-done.5
  67.2 0.6 copy-done.9
  67.8 70.1 %finish.1 = (bf16[2,8,16,768]{3,2,1,0:T(8,128)(2,1)}, bf16[2,8,16,768]{3,2,1,0:T(8,128)(2,1)}, f32[384,2304]{1,0:T(8,128)}, f32[384,768]{1,0:T(8,128)}, f32[27,7...) custom-call(bf16[256,1536]{1,0:T(8,128)(2,1)} %copy-done.4, bf16[256,1536]{1,0:T(8,128)(2,1)} %copy-done.5, ...), custom_call_target="tpu_custom_call" | custom-call | tf_op jit(solution)/shard_map/finish/pallas_call | solution.py:575
  137.9 0.8 slice_reduce_fusion
  138.8 0.1 reshape_squeeze.7
  138.8 0.1 mul.49
  138.9 0.6 mul.51
  139.5 1.3 multiply_reduce_fusion
  140.8 1.5 %broadcast_multiply_fusion.2 = f32[27,768]{1,0:T(8,128)} fusion(f32[27,768]{1,0:T(8,128)} %get-tuple-element.38), kind=kLoop, calls=%fused_computation.2 | loop fusion | flops 20736 | bytes 165888 | tf_op jit(solution)/shard_map/mul | solution.py:623
  142.4 2.4 %broadcast_multiply_fusion.1 = f32[384,768]{1,0:T(8,128)} fusion(f32[384,768]{1,0:T(8,128)} %get-tuple-element.37), kind=kLoop, calls=%fused_computation.1 | loop fusion | flops 294912 | bytes 2359296 | tf_op jit(solution)/shard_map/mul | solution.py:622
  144.7 4.1 %broadcast_multiply_fusion = f32[384,2304]{1,0:T(8,128)} fusion(f32[384,2304]{1,0:T(8,128)} %get-tuple-element.36), kind=kLoop, calls=%fused_computation | loop fusion | flops 884736 | bytes 7077888 | tf_op jit(solution)/shard_map/mul | solution.py:621
  148.8 0.0 copy-done.13
  148.8 0.7 copy.21
  149.6 0.7 copy.22
  (15 shorter events, 0.0 us)
Async XLA Ops:
  0.6 38.2 %copy-start.11 = (s32[2]{0:T(128)S(1)}, s32[2]{0:T(128)}, u32[]{:S(2)}) copy-start(s32[2]{0:T(128)} %shift.1) | copy-start | bytes 28
  2.2 1.0 copy-start.1
  3.2 1.0 copy-start.2
  4.2 1.1 copy-start.6
  5.2 0.9 copy-start.8
  6.1 59.2 %copy-start.10 = (f32[1,768]{1,0:T(1,128)}, f32[1,768]{1,0:T(1,128)S(1)}, u32[]{:S(2)}) copy-start(f32[1,768]{1,0:T(1,128)S(1)} %reshape.38.gain) | copy-start | bytes 9220
  37.9 0.9 copy-start.3
  38.8 26.5 %copy-start = (bf16[2,2,192,768]{3,2,1,0:T(8,128)(2,1)}, bf16[2,2,192,768]{3,2,1,0:T(8,128)(2,1)S(1)}, u32[]{:S(2)}) copy-start(bf16[2,2,192,768]{3,2,1,0:T(8,128)(2,1)S(1)} %get-tuple-element.27.wp) | copy-start | bytes 3538948
  38.8 26.5 %copy-start.7 = (bf16[2,8,16,768]{3,2,1,0:T(8,128)(2,1)}, bf16[2,8,16,768]{3,2,1,0:T(8,128)(2,1)S(1)}, u32[]{:S(2)}) copy-start(bf16[2,8,16,768]{3,2,1,0:T(8,128)(2,1)S(1)} %get-tuple-element.33.halo) | copy-start | bytes 1179652
  65.4 0.9 copy-start.4
  66.3 0.9 copy-start.5
  67.2 0.6 copy-start.9
  144.7 4.1 %copy-start.13 = (bf16[2,8,16,768]{3,2,1,0:T(8,128)(2,1)S(1)}, bf16[2,8,16,768]{3,2,1,0:T(8,128)(2,1)}, u32[]{:S(2)}) copy-start(bf16[2,8,16,768]{3,2,1,0:T(8,128)(2,1)} %get-tuple-element.34) | copy-start | bytes 1179652
  144.7 4.8 %copy-start.12 = (bf16[2,8,16,768]{3,2,1,0:T(8,128)(2,1)S(1)}, bf16[2,8,16,768]{3,2,1,0:T(8,128)(2,1)}, u32[]{:S(2)}) copy-start(bf16[2,8,16,768]{3,2,1,0:T(8,128)(2,1)} %get-tuple-element.35) | copy-start | bytes 1179652

commit v4 on v3

v4 whole, which is shorter than its diff:
```python
import math

import jax
import jax.numpy as jnp
from jax import lax
from jax.experimental import pallas as pl
from jax.experimental.pallas import tpu as pltpu
from jax.sharding import PartitionSpec as P

MESH = pl.DeviceIdType.MESH
BF = jnp.bfloat16
F32 = jnp.float32
XC = 4
ZC = 8
SEQ = 64
C = 768
MINE = 384
TILES = (0, 36, 18)
VMEM = pl.BlockSpec(memory_space=pltpu.VMEM)
SMEM = pl.BlockSpec(memory_space=pltpu.SMEM)
DMA = pltpu.SemaphoreType.DMA


def nn(a, b):
    return lax.dot_general(a, b, (((1,), (0,)), ((), ())), preferred_element_type=F32)


def nt(a, b):
    return lax.dot_general(a, b, (((1,), (1,)), ((), ())), preferred_element_type=F32)


def tn(a, b):
    return lax.dot_general(a, b, (((0,), (0,)), ((), ())), preferred_element_type=F32)


def iota(shape, dim):
    return lax.broadcasted_iota(jnp.int32, shape, dim)


def place():
    rep, dp, seq = lax.axis_index("rep"), lax.axis_index("dp"), lax.axis_index("seq")
    return (rep, dp, seq, lax.rem(seq, 2))


def send(src, dst, s, r, to):
    c = pltpu.make_async_remote_copy(
        src_ref=src, dst_ref=dst, send_sem=s, recv_sem=r, device_id=to, device_id_type=MESH
    )
    c.start()
    return c


def greet(peers):
    barrier = pltpu.get_barrier_semaphore()
    for peer in peers:
        pl.semaphore_signal(barrier, inc=1, device_id=peer, device_id_type=MESH)
    pl.semaphore_wait(barrier, len(peers))


def fill_padded(xf, before, own, after):
    rows = jnp.zeros((4, 1, 16, C), F32)
    xf[:, 0:1] = rows
    xf[:, 9:10] = rows
    xf[0, 1:9] = before
    xf[1:3, 1:9] = own
    xf[3, 1:9] = after


def taps(xf, weight, d, lanes, flipped):
    sums = [jnp.zeros((8, 16, 128), F32) for _ in range(3)]
    for a in range(3):
        for b in range(3):
            rows = xf[d + a, b : b + 8, :, lanes]
            for e in range(3):
                t = 9 * a + 3 * b + e
                t = 26 - t if flipped else t
                sums[e] = sums[e] + weight[t : t + 1, lanes][None] * rows
    w = iota((8, 16, 128), 1)
    left = jnp.where(w == 0, 0.0, pltpu.roll(sums[0], 1, 1))
    right = jnp.where(w == 15, 0.0, pltpu.roll(sums[2], 15, 1))
    return sums[1] + left + right


def chunk(j):
    return pl.ds(pl.multiple_of(j * 128, 128), 128)


def normalise(rows):
    centred = rows - jnp.mean(rows, axis=-1, keepdims=True)
    inverse = lax.rsqrt(jnp.mean(centred * centred, axis=-1, keepdims=True) + 1e-05)
    return (centred * inverse, inverse)


def arrange(w, into, dp):
    lane, other = iota((128, 128), 0), iota((128, 128), 1)
    moves = {}
    for had in range(2):
        for gets in range(2):
            hit = (lane - 64 * had == other - 64 * gets) & (other // 64 == gets)
            moves[had, gets] = jnp.where(hit, 1.0, 0.0).astype(BF)
    for c in range(2):
        for k in range(9):
            part, group = k // 3, k % 3
            pieces = []
            for gets in range(2):
                block = 2 * group + gets
                old = part * 12 + block // 3 * 6 + c * 3 + block % 3
                start = old // 2 * 128
                pieces.append(nn(w[:, start : start + 128], moves[old % 2, gets]))
            start = group * MINE + part * 128
            into[c, dp, :, start : start + 128] = (pieces[0] + pieces[1]).astype(BF)


def source_of(n, r):
    b, d, h, j = n >> 8, (n >> 6) & 3, (n >> 3) & 7, n & 7
    return d * 128 + h * 16 + ((8 * b + j + r) & 15)


def head_sums(x, ones):
    high = x.astype(BF)
    low = (x - high.astype(F32)).astype(BF)
    return nn(high, ones) + nn(low, ones)


def attention(shift, scales, core, g, b, qkv_s, ba_s, att_s, bqkv_s, allow_s, scale_s):
    ones = jnp.where(iota((128, 128), 0) // 32 == iota((128, 128), 1) // 32, 1.0, 0.0).astype(BF)
    lane_head = iota((256, 128), 1) // 32
    rows = pl.ds(pl.multiple_of(b * 256, 256), 256)
    query = qkv_s[rows, 0:128].astype(F32)
    key = qkv_s[rows, 128:256].astype(F32)
    value = qkv_s[rows, 256:384]
    ba = ba_s[rows, g * 128 : g * 128 + 128]
    inv_q = lax.rsqrt(head_sums(query * query, ones) + 1.0)
    inv_k = lax.rsqrt(head_sums(key * key, ones) + 1.0)
    uq = (query * inv_q).astype(BF)
    uk = (key * inv_k).astype(BF)
    att = jnp.zeros((256, 128), F32)
    back_v = jnp.zeros((256, 128), F32)
    back_uq = jnp.zeros((256, 128), F32)
    back_uk = jnp.zeros((256, 128), F32)
    zero = jnp.zeros((256, 128), BF)
    for h in range(4):
        here = lane_head == h
        scale = scales[core, g * 4 + h]
        uq_h = jnp.where(here, uq, zero)
        uk_h = jnp.where(here, uk, zero)
        v_h = jnp.where(here, value, zero)
        ba_h = jnp.where(here, ba, zero)
        cosine = nt(uk_h, uq)
        expo = jnp.exp(scale * cosine) * allow_s[b]
        prob = expo * (1.0 / jnp.sum(expo, axis=0, keepdims=True))
        weights = prob.astype(BF)
        att = att + tn(weights, v_h)
        back_v = back_v + nn(weights, ba_h)
        back_prob = nt(v_h, ba)
        mean = jnp.sum(prob * back_prob, axis=0, keepdims=True)
        back_score = prob * (back_prob - mean)
        scale_s[b, g * 4 + h : g * 4 + h + 1] = jnp.sum(back_score * cosine, axis=0, keepdims=True)
        scaled = (back_score * scale).astype(BF)
        back_uq = back_uq + tn(scaled, uk_h)
        back_uk = back_uk + nn(scaled, uq_h)
    att_s[rows, g * 128 : g * 128 + 128] = att.astype(BF)
    inner_q = head_sums(query * back_uq, ones)
    inner_k = head_sums(key * back_uk, ones)
    back_q = back_uq * inv_q - query * inner_q * (inv_q * inv_q * inv_q)
    back_k = back_uk * inv_k - key * inner_k * (inv_k * inv_k * inv_k)
    bqkv_s[rows, 0:128] = back_q.astype(BF)
    bqkv_s[rows, 128:256] = back_k.astype(BF)
    bqkv_s[rows, 256:384] = back_v.astype(BF)


def block_kernel(shift, scales, tokens, cot, wq_in, wp_in, weight, gain,
                 out, grad, gq_out, gp_out, conv_out, gain_out, scale_out,
                 halo, nwin, cwin, wq, wp, mixed, sel, res, x_s, xt_s, ct_s, qkv_s, ba_s, att_s, bqkv_s, allow_s,
                 scale_s, gq_s, gp_s, g, own, given,
                 recv, bn_s, bm, bmh, ph, xf, tf, sh, ra0, ra1, sa0, sa1, rb0, rb1, sb, rc, full,
                 sm, s2, s3, sz, qy1, qx1, qx2, qy2, qz, s_sem, r_sem, l_sem):
    rep, dp, seq, core = place()
    z = lax.rem(seq // 2, ZC)
    x = seq // (2 * ZC)
    y = rep * 2 + dp

    def at_y(step):
        there = lax.rem(y + step, 4)
        return (there // 2, lax.rem(there, 2), seq)

    def at_x(step):
        there = lax.rem(x + step, XC)
        return (rep, dp, (there * ZC + z) * 2 + core)

    def at_z(step):
        there = lax.rem(z + step, ZC)
        return (rep, dp, (x * ZC + there) * 2 + core)

    up = (rep, dp, lax.rem(seq + 1, SEQ))
    down = (rep, dp, lax.rem(seq + SEQ - 1, SEQ))
    partner = (rep, dp, lax.rem(seq + SEQ - 1 + 2 * core, SEQ))
    other_core = (rep, dp, seq + 1 - 2 * core)
    other_rep = (1 - rep, dp, seq)
    peers = [at_y(k) for k in range(1, 4)] + [at_x(k) for k in range(1, XC)]
    peers += [at_z(k) for k in range(1, ZC)] + [up, down]
    greet(peers)
    used = [0]

    def go(src, dst, to):
        n = used[0]
        used[0] += 1
        return send(src, dst, s_sem.at[n], r_sem.at[n], to)

    def finish(copies):
        for c in copies:
            c.wait()

    low, high = pl.ds(0, 36), pl.ds(36, 36)
    first = jnp.where(seq == 0, 0.0, 1.0).astype(F32)
    last = jnp.where(seq == SEQ - 1, 0.0, 1.0).astype(F32)
    half = 1 - core
    halos = [go(tokens.at[0], halo.at[1], down), go(tokens.at[1], halo.at[0], up)]
    local = [
        pltpu.make_async_copy(cot, cwin.at[half], l_sem.at[0]),
        pltpu.make_async_copy(wp_in, wp.at[:, dp], l_sem.at[1]),
    ]
    for c in local:
        c.start()
    y_to = lax.rem(y + 3 + 2 * core, 4)
    y_peer = (y_to // 2, lax.rem(y_to, 2), seq)
    wp_came = go(wp_in.at[core], wp.at[core, dp], y_peer)
    cots = go(cot, cwin.at[half], partner)
    arrange(wq_in, wq, dp)
    wq_came = []
    for k in range(3):
        piece = wq.at[core, dp, :, k * MINE : k * MINE + MINE]
        wq_came.append(go(piece, piece, y_peer))
    finish(halos)
    fill_padded(tf, halo[0].astype(F32) * first, tokens[...].astype(F32), halo[1].astype(F32) * last)

    def mix_step(i, carry):
        d, j = i // 6, lax.rem(i, 6)
        lanes = chunk(j)
        mixed[d, :, :, lanes] = tf[d + 1, 1:9, :, lanes] + taps(tf, weight, d, lanes, False)
        return carry

    lax.fori_loop(0, 12, mix_step, 0)

    def unit_step(i, carry):
        d, h = i // 2, lax.rem(i, 2) * 4
        unit, _ = normalise(mixed[d, pl.ds(h, 4)].reshape(64, C))
        nwin[half, pl.ds(pl.multiple_of(i * 64, 64), 64)] = (unit * gain[...]).astype(BF)
        return carry

    lax.fori_loop(0, 4, unit_step, 0)
    norms = go(nwin.at[half], nwin.at[half], partner)

    s, r = shift[0], shift[1]
    sel[...] = jnp.where(iota((512, 512), 1) == source_of(iota((512, 512), 0), r), 1.0, 0.0).astype(BF)
    for k in range(2):
        target = source_of(iota((256, 512), 1), r)
        res[k] = jnp.where(iota((256, 512), 0) + 256 * k == target, 1.0, 0.0).astype(BF)

    def code(n, b):
        h, j = (n >> 3) & 7, n & 7
        return jnp.where(h < s, 2, 0) + jnp.where(8 * b + j + r >= 16, 1, 0)

    for b in range(2):
        same = code(iota((256, 256), 0), b) == code(iota((256, 256), 1), b)
        allow_s[b] = jnp.where(same, 1.0, 0.0).astype(F32)
    scale_s[...] = jnp.zeros((2, 16, 256), F32)
    for c in local:
        c.wait()
    cots.wait()
    ct_s[...] = nn(sel[...], cwin[...].reshape(512, C)).astype(BF)
    wp_came.wait()
    ba_s[...] = nt(ct_s[...], wp[core].reshape(MINE, C)).astype(BF)
    norms.wait()
    ordered = nn(sel[...], nwin[...].reshape(512, C))
    x_s[...] = ordered.astype(BF)
    xt_s[...] = ordered.T.astype(BF)

    exchanges, stage, swaps = [], [], []
    for k in range(3):
        wq_came[k].wait()
        if k == 2:
            piece = wq.at[core, 1 - dp]
            swaps.append(go(piece, piece, other_core))
            piece = wp.at[core, 1 - dp]
            swaps.append(go(piece, piece, other_core))
        columns = wq[core, :, :, k * MINE : k * MINE + MINE].reshape(C, MINE)
        qkv_s[...] = nn(x_s[...], columns).astype(BF)

        def window(b, carry):
            attention(shift, scales, core, k, b, qkv_s, ba_s, att_s, bqkv_s, allow_s, scale_s)
            return carry

        lax.fori_loop(0, 2, window, 0)
        lanes = slice(k * 128, k * 128 + 128)
        given[k, :, 0:128] = nn(res[core], att_s[:, lanes]).astype(BF)
        given[k, :, 128:] = nn(res[core], bqkv_s[...]).astype(BF)
        exchanges.append(go(given.at[k], recv.at[k], partner))
        gq_s[...] = nn(xt_s[...], bqkv_s[...])

        def store(i, carry):
            d, p, to = i // 8, lax.rem(i // 4, 2), lax.rem(i, 4)
            for c in range(3):
                block = gq_s[pl.ds(pl.multiple_of(i * 48, 48), 48), c * 128 : (c + 1) * 128]
                start = TILES[k] + c * 6
                g[d, p, to, start : start + 6] = block.reshape(6, 8, 128).astype(BF)
            return carry

        lax.fori_loop(0, 16, store, 0)
        tiles = pl.ds(TILES[k], 18)
        away = pl.ds(TILES[k] % 36, 18)
        for step in range(1, 4):
            if k == 1:
                stage.append(go(g.at[:, :, lax.rem(x + step, XC), tiles], ra1.at[step - 1, :, :, away], at_x(step)))
            else:
                to = at_y(step)
                stage.append(go(g.at[to[1], to[0], :, tiles], ra0.at[step - 1, :, away], to))
        own[k, :, 0:128] = nn(res[half], att_s[:, lanes]).astype(BF)
        own[k, :, 128:] = nn(res[half], bqkv_s[...]).astype(BF)
    gp_s[...] = tn(att_s[...], ct_s[...])

    def store_proj(i, carry):
        d, p, to = i // 8, lax.rem(i // 4, 2), lax.rem(i, 4)
        for c in range(6):
            block = gp_s[pl.ds(pl.multiple_of(i * 24, 24), 24), c * 128 : (c + 1) * 128]
            g[d, p, to, 54 + c * 3 : 57 + c * 3] = block.reshape(3, 8, 128).astype(BF)
        return carry

    lax.fori_loop(0, 16, store_proj, 0)
    tiles, away = pl.ds(54, 18), pl.ds(18, 18)
    for step in range(1, 4):
        stage.append(go(g.at[:, :, lax.rem(x + step, XC), tiles], ra1.at[step - 1, :, :, away], at_x(step)))

    def wq_of(c, k):
        return wq[c, :, :, k * MINE : k * MINE + MINE].reshape(C, MINE)

    finish(swaps)
    back = nt(own[0, :, 128:], wq_of(core, 0))
    for k in range(1, 3):
        back = back + nt(own[k, :, 128:], wq_of(core, k))
    for k in range(3):
        exchanges[k].wait()
        back = back + nt(recv[k, :, 128:], wq_of(1 - core, k))
    bn_s[...] = back.astype(BF)
    def norm_step(i, total):
        d, h = i // 2, lax.rem(i, 2) * 4
        rows = pl.ds(pl.multiple_of(i * 64, 64), 64)
        unit, inverse = normalise(mixed[d, pl.ds(h, 4)].reshape(64, C))
        back_float = bn_s[rows].astype(F32)
        total = total + jnp.sum((back_float * unit).reshape(8, 8, C), axis=0)
        grad_unit = back_float * gain[...]
        mean = jnp.mean(grad_unit, axis=-1, keepdims=True)
        slope = jnp.mean(grad_unit * unit, axis=-1, keepdims=True)
        result = cot[rows].astype(F32) + inverse * (grad_unit - mean - unit * slope)
        bm[d, pl.ds(h, 4)] = result.reshape(4, 16, C)
        bmh[d, pl.ds(h, 4)] = result.astype(BF).reshape(4, 16, C)
        return total

    gain_part = jnp.sum(lax.fori_loop(0, 4, norm_step, jnp.zeros((8, C), F32)), axis=0, keepdims=True)
    planes = [go(bmh.at[0], ph.at[1], down), go(bmh.at[1], ph.at[0], up)]
    finish(stage)

    def add_a(i, carry):
        total = g[dp, rep, i, low].astype(F32)
        for k in range(3):
            total = total + ra0[k, i].astype(F32)
        sa0[i] = total.astype(BF)
        d, r = lax.rem(i, 2), i // 2
        total = g[d, r, x, high].astype(F32)
        for k in range(XC - 1):
            total = total + ra1[k, d, r].astype(F32)
        sa1[d, r] = total.astype(BF)
        return carry

    lax.fori_loop(0, 4, add_a, 0)
    stage = []
    for k in range(1, XC):
        stage.append(go(sa0.at[lax.rem(x + k, XC)], rb0.at[k - 1], at_x(k)))
    for k in range(1, 4):
        to = at_y(k)
        stage.append(go(sa1.at[to[1], to[0]], rb1.at[k - 1], to))

    wp_mine, wp_other = wp[core].reshape(MINE, C), wp[1 - core].reshape(MINE, C)
    proj = jnp.zeros((256, C), F32)
    for k in range(3):
        rows = slice(k * 128, k * 128 + 128)
        proj = proj + nn(own[k, :, 0:128], wp_mine[rows]) + nn(recv[k, :, 0:128], wp_other[rows])
    out[...] = (mixed[...].reshape(256, C) + proj).astype(BF).reshape(2, 8, 16, C)

    finish(planes)
    fill_padded(xf, ph[0].astype(F32) * first, bm[...], ph[1].astype(F32) * last)

    def filter_step(i, carry):
        d, j = i // 6, lax.rem(i, 6)
        lanes = chunk(j)
        here = xf[d + 1, 1:9, :, lanes]
        grad[d, :, :, lanes] = (here + taps(xf, weight, d, lanes, True)).astype(BF)
        w = iota((8, 16, 128), 1)
        sh[0, d, :, :, lanes] = jnp.where(w == 15, 0.0, pltpu.roll(here, 15, 1))
        sh[1, d, :, :, lanes] = here
        sh[2, d, :, :, lanes] = jnp.where(w == 0, 0.0, pltpu.roll(here, 1, 1))
        return carry

    lax.fori_loop(0, 12, filter_step, 0)

    finish(stage)
    total = sa0[x].astype(F32)
    for k in range(XC - 1):
        total = total + rb0[k].astype(F32)
    sb[low] = total.astype(BF)
    total = sa1[dp, rep].astype(F32)
    for k in range(3):
        total = total + rb1[k].astype(F32)
    sb[high] = total.astype(BF)
    stage = []
    for k in range(1, ZC):
        stage.append(go(sb.at[pl.ds(lax.rem(z + k, ZC) * 9, 9)], rc.at[k - 1], at_z(k)))

    sm[...] = jnp.zeros((8, 32, 128), F32)

    def conv_step(j, carry):
        lanes = chunk(j)
        for a in range(3):
            for b in range(3):
                rows = tf[a : a + 2, b : b + 8, :, lanes]
                for e in range(3):
                    total = jnp.sum((sh[e, :, :, :, lanes] * rows).reshape(16, 16, 128), axis=0)
                    t = 9 * a + 3 * b + e
                    sm[j, t : t + 1] = jnp.sum(total, axis=0, keepdims=True)
        return carry

    lax.fori_loop(0, 6, conv_step, 0)
    for j in range(6):
        sm[j, 27:28] = gain_part[:, j * 128 : j * 128 + 128]
    scale = jnp.sum(scale_s[0] + scale_s[1], axis=-1, keepdims=True)
    sm[6, pl.ds(pl.multiple_of(core * 16, 16), 16)] = jnp.broadcast_to(scale, (16, 128))
    few, rest = pl.ds(0, 4), pl.ds(4, 4)
    little = []
    for k in range(1, 4):
        little.append(go(sm.at[few], qy1.at[k - 1], at_y(k)))
        little.append(go(sm.at[rest], qx1.at[k - 1], at_x(k)))

    finish(stage)
    mine = pl.ds(z * 9, 9)
    total = sb[mine].astype(F32)
    for k in range(ZC - 1):
        total = total + rc[k].astype(F32)
    full[core, rep, x, mine] = total.astype(BF)
    stage = []
    piece = full.at[core, rep, x, mine]
    for k in range(1, ZC):
        stage.append(go(piece, piece, at_z(k)))

    finish(little)
    s2[few] = sm[few] + qy1[0] + qy1[1] + qy1[2]
    s2[rest] = sm[rest] + qx1[0] + qx1[1] + qx1[2]
    little = []
    for k in range(1, 4):
        little.append(go(s2.at[few], qx2.at[k - 1], at_x(k)))
        little.append(go(s2.at[rest], qy2.at[k - 1], at_y(k)))

    finish(stage)
    piece = full.at[core, rep, x, low]
    stage = [go(piece, piece, other_rep)]
    piece = full.at[core, rep, x, high]
    stage += [go(piece, piece, at_x(k)) for k in range(1, XC)]
    piece = full.at[core, rep, x]
    handed = [go(piece, piece, other_core)]

    finish(little)
    s3[few] = s2[few] + qx2[0] + qx2[1] + qx2[2]
    s3[rest] = s2[rest] + qy2[0] + qy2[1] + qy2[2]
    little = [go(s3.at[lax.rem(z + k, ZC)], qz.at[k - 1], at_z(k)) for k in range(1, ZC)]

    finish(stage)
    piece = full.at[core, :, x, low]
    along = [go(piece, piece, at_x(k)) for k in range(1, XC)]
    piece = full.at[core, rep, :, high]
    across = go(piece, piece, other_rep)
    piece = full.at[core, 1 - rep, x, low]
    handed.append(go(piece, piece, other_core))
    for k in range(1, XC):
        piece = full.at[core, rep, lax.rem(x + k, XC), high]
        handed.append(go(piece, piece, other_core))

    finish(little)
    total = s3[z]
    for k in range(ZC - 1):
        total = total + qz[k]
    sz[core, z] = total
    little = [go(sz.at[core, z], sz.at[core, z], at_z(k)) for k in range(1, ZC)]

    for k in range(1, XC):
        along[k - 1].wait()
        piece = full.at[core, :, lax.rem(x + XC - k, XC), low]
        handed.append(go(piece, piece, other_core))
    across.wait()
    piece = full.at[core, 1 - rep, :, high]
    handed.append(go(piece, piece, other_core))
    finish(little)
    little = go(sz.at[core], sz.at[core], other_core)
    finish(handed)

    lane = iota((48, 128), 1)

    def assemble(i, carry):
        r, k = i // 4, lax.rem(i, 4)
        rows = pl.ds(pl.multiple_of(i * 48, 48), 48)
        for part in range(3):
            for m in range(6):
                halves = []
                for gets in range(2):
                    block = 2 * m + gets
                    c = block % 6 // 3
                    old = block // 6 * 3 + block % 3
                    start = TILES[old // 2] + part * 6
                    tile = full[c, r, k, start : start + 6].astype(F32).reshape(48, 128)
                    halves.append(tile if old % 2 == gets else pltpu.roll(tile, 64, 1))
                start = part * C + m * 128
                gq_out[rows, start : start + 128] = jnp.where(lane < 64, halves[0], halves[1])
        for c in range(2):
            for m in range(6):
                tile = full[c, r, k, 54 + m * 3 : 57 + m * 3].astype(F32).reshape(24, 128)
                start = pl.multiple_of(c * 192 + i * 24, 8)
                gp_out[pl.ds(start, 24), m * 128 : m * 128 + 128] = tile
        return carry

    lax.fori_loop(0, 8, assemble, 0)
    little.wait()
    for j in range(6):
        total = sz[0, j] + sz[1, j]
        conv_out[:, j * 128 : j * 128 + 128] = total[0:27]
        gain_out[:, j * 128 : j * 128 + 128] = total[27:28]
    scale_out[...] = sz[0, 6] + sz[1, 6]


def whole_block(shift, scales, tokens, cot, wq, wp, weight, gain):
    shape = jax.ShapeDtypeStruct
    field = (2, 8, 16, C)
    tile = (8, 128)
    some = (32, 128)
    V = pltpu.VMEM
    copies = 96
    return pl.pallas_call(
        block_kernel,
        out_shape=(
            shape(field, BF), shape(field, BF), shape((MINE, 3 * C), F32), shape((MINE, C), F32),
            shape((27, C), F32), shape((1, C), F32), shape(some, F32),
        ),
        in_specs=[SMEM, SMEM] + [VMEM] * 6,
        out_specs=(VMEM,) * 7,
        scratch_shapes=[
            V(field, BF), V((2, 256, C), BF), V((2, 256, C), BF),
            V((2, 2, MINE, 3 * MINE), BF), V((2, 2, MINE // 2, C), BF), V(field, F32),
            V((512, 512), BF), V((2, 256, 512), BF),
            V((512, C), BF), V((C, 512), BF), V((512, C), BF), V((512, MINE), BF), V((512, MINE), BF),
            V((512, MINE), BF), V((512, MINE), BF), V((2, 256, 256), F32),
            V((2, 16, 256), F32), V((C, MINE), F32), V((MINE, C), F32), V((2, 2, XC, 72) + tile, BF),
            V((3, 256, 512), BF), V((3, 256, 512), BF),
            V((3, 256, 512), BF), V((256, C), BF),
            V(field, F32), V(field, BF), V(field, BF),
            V((4, 10, 16, C), F32), V((4, 10, 16, C), F32), V((3,) + field, F32),
            V((3, XC, 36) + tile, BF), V((XC - 1, 2, 2, 36) + tile, BF),
            V((XC, 36) + tile, BF), V((2, 2, 36) + tile, BF),
            V((XC - 1, 36) + tile, BF), V((3, 36) + tile, BF),
            V((72,) + tile, BF), V((ZC - 1, 9) + tile, BF),
            V((2, 2, XC, 72) + tile, BF),
            V((8,) + some, F32), V((8,) + some, F32), V((8,) + some, F32), V((2, 8) + some, F32),
            V((3, 4) + some, F32), V((3, 4) + some, F32), V((3, 4) + some, F32), V((3, 4) + some, F32),
            V((ZC - 1,) + some, F32),
            DMA((copies,)), DMA((copies,)), DMA((2,)),
        ],
        compiler_params=pltpu.CompilerParams(
            collective_id=0, has_side_effects=True, vmem_limit_bytes=60 << 20
        ),
        name="whole_block",
    )(shift, scales, tokens, cot, wq, wp, weight, gain)


def per_device(tokens, cotangent, w_qkv, w_proj, conv_weight, norm_gain, head_scale, shift_offsets):
    slab = tokens[0]
    cot = cotangent[0].reshape(256, C)
    gain = norm_gain.reshape(1, C)
    scales = head_scale.reshape(2, 2, 6).transpose(1, 0, 2).reshape(2, 12)
    output, grad_tokens, grad_qkv, grad_proj, conv, gain_sum, scale = whole_block(
        shift_offsets, scales, slab, cot, w_qkv, w_proj.reshape(2, 192, C), conv_weight, gain
    )
    factor = 1.0 / math.sqrt(lax.axis_size("rep") * lax.axis_size("dp") * SEQ * 256)
    scale = scale[:, 0].reshape(2, 16)[:, :12].reshape(2, 2, 6).transpose(1, 0, 2).reshape(24)
    return (
        output[None],
        grad_tokens[None],
        grad_qkv * factor,
        grad_proj * factor,
        conv * factor,
        gain_sum.reshape(C) * factor,
        scale * factor,
    )


def solution(mesh):
    in_specs = (
        P(("rep", "dp"), "seq", None, None, None),
        P(("rep", "dp"), "seq", None, None, None),
        P("dp", None),
        P("dp", None),
        P(),
        P(),
        P(),
        P(),
    )
    out_specs = (
        P(("rep", "dp"), "seq", None, None, None),
        P(("rep", "dp"), "seq", None, None, None),
        P("dp", None),
        P("dp", None),
        P(),
        P(),
        P(),
    )
    return jax.shard_map(
        per_device, mesh=mesh, in_specs=in_specs, out_specs=out_specs, check_vma=False
    )
```

time: 151 us -> 117 us (0.77)
  Pallas kernels: 128 us -> 101 us
  local copies, waits for them, and re-layouts: 11.9 us -> 5.76 us
    pallas_call x3 -> x1, Pallas kernels: 128 us -> 101 us  [whole_block(): pl.pallas_call(block_kernel, out_shape=(shape(field, BF), shape(field, BF...]
    unnamed x30 -> x6, local copies, waits for them, and re-layouts: 8.76 us -> 1.5 us
where the time goes in v4:
time: 117 us
  Pallas kernels  101 us (86%)
  other arithmetic  9.28 us (8%)
  local copies, waits for them, and re-layouts  5.76 us (5%)
    pallas_call x1, Pallas kernels, whole_block(): pl.pallas_call(block_kernel, out_shape=(shape(field, BF), shape(field, BF...  101 us
    mul x1, other arithmetic, per_device(): grad_qkv * factor  4.09 us
    mul x1, other arithmetic, per_device(): grad_proj * factor  2.36 us

profile of v4, /device:TPU:1, one launch (start us, length us, event | category | flops | bytes accessed | tf_op | source)
XLA Modules:
  0.0 116.5 jit_solution(3840457625516055589)
XLA Ops:
  0.6 0.7 reshape.35
  1.4 0.6 reshape.36.scales
  2.0 1.3 %reshape.38.gain = f32[1,768]{1,0:T(1,128)} reshape(f32[768]{0:T(1024)} %param.13) | data formatting | bytes 6144 | tf_op jit(solution)/shard_map/reshape | solution.py:583
  3.3 100.8 %whole_block.1 = (bf16[2,8,16,768]{3,2,1,0:T(8,128)(2,1)}, bf16[2,8,16,768]{3,2,1,0:T(8,128)(2,1)}, f32[384,2304]{1,0:T(8,128)}, f32[384,768]{1,0:T(8,128)}, f32...) custom-call(s32[2]{0:T(128)} %shift.1, f32[2,12]{1,0:T(2,128)} %reshape.36.scales, ...), custom_call_target="tpu_custom_call" | custom-call | tf_op jit(solution)/shard_map/whole_block/pallas_call | solution.py:544
  104.1 0.8 slice_reduce_fusion
  104.9 0.1 reshape_squeeze.7
  105.0 0.1 mul.49
  105.1 0.6 mul.51
  105.7 1.3 %multiply_reduce_fusion = f32[768]{0:T(1024)} fusion(f32[1,768]{1,0:T(1,128)} %get-tuple-element.19), kind=kLoop, calls=%fused_computation.4 | loop fusion | flops 768 | bytes 6144 | tf_op jit(solution)/shard_map/mul | solution.py:596
  107.0 1.5 %broadcast_multiply_fusion.2 = f32[27,768]{1,0:T(8,128)} fusion(f32[27,768]{1,0:T(8,128)} %get-tuple-element.18), kind=kLoop, calls=%fused_computation.2 | loop fusion | flops 20736 | bytes 165888 | tf_op jit(solution)/shard_map/mul | solution.py:595
  108.5 2.4 %broadcast_multiply_fusion.1 = f32[384,768]{1,0:T(8,128)} fusion(f32[384,768]{1,0:T(8,128)} %get-tuple-element.17), kind=kLoop, calls=%fused_computation.1 | loop fusion | flops 294912 | bytes 2359296 | tf_op jit(solution)/shard_map/mul | solution.py:594
  110.9 0.0 copy-start.1
  110.9 0.0 copy-start
  110.9 4.1 %broadcast_multiply_fusion = f32[384,2304]{1,0:T(8,128)} fusion(f32[384,2304]{1,0:T(8,128)} %get-tuple-element.16), kind=kLoop, calls=%fused_computation | loop fusion | flops 884736 | bytes 7077888 | tf_op jit(solution)/shard_map/mul | solution.py:593
  115.0 0.0 copy-done.1
  115.0 0.7 copy.21
  115.8 0.0 copy-done
  115.8 0.7 copy.22
  (3 shorter events, 0.0 us)
Async XLA Ops:
  110.9 4.1 %copy-start.1 = (bf16[2,8,16,768]{3,2,1,0:T(8,128)(2,1)S(1)}, bf16[2,8,16,768]{3,2,1,0:T(8,128)(2,1)}, u32[]{:S(2)}) copy-start(bf16[2,8,16,768]{3,2,1,0:T(8,128)(2,1)} %get-tuple-element.14) | copy-start | bytes 1179652
  110.9 4.8 %copy-start = (bf16[2,8,16,768]{3,2,1,0:T(8,128)(2,1)S(1)}, bf16[2,8,16,768]{3,2,1,0:T(8,128)(2,1)}, u32[]{:S(2)}) copy-start(bf16[2,8,16,768]{3,2,1,0:T(8,128)(2,1)} %get-tuple-element.15) | copy-start | bytes 1179652

commit v5 on v4

--- a/solution.py
+++ b/solution.py
@@ -1,3 +1,4 @@
+import functools
 import math
 
 import jax
@@ -141,7 +142,7 @@
     zero = jnp.zeros((256, 128), BF)
     for h in range(4):
         here = lane_head == h
-        scale = scales[core, g * 4 + h]
+        scale = scales[(g * 4 + h) // 6 * 12 + core * 6 + (g * 4 + h) % 6]
         uq_h = jnp.where(here, uq, zero)
         uk_h = jnp.where(here, uk, zero)
         v_h = jnp.where(here, value, zero)
@@ -170,10 +171,10 @@
 
 
 def block_kernel(shift, scales, tokens, cot, wq_in, wp_in, weight, gain,
-                 out, grad, gq_out, gp_out, conv_out, gain_out, scale_out,
+                 out, grad, full, small_out,
                  halo, nwin, cwin, wq, wp, mixed, sel, res, x_s, xt_s, ct_s, qkv_s, ba_s, att_s, bqkv_s, allow_s,
                  scale_s, gq_s, gp_s, g, own, given,
-                 recv, bn_s, bm, bmh, ph, xf, tf, sh, ra0, ra1, sa0, sa1, rb0, rb1, sb, rc, full,
+                 recv, bn_s, bm, bmh, ph, xf, tf, sh, ra0, ra1, sa0, sa1, rb0, rb1, sb, rc,
                  sm, s2, s3, sz, qy1, qx1, qx2, qy2, qz, s_sem, r_sem, l_sem):
     rep, dp, seq, core = place()
     z = lax.rem(seq // 2, ZC)
@@ -218,13 +219,14 @@
     halos = [go(tokens.at[0], halo.at[1], down), go(tokens.at[1], halo.at[0], up)]
     local = [
         pltpu.make_async_copy(cot, cwin.at[half], l_sem.at[0]),
-        pltpu.make_async_copy(wp_in, wp.at[:, dp], l_sem.at[1]),
+        pltpu.make_async_copy(wp_in.at[pl.ds(0, 192)], wp.at[0, dp], l_sem.at[1]),
+        pltpu.make_async_copy(wp_in.at[pl.ds(192, 192)], wp.at[1, dp], l_sem.at[2]),
     ]
     for c in local:
         c.start()
     y_to = lax.rem(y + 3 + 2 * core, 4)
     y_peer = (y_to // 2, lax.rem(y_to, 2), seq)
-    wp_came = go(wp_in.at[core], wp.at[core, dp], y_peer)
+    wp_came = go(wp_in.at[pl.ds(pl.multiple_of(core * 192, 64), 192)], wp.at[core, dp], y_peer)
     cots = go(cot, cwin.at[half], partner)
     arrange(wq_in, wq, dp)
     wq_came = []
@@ -245,7 +247,7 @@
     def unit_step(i, carry):
         d, h = i // 2, lax.rem(i, 2) * 4
         unit, _ = normalise(mixed[d, pl.ds(h, 4)].reshape(64, C))
-        nwin[half, pl.ds(pl.multiple_of(i * 64, 64), 64)] = (unit * gain[...]).astype(BF)
+        nwin[half, pl.ds(pl.multiple_of(i * 64, 64), 64)] = (unit * gain[...].reshape(1, C)).astype(BF)
         return carry
 
     lax.fori_loop(0, 4, unit_step, 0)
@@ -348,7 +350,7 @@
         unit, inverse = normalise(mixed[d, pl.ds(h, 4)].reshape(64, C))
         back_float = bn_s[rows].astype(F32)
         total = total + jnp.sum((back_float * unit).reshape(8, 8, C), axis=0)
-        grad_unit = back_float * gain[...]
+        grad_unit = back_float * gain[...].reshape(1, C)
         mean = jnp.mean(grad_unit, axis=-1, keepdims=True)
         slope = jnp.mean(grad_unit * unit, axis=-1, keepdims=True)
         result = cot[rows].astype(F32) + inverse * (grad_unit - mean - unit * slope)
@@ -501,37 +503,67 @@
     little = go(sz.at[core], sz.at[core], other_core)
     finish(handed)
 
+    little.wait()
+    small_out[...] = sz[0] + sz[1]
+
+
+def assemble_kernel(factor, full, small, out_in, grad_in, gq_out, gp_out, conv_out, gain_out, scale_out, out, grad):
+    out[...] = out_in[...]
+    grad[...] = grad_in[...]
     lane = iota((48, 128), 1)
-
-    def assemble(i, carry):
-        r, k = i // 4, lax.rem(i, 4)
-        rows = pl.ds(pl.multiple_of(i * 48, 48), 48)
-        for part in range(3):
-            for m in range(6):
-                halves = []
-                for gets in range(2):
-                    block = 2 * m + gets
-                    c = block % 6 // 3
-                    old = block // 6 * 3 + block % 3
-                    start = TILES[old // 2] + part * 6
-                    tile = full[c, r, k, start : start + 6].astype(F32).reshape(48, 128)
-                    halves.append(tile if old % 2 == gets else pltpu.roll(tile, 64, 1))
-                start = part * C + m * 128
-                gq_out[rows, start : start + 128] = jnp.where(lane < 64, halves[0], halves[1])
-        for c in range(2):
-            for m in range(6):
-                tile = full[c, r, k, 54 + m * 3 : 57 + m * 3].astype(F32).reshape(24, 128)
-                start = pl.multiple_of(c * 192 + i * 24, 8)
-                gp_out[pl.ds(start, 24), m * 128 : m * 128 + 128] = tile
-        return carry
-
-    lax.fori_loop(0, 8, assemble, 0)
-    little.wait()
-    for j in range(6):
-        total = sz[0, j] + sz[1, j]
-        conv_out[:, j * 128 : j * 128 + 128] = total[0:27]
-        gain_out[:, j * 128 : j * 128 + 128] = total[27:28]
-    scale_out[...] = sz[0, 6] + sz[1, 6]
+    for part in range(3):
+        for m in range(6):
+            halves = []
+            for gets in range(2):
+                block = 2 * m + gets
+                c = block % 6 // 3
+                old = block // 6 * 3 + block % 3
+                start = TILES[old // 2] + part * 6
+                tile = full[c, 0, 0, start : start + 6].astype(F32).reshape(48, 128)
+                halves.append(tile if old % 2 == gets else pltpu.roll(tile, 64, 1))
+            start = part * C + m * 128
+            gq_out[:, start : start + 128] = jnp.where(lane < 64, halves[0], halves[1]) * factor
+    for c in range(2):
+        for m in range(6):
+            tile = full[c, 0, 0, 54 + m * 3 : 57 + m * 3].astype(F32).reshape(24, 128)
+            gp_out[c, :, m * 128 : m * 128 + 128] = tile * factor
+
+    @pl.when(pl.program_id(0) == 0)
+    def _():
+        for j in range(6):
+            conv_out[:, j * 128 : j * 128 + 128] = small[j, 0:27] * factor
+            gain_out[:, j * 128 : j * 128 + 128] = small[j, 27:28] * factor
+        head, row = iota((32, 128), 1), iota((32, 128), 0)
+        mine = row == head % 12 // 6 * 16 + head // 12 * 6 + head % 6
+        scale_out[...] = jnp.sum(jnp.where(mine, small[6], 0.0), axis=0, keepdims=True) * factor
+
+
+def assemble(factor, full, small, out, grad):
+    shape = jax.ShapeDtypeStruct
+    return pl.pallas_call(
+        functools.partial(assemble_kernel, factor),
+        grid=(8,),
+        out_shape=(
+            shape((MINE, 3 * C), F32), shape((2, 192, C), F32),
+            shape((27, C), F32), shape((1, C), F32), shape((1, 128), F32),
+            shape(out.shape, BF), shape(out.shape, BF),
+        ),
+        in_specs=[
+            pl.BlockSpec((2, 1, 1, 72, 8, 128), lambda i: (0, i // 4, i % 4, 0, 0, 0)),
+            pl.BlockSpec((8, 32, 128), lambda i: (0, 0, 0)),
+            pl.BlockSpec((1, 2, 16, C), lambda i: (i // 4, i % 4, 0, 0)),
+            pl.BlockSpec((1, 2, 16, C), lambda i: (i // 4, i % 4, 0, 0)),
+        ],
+        out_specs=(
+            pl.BlockSpec((48, 3 * C), lambda i: (i, 0)), pl.BlockSpec((2, 24, C), lambda i: (0, i, 0)),
+            pl.BlockSpec((27, C), lambda i: (0, 0)), pl.BlockSpec((1, C), lambda i: (0, 0)),
+            pl.BlockSpec((1, 128), lambda i: (0, 0)),
+            pl.BlockSpec((1, 2, 16, C), lambda i: (i // 4, i % 4, 0, 0)),
+            pl.BlockSpec((1, 2, 16, C), lambda i: (i // 4, i % 4, 0, 0)),
+        ),
+        compiler_params=pltpu.CompilerParams(vmem_limit_bytes=60 << 20),
+        name="assemble",
+    )(full, small, out, grad)
 
 
 def whole_block(shift, scales, tokens, cot, wq, wp, weight, gain):
@@ -544,11 +576,10 @@
     return pl.pallas_call(
         block_kernel,
         out_shape=(
-            shape(field, BF), shape(field, BF), shape((MINE, 3 * C), F32), shape((MINE, C), F32),
-            shape((27, C), F32), shape((1, C), F32), shape(some, F32),
+            shape(field, BF), shape(field, BF), shape((2, 2, XC, 72) + tile, BF), shape((8,) + some, F32),
         ),
         in_specs=[SMEM, SMEM] + [VMEM] * 6,
-        out_specs=(VMEM,) * 7,
+        out_specs=(VMEM,) * 4,
         scratch_shapes=[
             V(field, BF), V((2, 256, C), BF), V((2, 256, C), BF),
             V((2, 2, MINE, 3 * MINE), BF), V((2, 2, MINE // 2, C), BF), V(field, F32),
@@ -564,11 +595,10 @@
             V((XC, 36) + tile, BF), V((2, 2, 36) + tile, BF),
             V((XC - 1, 36) + tile, BF), V((3, 36) + tile, BF),
             V((72,) + tile, BF), V((ZC - 1, 9) + tile, BF),
-            V((2, 2, XC, 72) + tile, BF),
             V((8,) + some, F32), V((8,) + some, F32), V((8,) + some, F32), V((2, 8) + some, F32),
             V((3, 4) + some, F32), V((3, 4) + some, F32), V((3, 4) + some, F32), V((3, 4) + some, F32),
             V((ZC - 1,) + some, F32),
-            DMA((copies,)), DMA((copies,)), DMA((2,)),
+            DMA((copies,)), DMA((copies,)), DMA((3,)),
         ],
         compiler_params=pltpu.CompilerParams(
             collective_id=0, has_side_effects=True, vmem_limit_bytes=60 << 20
@@ -578,23 +608,21 @@
 
 
 def per_device(tokens, cotangent, w_qkv, w_proj, conv_weight, norm_gain, head_scale, shift_offsets):
-    slab = tokens[0]
-    cot = cotangent[0].reshape(256, C)
-    gain = norm_gain.reshape(1, C)
-    scales = head_scale.reshape(2, 2, 6).transpose(1, 0, 2).reshape(2, 12)
-    output, grad_tokens, grad_qkv, grad_proj, conv, gain_sum, scale = whole_block(
-        shift_offsets, scales, slab, cot, w_qkv, w_proj.reshape(2, 192, C), conv_weight, gain
+    output, grad_tokens, full, small = whole_block(
+        shift_offsets, head_scale, tokens[0], cotangent[0].reshape(256, C), w_qkv, w_proj, conv_weight, norm_gain
     )
     factor = 1.0 / math.sqrt(lax.axis_size("rep") * lax.axis_size("dp") * SEQ * 256)
-    scale = scale[:, 0].reshape(2, 16)[:, :12].reshape(2, 2, 6).transpose(1, 0, 2).reshape(24)
+    grad_qkv, grad_proj, grad_conv, grad_gain, grad_scale, output, grad_tokens = assemble(
+        factor, full, small, output, grad_tokens
+    )
     return (
         output[None],
         grad_tokens[None],
-        grad_qkv * factor,
-        grad_proj * factor,
-        conv * factor,
-        gain_sum.reshape(C) * factor,
-        scale * factor,
+        grad_qkv,
+        grad_proj.reshape(MINE, C),
+        grad_conv,
+        grad_gain.reshape(C),
+        grad_scale[0, :24],
     )
 
 

time: 117 us -> 110 us (0.940)
  other arithmetic: 9.28 us -> 1.27 us
  Pallas kernels: 101 us -> 106 us
  local copies, waits for them, and re-layouts: 5.76 us -> 1.17 us
    mul x5 -> x0, other arithmetic: 9.28 us -> none  [the longest x1 4.09 us: per_device(): grad_qkv * factor]
    pallas_call x0 -> x1, Pallas kernels: none -> 6.99 us  [assemble(): pl.pallas_call(functools.partial(assemble_kernel, factor), grid=(8,), out...]
    reshape x3 -> x0, local copies, waits for them, and re-layouts: 2.65 us -> none  [the longest x2 1.38 us: per_device(): scales = head_scale.reshape(2, 2, 6).transpose(1, 0, 2).reshape(2, 12)]
    unnamed x6 -> x0, local copies, waits for them, and re-layouts: 1.5 us -> none
    pallas_call x1, Pallas kernels: 101 us -> 99.3 us  [whole_block(): pl.pallas_call(block_kernel, out_shape=(shape(field, BF), shape(field, BF...]
    pallas_call x0 -> x1, other arithmetic: none -> 1.27 us  [assemble(): pl.pallas_call(functools.partial(assemble_kernel, factor), grid=(8,), out...]
where the time goes in v5:
time: 110 us; the launch traced here: 109 us
  Pallas kernels  106 us (96%)
  other arithmetic  1.27 us (1%)
  local copies, waits for them, and re-layouts  1.17 us (1%)
    pallas_call x1, Pallas kernels, whole_block(): pl.pallas_call(block_kernel, out_shape=(shape(field, BF), shape(field, BF...  99.3 us
    pallas_call x1, Pallas kernels, assemble(): pl.pallas_call(functools.partial(assemble_kernel, factor), grid=(8,), out...  6.99 us

profile of v5, /device:TPU:1, one launch (start us, length us, event | category | flops | bytes accessed | tf_op | source)
XLA Modules:
  0.0 109.4 jit_solution(12828266478442591480)
XLA Ops:
  0.6 99.3 %whole_block.1 = (bf16[2,8,16,768]{3,2,1,0:T(8,128)(2,1)}, bf16[2,8,16,768]{3,2,1,0:T(8,128)(2,1)}, bf16[2,2,4,72,8,128]{5,4,3,2,1,0:T(8,128)(2,1)}, f32[8,32,128]{2,1,0:T(8,128)}) custom-call(s32[2]{0:T(128)} %shift.1, f32[24]{0:T(128)} %scales.1, bf16[2,8,16,768]{3,2,1,0:T(8,128)(2,1)} %bitcast.7, bf16[256,768]{1,0:T(8,128)(2,1)} %bitcast.8, ...), custom_call_target="tpu_custom_call" | custom-call | tf_op jit(solution)/shard_map/whole_block/pallas_call | solution.py:576
  100.0 7.0 %assemble.1 = (f32[384,2304]{1,0:T(8,128)}, f32[2,192,768]{2,1,0:T(8,128)}, f32[27,768]{1,0:T(8,128)}, f32[1,768]{1,0:T(1,128)}, f32[1,128]{1,0:T(1,128)}, /*ind...) custom-call(bf16[2,2,4,72,8,128]{5,4,3,2,1,0:T(8,128)(2,1)} %get-tuple-element.18.full, ...), custom_call_target="tpu_custom_call" | custom-call | tf_op jit(solution)/shard_map/assemble/pallas_call | solution.py:543
  107.0 1.2 %slice_bitcast_fusion = f32[24]{0:T(128)} fusion(f32[1,128]{1,0:T(1,128)} %get-tuple-element.28), kind=kLoop, calls=%fused_computation | loop fusion | bytes 192 | tf_op jit(solution)/shard_map/squeeze | solution.py:625
  108.1 1.3 %reduce = f32[768]{0:T(1024)} reduce(f32[1,768]{1,0:T(1,128)} %get-tuple-element.27, f32[]{:T(128)} %constant.2), dimensions={0}, to_apply=%get-tuple-element.27.reduce_sub_computation | reduce | bytes 6148 | tf_op jit(solution)/shard_map/assemble/pallas_call | solution.py:543

commit v6 on v5

--- a/solution.py
+++ b/solution.py
@@ -170,9 +170,9 @@
     bqkv_s[rows, 256:384] = back_v.astype(BF)
 
 
-def block_kernel(shift, scales, tokens, cot, wq_in, wp_in, weight, gain,
+def block_kernel(shift, scales, tokens_in, cot, wq_any, wp_in, weight, gain,
                  out, grad, full, small_out,
-                 halo, nwin, cwin, wq, wp, mixed, sel, res, x_s, xt_s, ct_s, qkv_s, ba_s, att_s, bqkv_s, allow_s,
+                 tokens, wq_in, halo, nwin, cwin, wq, wp, mixed, sel, res, x_s, xt_s, ct_s, qkv_s, ba_s, att_s, bqkv_s, allow_s,
                  scale_s, gq_s, gp_s, g, own, given,
                  recv, bn_s, bm, bmh, ph, xf, tf, sh, ra0, ra1, sa0, sa1, rb0, rb1, sb, rc,
                  sm, s2, s3, sz, qy1, qx1, qx2, qy2, qz, s_sem, r_sem, l_sem):
@@ -200,6 +200,16 @@
     other_rep = (1 - rep, dp, seq)
     peers = [at_y(k) for k in range(1, 4)] + [at_x(k) for k in range(1, XC)]
     peers += [at_z(k) for k in range(1, ZC)] + [up, down]
+    half = 1 - core
+    local = [
+        pltpu.make_async_copy(tokens_in, tokens, l_sem.at[0]),
+        pltpu.make_async_copy(wq_any, wq_in, l_sem.at[1]),
+        pltpu.make_async_copy(cot, cwin.at[half], l_sem.at[2]),
+        pltpu.make_async_copy(wp_in.at[pl.ds(0, 192)], wp.at[0, dp], l_sem.at[3]),
+        pltpu.make_async_copy(wp_in.at[pl.ds(192, 192)], wp.at[1, dp], l_sem.at[4]),
+    ]
+    for c in local:
+        c.start()
     greet(peers)
     used = [0]
 
@@ -215,43 +225,35 @@
     low, high = pl.ds(0, 36), pl.ds(36, 36)
     first = jnp.where(seq == 0, 0.0, 1.0).astype(F32)
     last = jnp.where(seq == SEQ - 1, 0.0, 1.0).astype(F32)
-    half = 1 - core
-    halos = [go(tokens.at[0], halo.at[1], down), go(tokens.at[1], halo.at[0], up)]
-    local = [
-        pltpu.make_async_copy(cot, cwin.at[half], l_sem.at[0]),
-        pltpu.make_async_copy(wp_in.at[pl.ds(0, 192)], wp.at[0, dp], l_sem.at[1]),
-        pltpu.make_async_copy(wp_in.at[pl.ds(192, 192)], wp.at[1, dp], l_sem.at[2]),
-    ]
-    for c in local:
-        c.start()
+    halos = [go(tokens_in.at[0], halo.at[1], down), go(tokens_in.at[1], halo.at[0], up)]
     y_to = lax.rem(y + 3 + 2 * core, 4)
     y_peer = (y_to // 2, lax.rem(y_to, 2), seq)
     wp_came = go(wp_in.at[pl.ds(pl.multiple_of(core * 192, 64), 192)], wp.at[core, dp], y_peer)
     cots = go(cot, cwin.at[half], partner)
+    local[1].wait()
     arrange(wq_in, wq, dp)
     wq_came = []
     for k in range(3):
         piece = wq.at[core, dp, :, k * MINE : k * MINE + MINE]
         wq_came.append(go(piece, piece, y_peer))
+    local[0].wait()
     finish(halos)
     fill_padded(tf, halo[0].astype(F32) * first, tokens[...].astype(F32), halo[1].astype(F32) * last)
 
-    def mix_step(i, carry):
-        d, j = i // 6, lax.rem(i, 6)
-        lanes = chunk(j)
-        mixed[d, :, :, lanes] = tf[d + 1, 1:9, :, lanes] + taps(tf, weight, d, lanes, False)
-        return carry
-
-    lax.fori_loop(0, 12, mix_step, 0)
-
-    def unit_step(i, carry):
-        d, h = i // 2, lax.rem(i, 2) * 4
-        unit, _ = normalise(mixed[d, pl.ds(h, 4)].reshape(64, C))
-        nwin[half, pl.ds(pl.multiple_of(i * 64, 64), 64)] = (unit * gain[...].reshape(1, C)).astype(BF)
-        return carry
-
-    lax.fori_loop(0, 4, unit_step, 0)
-    norms = go(nwin.at[half], nwin.at[half], partner)
+    norms = []
+    for d in range(2):
+        def mix_step(j, carry):
+            lanes = chunk(j)
+            mixed[d, :, :, lanes] = tf[d + 1, 1:9, :, lanes] + taps(tf, weight, d, lanes, False)
+            return carry
+
+        lax.fori_loop(0, 6, mix_step, 0)
+        for h in range(0, 8, 4):
+            unit, _ = normalise(mixed[d, h : h + 4].reshape(64, C))
+            start = d * 128 + h * 16
+            nwin[half, start : start + 64] = (unit * gain[...].reshape(1, C)).astype(BF)
+        piece = nwin.at[half, pl.ds(d * 128, 128)]
+        norms.append(go(piece, piece, partner))
 
     s, r = shift[0], shift[1]
     sel[...] = jnp.where(iota((512, 512), 1) == source_of(iota((512, 512), 0), r), 1.0, 0.0).astype(BF)
@@ -267,13 +269,13 @@
         same = code(iota((256, 256), 0), b) == code(iota((256, 256), 1), b)
         allow_s[b] = jnp.where(same, 1.0, 0.0).astype(F32)
     scale_s[...] = jnp.zeros((2, 16, 256), F32)
-    for c in local:
+    for c in local[2:]:
         c.wait()
     cots.wait()
     ct_s[...] = nn(sel[...], cwin[...].reshape(512, C)).astype(BF)
     wp_came.wait()
     ba_s[...] = nt(ct_s[...], wp[core].reshape(MINE, C)).astype(BF)
-    norms.wait()
+    finish(norms)
     ordered = nn(sel[...], nwin[...].reshape(512, C))
     x_s[...] = ordered.astype(BF)
     xt_s[...] = ordered.T.astype(BF)
@@ -353,7 +355,7 @@
         grad_unit = back_float * gain[...].reshape(1, C)
         mean = jnp.mean(grad_unit, axis=-1, keepdims=True)
         slope = jnp.mean(grad_unit * unit, axis=-1, keepdims=True)
-        result = cot[rows].astype(F32) + inverse * (grad_unit - mean - unit * slope)
+        result = cwin[half, rows].astype(F32) + inverse * (grad_unit - mean - unit * slope)
         bm[d, pl.ds(h, 4)] = result.reshape(4, 16, C)
         bmh[d, pl.ds(h, 4)] = result.astype(BF).reshape(4, 16, C)
         return total
@@ -532,10 +534,10 @@
     def _():
         for j in range(6):
             conv_out[:, j * 128 : j * 128 + 128] = small[j, 0:27] * factor
-            gain_out[:, j * 128 : j * 128 + 128] = small[j, 27:28] * factor
+            gain_out[j * 128 : j * 128 + 128] = small[j, 27] * factor
         head, row = iota((32, 128), 1), iota((32, 128), 0)
         mine = row == head % 12 // 6 * 16 + head // 12 * 6 + head % 6
-        scale_out[...] = jnp.sum(jnp.where(mine, small[6], 0.0), axis=0, keepdims=True) * factor
+        scale_out[...] = jnp.sum(jnp.where(mine, small[6], 0.0), axis=0) * factor
 
 
 def assemble(factor, full, small, out, grad):
@@ -545,7 +547,7 @@
         grid=(8,),
         out_shape=(
             shape((MINE, 3 * C), F32), shape((2, 192, C), F32),
-            shape((27, C), F32), shape((1, C), F32), shape((1, 128), F32),
+            shape((27, C), F32), shape((C,), F32), shape((128,), F32),
             shape(out.shape, BF), shape(out.shape, BF),
         ),
         in_specs=[
@@ -556,8 +558,8 @@
         ],
         out_specs=(
             pl.BlockSpec((48, 3 * C), lambda i: (i, 0)), pl.BlockSpec((2, 24, C), lambda i: (0, i, 0)),
-            pl.BlockSpec((27, C), lambda i: (0, 0)), pl.BlockSpec((1, C), lambda i: (0, 0)),
-            pl.BlockSpec((1, 128), lambda i: (0, 0)),
+            pl.BlockSpec((27, C), lambda i: (0, 0)), pl.BlockSpec((C,), lambda i: (0,)),
+            pl.BlockSpec((128,), lambda i: (0,)),
             pl.BlockSpec((1, 2, 16, C), lambda i: (i // 4, i % 4, 0, 0)),
             pl.BlockSpec((1, 2, 16, C), lambda i: (i // 4, i % 4, 0, 0)),
         ),
@@ -578,10 +580,10 @@
         out_shape=(
             shape(field, BF), shape(field, BF), shape((2, 2, XC, 72) + tile, BF), shape((8,) + some, F32),
         ),
-        in_specs=[SMEM, SMEM] + [VMEM] * 6,
+        in_specs=[SMEM, SMEM] + [pl.BlockSpec(memory_space=pl.ANY)] * 4 + [VMEM] * 2,
         out_specs=(VMEM,) * 4,
         scratch_shapes=[
-            V(field, BF), V((2, 256, C), BF), V((2, 256, C), BF),
+            V(field, BF), V((MINE, 3 * C), BF), V(field, BF), V((2, 256, C), BF), V((2, 256, C), BF),
             V((2, 2, MINE, 3 * MINE), BF), V((2, 2, MINE // 2, C), BF), V(field, F32),
             V((512, 512), BF), V((2, 256, 512), BF),
             V((512, C), BF), V((C, 512), BF), V((512, C), BF), V((512, MINE), BF), V((512, MINE), BF),
@@ -598,7 +600,7 @@
             V((8,) + some, F32), V((8,) + some, F32), V((8,) + some, F32), V((2, 8) + some, F32),
             V((3, 4) + some, F32), V((3, 4) + some, F32), V((3, 4) + some, F32), V((3, 4) + some, F32),
             V((ZC - 1,) + some, F32),
-            DMA((copies,)), DMA((copies,)), DMA((3,)),
+            DMA((copies,)), DMA((copies,)), DMA((5,)),
         ],
         compiler_params=pltpu.CompilerParams(
             collective_id=0, has_side_effects=True, vmem_limit_bytes=60 << 20
@@ -621,8 +623,8 @@
         grad_qkv,
         grad_proj.reshape(MINE, C),
         grad_conv,
-        grad_gain.reshape(C),
-        grad_scale[0, :24],
+        grad_gain,
+        grad_scale[:24],
     )
 
 

time: 110 us -> 110 us (level)
  Pallas kernels: 106 us -> 109 us
  other arithmetic: 1.27 us -> 0 us
  local copies, waits for them, and re-layouts: 1.17 us -> 0 us
    pallas_call x1, Pallas kernels: 99.3 us -> 102 us  [whole_block(): pl.pallas_call(block_kernel, out_shape=(shape(field, BF), shape(field, BF...]
    pallas_call x1 -> x0, other arithmetic: 1.27 us -> none  [assemble(): pl.pallas_call(functools.partial(assemble_kernel, factor), grid=(8,), out...]
    squeeze x1 -> x0, local copies, waits for them, and re-layouts: 1.17 us -> none  [per_device(): grad_scale[0, :24]]
where the time goes in v6:
time: 110 us
  Pallas kernels  109 us (99%)
    pallas_call x1, Pallas kernels, whole_block(): pl.pallas_call(block_kernel, out_shape=(shape(field, BF), shape(field, BF...  102 us
    pallas_call x1, Pallas kernels, assemble(): pl.pallas_call(functools.partial(assemble_kernel, factor), grid=(8,), out...  6.99 us

profile of v6, /device:TPU:1, one launch (start us, length us, event | category | flops | bytes accessed | tf_op | source)
XLA Modules:
  0.0 109.8 jit_solution(16888076646413585606)
XLA Ops:
  0.6 102.0 %whole_block.1 = (bf16[2,8,16,768]{3,2,1,0:T(8,128)(2,1)}, bf16[2,8,16,768]{3,2,1,0:T(8,128)(2,1)}, bf16[2,2,4,72,8,128]{5,4,3,2,1,0:T(8,128)(2,1)}, f32[8,32,128]{2,1,0:T(8,128)}) custom-call(s32[2]{0:T(128)} %shift.1, f32[24]{0:T(128)} %scales.1, bf16[2,8,16,768]{3,2,1,0:T(8,128)(2,1)} %bitcast.6, bf16[256,768]{1,0:T(8,128)(2,1)} %bitcast.7, ...), custom_call_target="tpu_custom_call" | custom-call | tf_op jit(solution)/shard_map/whole_block/pallas_call | solution.py:578
  102.7 7.0 %assemble.1 = (f32[384,2304]{1,0:T(8,128)}, f32[2,192,768]{2,1,0:T(8,128)}, f32[27,768]{1,0:T(8,128)}, f32[768]{0:T(1024)}, f32[128]{0:T(128)}, /*index=5*/bf16[...) custom-call(bf16[2,2,4,72,8,128]{5,4,3,2,1,0:T(8,128)(2,1)} %get-tuple-element.18.full, ...), custom_call_target="tpu_custom_call" | custom-call | tf_op jit(solution)/shard_map/assemble/pallas_call | solution.py:545

commit v7 on v6

--- a/solution.py
+++ b/solution.py
@@ -280,6 +280,10 @@
     x_s[...] = ordered.astype(BF)
     xt_s[...] = ordered.T.astype(BF)
 
+    def keep_own(k):
+        own[k, :, 0:128] = nn(res[half], att_s[:, k * 128 : k * 128 + 128]).astype(BF)
+        own[k, :, 128:] = nn(res[half], bqkv_s[...]).astype(BF)
+
     exchanges, stage, swaps = [], [], []
     for k in range(3):
         wq_came[k].wait()
@@ -319,8 +323,8 @@
             else:
                 to = at_y(step)
                 stage.append(go(g.at[to[1], to[0], :, tiles], ra0.at[step - 1, :, away], to))
-        own[k, :, 0:128] = nn(res[half], att_s[:, lanes]).astype(BF)
-        own[k, :, 128:] = nn(res[half], bqkv_s[...]).astype(BF)
+        if k < 2:
+            keep_own(k)
     gp_s[...] = tn(att_s[...], ct_s[...])
 
     def store_proj(i, carry):
@@ -334,6 +338,8 @@
     tiles, away = pl.ds(54, 18), pl.ds(18, 18)
     for step in range(1, 4):
         stage.append(go(g.at[:, :, lax.rem(x + step, XC), tiles], ra1.at[step - 1, :, :, away], at_x(step)))
+
+    keep_own(2)
 
     def wq_of(c, k):
         return wq[c, :, :, k * MINE : k * MINE + MINE].reshape(C, MINE)
@@ -513,22 +519,24 @@
     out[...] = out_in[...]
     grad[...] = grad_in[...]
     lane = iota((48, 128), 1)
-    for part in range(3):
-        for m in range(6):
-            halves = []
-            for gets in range(2):
-                block = 2 * m + gets
-                c = block % 6 // 3
-                old = block // 6 * 3 + block % 3
-                start = TILES[old // 2] + part * 6
-                tile = full[c, 0, 0, start : start + 6].astype(F32).reshape(48, 128)
-                halves.append(tile if old % 2 == gets else pltpu.roll(tile, 64, 1))
-            start = part * C + m * 128
-            gq_out[:, start : start + 128] = jnp.where(lane < 64, halves[0], halves[1]) * factor
-    for c in range(2):
-        for m in range(6):
-            tile = full[c, 0, 0, 54 + m * 3 : 57 + m * 3].astype(F32).reshape(24, 128)
-            gp_out[c, :, m * 128 : m * 128 + 128] = tile * factor
+    for k in range(2):
+        for part in range(3):
+            for m in range(6):
+                halves = []
+                for gets in range(2):
+                    block = 2 * m + gets
+                    c = block % 6 // 3
+                    old = block // 6 * 3 + block % 3
+                    start = TILES[old // 2] + part * 6
+                    tile = full[c, 0, k, start : start + 6].astype(F32).reshape(48, 128)
+                    halves.append(tile if old % 2 == gets else pltpu.roll(tile, 64, 1))
+                start = part * C + m * 128
+                rows = slice(k * 48, k * 48 + 48)
+                gq_out[rows, start : start + 128] = jnp.where(lane < 64, halves[0], halves[1]) * factor
+        for c in range(2):
+            for m in range(6):
+                tile = full[c, 0, k, 54 + m * 3 : 57 + m * 3].astype(F32).reshape(24, 128)
+                gp_out[c, k * 24 : k * 24 + 24, m * 128 : m * 128 + 128] = tile * factor
 
     @pl.when(pl.program_id(0) == 0)
     def _():
@@ -544,24 +552,24 @@
     shape = jax.ShapeDtypeStruct
     return pl.pallas_call(
         functools.partial(assemble_kernel, factor),
-        grid=(8,),
+        grid=(4,),
         out_shape=(
             shape((MINE, 3 * C), F32), shape((2, 192, C), F32),
             shape((27, C), F32), shape((C,), F32), shape((128,), F32),
             shape(out.shape, BF), shape(out.shape, BF),
         ),
         in_specs=[
-            pl.BlockSpec((2, 1, 1, 72, 8, 128), lambda i: (0, i // 4, i % 4, 0, 0, 0)),
+            pl.BlockSpec((2, 1, 2, 72, 8, 128), lambda i: (0, i // 2, i % 2, 0, 0, 0)),
             pl.BlockSpec((8, 32, 128), lambda i: (0, 0, 0)),
-            pl.BlockSpec((1, 2, 16, C), lambda i: (i // 4, i % 4, 0, 0)),
-            pl.BlockSpec((1, 2, 16, C), lambda i: (i // 4, i % 4, 0, 0)),
+            pl.BlockSpec((1, 4, 16, C), lambda i: (i // 2, i % 2, 0, 0)),
+            pl.BlockSpec((1, 4, 16, C), lambda i: (i // 2, i % 2, 0, 0)),
         ],
         out_specs=(
-            pl.BlockSpec((48, 3 * C), lambda i: (i, 0)), pl.BlockSpec((2, 24, C), lambda i: (0, i, 0)),
+            pl.BlockSpec((96, 3 * C), lambda i: (i, 0)), pl.BlockSpec((2, 48, C), lambda i: (0, i, 0)),
             pl.BlockSpec((27, C), lambda i: (0, 0)), pl.BlockSpec((C,), lambda i: (0,)),
             pl.BlockSpec((128,), lambda i: (0,)),
-            pl.BlockSpec((1, 2, 16, C), lambda i: (i // 4, i % 4, 0, 0)),
-            pl.BlockSpec((1, 2, 16, C), lambda i: (i // 4, i % 4, 0, 0)),
+            pl.BlockSpec((1, 4, 16, C), lambda i: (i // 2, i % 2, 0, 0)),
+            pl.BlockSpec((1, 4, 16, C), lambda i: (i // 2, i % 2, 0, 0)),
         ),
         compiler_params=pltpu.CompilerParams(vmem_limit_bytes=60 << 20),
         name="assemble",

time: 110 us -> 109 us (level)
    pallas_call x1, Pallas kernels: 6.99 us -> 5.16 us  [assemble(): pl.pallas_call(functools.partial(assemble_kernel, factor), grid=(4,), out...]
where the time goes in v7:
time: 109 us
  Pallas kernels  108 us (99%)
    pallas_call x1, Pallas kernels, whole_block(): pl.pallas_call(block_kernel, out_shape=(shape(field, BF), shape(field, BF...  103 us
    pallas_call x1, Pallas kernels, assemble(): pl.pallas_call(functools.partial(assemble_kernel, factor), grid=(4,), out...  5.16 us

profile of v7, /device:TPU:1, one launch (start us, length us, event | category | flops | bytes accessed | tf_op | source)
XLA Modules:
  0.0 109.0 jit_solution(5419722282594679447)
XLA Ops:
  0.6 103.1 %whole_block.1 = (bf16[2,8,16,768]{3,2,1,0:T(8,128)(2,1)}, bf16[2,8,16,768]{3,2,1,0:T(8,128)(2,1)}, bf16[2,2,4,72,8,128]{5,4,3,2,1,0:T(8,128)(2,1)}, f32[8,32,128]{2,1,0:T(8,128)}) custom-call(s32[2]{0:T(128)} %shift.1, f32[24]{0:T(128)} %scales.1, bf16[2,8,16,768]{3,2,1,0:T(8,128)(2,1)} %bitcast.6, bf16[256,768]{1,0:T(8,128)(2,1)} %bitcast.7, ...), custom_call_target="tpu_custom_call" | custom-call | tf_op jit(solution)/shard_map/whole_block/pallas_call | solution.py:586
  103.7 5.2 %assemble.1 = (f32[384,2304]{1,0:T(8,128)}, f32[2,192,768]{2,1,0:T(8,128)}, f32[27,768]{1,0:T(8,128)}, f32[768]{0:T(1024)}, f32[128]{0:T(128)}, /*index=5*/bf16[...) custom-call(bf16[2,2,4,72,8,128]{5,4,3,2,1,0:T(8,128)(2,1)} %get-tuple-element.18.full, ...), custom_call_target="tpu_custom_call" | custom-call | tf_op jit(solution)/shard_map/assemble/pallas_call | solution.py:553
